TPU v7x, 256 devices: a whole 4x4x8 slice. The times are simulated.
256 devices in a mesh: ctx: 16 (over z_lo, y, core), uly: 16 (over x, z_hi).
Axes of the slice: x: 4, y: 4, z: 8 (z_hi: 4, z_lo: 2; z = z_hi * 2 + z_lo), core: 2. Of those that a mesh axis runs over, the one named last changes fastest.
Arguments:
- query: bfloat16 [32768, 5120], P(('ctx', 'uly')), may hold values from -8 to 8
- key: bfloat16 [32768, 5120], P(('ctx', 'uly')), may hold values from -8 to 8
- value: bfloat16 [32768, 5120], P(('ctx', 'uly')), may hold values from -6 to 6
- dout: bfloat16 [32768, 5120], P(('ctx', 'uly')), may hold values from -6 to 6
- tile_mask: int32 [40, 256, 5], replicated, may hold values from 0 to 1, as said below
Outputs:
- grad_query: bfloat16 [32768, 5120], P(('ctx', 'uly'))
- grad_key: bfloat16 [32768, 5120], P(('ctx', 'uly'))
- grad_value: bfloat16 [32768, 5120], P(('ctx', 'uly'))
Inputs may be any that keep to these rules, and one draw needn't show every extreme that they name: `tile_mask`: the tile of a block with itself (offset 2) is active for every head and block.
All inputs are finite; a program needn't handle non-finite values.
Results may differ from a plain program's by a relative error of at most 0.0053.
Values may be sent and summed in bfloat16 or wider, within the bound.
No kernel may reach another device: no remote copies, remote signals or barrier semaphores. Data moves between devices by JAX's collectives and lax.ppermute only.
A program may use at most 128 MiB of HBM per device.

v0:
```python
import math

import jax
import jax.numpy as jnp
from jax import lax
from jax.sharding import PartitionSpec as P

BLK = 128


def side_by_side(arrays, axis, split_dim, concat_dim, along):
    both = jnp.concatenate(arrays, axis=along)
    out, at, finished = (
        lax.all_to_all(both, axis, split_axis=split_dim, concat_axis=concat_dim, tiled=True),
        0,
        [],
    )
    for a in arrays:
        finished.append(lax.slice_in_dim(out, at, at + a.shape[along], axis=along))
        at += a.shape[along]
    return tuple(finished)


def padded_2(x, sides, width):
    for axis, dim in sides:
        size, length = (lax.axis_size(axis), x.shape[dim])
        up = [(i, (i + 1) % size) for i in range(size - 1)]
        down = [(j, i) for i, j in up]
        last = lax.slice_in_dim(x, length - width, length, axis=dim)
        initial = lax.slice_in_dim(x, 0, width, axis=dim)
        before = lax.ppermute(last, axis, up)
        after = lax.ppermute(initial, axis, down)
        x = jnp.concatenate([before, x, after], axis=dim)
    return x


def passed_along(value, axis, steps):
    count = lax.axis_size(axis)
    initial, last = (max(0, -steps), min(count, count - steps))
    return lax.ppermute(value, axis, [(source, source + steps) for source in range(initial, last)])


def window_stack(blocks, block_count, tile_span):
    return jnp.stack([blocks[offset : offset + block_count] for offset in range(tile_span)], 1)


def attend_grad(query_matrix, key_ext, value_ext, output_gradient, active, logit_scale):
    block_count = query_matrix.shape[0]
    tile_span = active.shape[1]
    windowed_keys = window_stack(key_ext, block_count, tile_span)
    windowed_values = window_stack(value_ext, block_count, tile_span)
    attention_logits = (
        jnp.einsum(
            "mip,mejp->meij", query_matrix, windowed_keys, preferred_element_type=jnp.float32
        )
        * logit_scale
    )
    masked = jnp.where(active[:, :, None, None], attention_logits, -jnp.inf)
    row_top = jnp.max(masked, axis=(1, 3), keepdims=True)
    weights = jnp.exp(masked - row_top)
    denom_sum = jnp.sum(weights, axis=(1, 3), keepdims=True)
    prob_f = weights / denom_sum
    backward_probability = prob_f.astype(jnp.bfloat16)
    probability_gradient = jnp.einsum(
        "mip,mejp->meij", output_gradient, windowed_values, preferred_element_type=jnp.float32
    )
    row_delta = jnp.sum(prob_f * probability_gradient, axis=(1, 3), keepdims=True)
    score_gradient = (prob_f * (probability_gradient - row_delta)).astype(jnp.bfloat16)
    query_gradient_rows = (
        jnp.einsum(
            "luar,lurs->las", score_gradient, windowed_keys, preferred_element_type=jnp.float32
        )
        * logit_scale
    )
    windowed_key_gradient = (
        jnp.einsum(
            "gxin,gie->gxne", score_gradient, query_matrix, preferred_element_type=jnp.float32
        )
        * logit_scale
    )
    windowed_value_gradient = jnp.einsum(
        "gxin,gie->gxne", backward_probability, output_gradient, preferred_element_type=jnp.float32
    )
    key_grad = sum(
        (
            jnp.pad(
                windowed_key_gradient[:, offset], ((offset, tile_span - 1 - offset), (0, 0), (0, 0))
            )
            for offset in range(tile_span)
        )
    )
    value_grad = sum(
        (
            jnp.pad(
                windowed_value_gradient[:, offset],
                ((offset, tile_span - 1 - offset), (0, 0), (0, 0)),
            )
            for offset in range(tile_span)
        )
    )
    return (query_gradient_rows, key_grad, value_grad)


def block_mask(tile_mask, head_index, first_block, block_count, all_blocks):
    tile_span = tile_mask.shape[2]
    reach_blocks = tile_span // 2
    mask_head = lax.dynamic_index_in_dim(tile_mask, head_index, 0, keepdims=False)
    padded = jnp.pad(mask_head, ((2 * reach_blocks, 2 * reach_blocks), (0, 0)))
    local_mask = lax.dynamic_slice_in_dim(padded, first_block + 2 * reach_blocks, block_count, 0)
    query_block = first_block + jnp.arange(block_count, dtype=jnp.int32)
    offsets = jnp.arange(tile_span, dtype=jnp.int32) - reach_blocks
    key_block = query_block[:, None] + offsets[None, :]
    key_ok = (key_block >= 0) & (key_block < all_blocks)
    query_ok = (query_block >= 0) & (query_block < all_blocks)
    return jnp.where(query_ok[:, None], (local_mask != 0) & key_ok, offsets[None, :] == 0)


def shards(query, key, value, dout, tile_mask):
    n_uly = lax.axis_size("uly")
    tok_rows, model_width = query.shape
    n_heads = tile_mask.shape[0]
    head_dim = model_width // n_heads
    tile_span = tile_mask.shape[2]
    reach_blocks = tile_span // 2
    block_rows = BLK
    slab_rows = tok_rows * n_uly
    n_blocks = slab_rows // block_rows
    all_blocks = tile_mask.shape[1]
    logit_scale = 1.0 / math.sqrt(head_dim)
    rim_rows = reach_blocks * block_rows
    head_range = jnp.arange(n_heads, dtype=jnp.int32)
    slots_dev = (n_heads + n_uly - 1) // n_uly
    n_slots = n_uly * slots_dev
    slot_ids = jnp.arange(n_slots, dtype=jnp.int32)
    owners = slot_ids // slots_dev
    within = slot_ids % slots_dev
    dealt_head = within * n_uly + owners
    is_live = dealt_head < n_heads
    slot_head = jnp.minimum(dealt_head, n_heads - 1)
    head_hot = (slot_head[:, None] == head_range[None, :]) & is_live[:, None]
    slot_of_head = jnp.sum(jnp.where(head_hot, slot_ids[:, None], 0), 0)
    live_cast = is_live.astype(jnp.bfloat16)[None, :, None]

    def outgoing(source):
        return jnp.take(source.reshape(tok_rows, n_heads, head_dim), slot_head, axis=1) * live_cast

    k_recv, v_recv = side_by_side((outgoing(key), outgoing(value)), "uly", 1, 0, 2)
    q_recv, g_recv = side_by_side((outgoing(query), outgoing(dout)), "uly", 1, 0, 2)
    my_uly = lax.axis_index("uly")
    my_ctx = lax.axis_index("ctx")
    mine_head = lax.dynamic_slice_in_dim(slot_head, my_uly * slots_dev, slots_dev)
    pair_rows = padded_2(jnp.stack((k_recv, v_recv), 1), (("ctx", 0),), rim_rows)
    query_ext = 0
    n_query = n_blocks + 2 * query_ext
    n_keys = n_query + 2 * reach_blocks
    first_block = my_ctx * n_blocks - query_ext
    query_list = []
    pair_list = []
    for slot_index in range(slots_dev):
        q_rows = q_recv[:, slot_index]
        k_rows = pair_rows[:, 0, slot_index]
        v_rows = pair_rows[:, 1, slot_index]
        g_rows = g_recv[:, slot_index]
        active = block_mask(tile_mask, mine_head[slot_index], first_block, n_query, all_blocks)
        query_gradient_rows, key_grad, value_grad = attend_grad(
            q_rows.reshape(n_query, block_rows, head_dim),
            k_rows.reshape(n_keys, block_rows, head_dim),
            v_rows.reshape(n_keys, block_rows, head_dim),
            g_rows.reshape(n_query, block_rows, head_dim),
            active,
            logit_scale,
        )
        pair_grad = jnp.stack(
            (
                key_grad.reshape(n_keys * block_rows, head_dim),
                value_grad.reshape(n_keys * block_rows, head_dim),
            ),
            1,
        )
        result = (query_gradient_rows.reshape(n_query * block_rows, head_dim), pair_grad)
        query_list.append(result[0])
        pair_list.append(result[1])
    query_grads = jnp.stack(query_list, 1).astype(jnp.bfloat16)
    pair_grads = jnp.stack(pair_list, 2)
    own_rows = pair_grads[rim_rows : rim_rows + slab_rows]
    lower_rim = pair_grads[:rim_rows]
    upper_rim = pair_grads[rim_rows + slab_rows :]
    from_next = passed_along(lower_rim.astype(jnp.bfloat16), "ctx", -1).astype(lower_rim.dtype)
    from_prev = passed_along(upper_rim.astype(jnp.bfloat16), "ctx", 1).astype(upper_rim.dtype)
    own_rows = own_rows.at[:rim_rows].add(from_prev).at[slab_rows - rim_rows :].add(from_next)
    summed = own_rows.astype(jnp.bfloat16)
    back_query, back_key, back_value = (
        lax.all_to_all(query_grads, "uly", split_axis=0, concat_axis=1, tiled=True),
        lax.all_to_all(summed[:, 0], "uly", split_axis=0, concat_axis=1, tiled=True),
        lax.all_to_all(summed[:, 1], "uly", split_axis=0, concat_axis=1, tiled=True),
    )

    def to_tokens(source):
        return jnp.take(source, slot_of_head, axis=1).reshape(tok_rows, model_width)

    return (to_tokens(back_query), to_tokens(back_key), to_tokens(back_value))


def solution(mesh):
    placed = (
        P(("ctx", "uly"), None),
        P(("ctx", "uly"), None),
        P(("ctx", "uly"), None),
        P(("ctx", "uly"), None),
        P(),
    )
    return jax.shard_map(
        shards,
        mesh=mesh,
        in_specs=placed,
        out_specs=(P(("ctx", "uly"), None), P(("ctx", "uly"), None), P(("ctx", "uly"), None)),
        check_vma=False,
    )
```

profile of v0, /device:TPU:105, one launch (start us, length us, event | category | flops | bytes accessed | tf_op | source)
XLA Modules:
  0.0 494.5 jit_solution(14092440839744375791)
XLA Ops:
  3.8 2.4 copy.182
  8.0 1.9 gather_fusion.2
  10.0 2.0 gather_fusion
  13.5 2.0 gather_fusion.1
  17.0 1.9 copy.190
  18.9 2.0 gather_fusion.3
  20.9 4.0 bitcast_multiply_fusion.4
  24.9 2.1 pad_maximum_fusion.3
  27.0 9.1 %all-to-all-start.1 = ((bf16[128,48,256]{2,0,1:T(8,128)(2,1)}), bf16[128,48,256]{2,0,1:T(8,128)(2,1)S(1)}, u32[]{:S(2)}, u32[]{:S(2)}) async-start(bf16[128,48,256]{2,0,1:T(8,128)(2,1)} %pad_maximum_fusion.3), calls=%async_computation.1 | async-start | bytes 6291456 | tf_op jit(solution)/shard_map/all_to_all | solution.py:14
  36.1 4.0 pad_maximum_fusion.2
  40.1 70.9 %all-to-all-done.1 = bf16[128,48,256]{2,0,1:T(8,128)(2,1)S(1)} async-done(((bf16[128,48,256]{2,0,1:T(8,128)(2,1)}), bf16[128,48,256]{2,0,1:T(8,128)(2,1)S(1)}, u32[]{:S(2)}, u32[]{:S(2)}) %all-to-all-start.1) | async-done | bytes 3145760 | tf_op jit(solution)/shard_map/all_to_all | solution.py:14
  112.7 5.9 %all-to-all-start = ((bf16[128,48,256]{2,0,1:T(8,128)(2,1)}), bf16[128,48,256]{2,0,1:T(8,128)(2,1)S(1)}, u32[]{:S(2)}, u32[]{:S(2)}) async-start(bf16[128,48,256]{2,0,1:T(8,128)(2,1)} %pad_maximum_fusion.2), calls=%async_computation | async-start | bytes 6291456 | tf_op jit(solution)/shard_map/all_to_all | solution.py:14
  126.4 2.2 copy.191
  128.6 1.9 fusion.53
  130.5 59.8 %all-to-all-done = bf16[128,48,256]{2,0,1:T(8,128)(2,1)S(1)} async-done(((bf16[128,48,256]{2,0,1:T(8,128)(2,1)}), bf16[128,48,256]{2,0,1:T(8,128)(2,1)S(1)}, u32[]{:S(2)}, u32[]{:S(2)}) %all-to-all-start) | async-done | bytes 3145760 | tf_op jit(solution)/shard_map/all_to_all | solution.py:14
  191.2 2.7 collective-permute-start.1
  193.9 3.3 collective-permute-start
  197.3 3.5 collective-permute-done.1
  210.9 2.0 fusion.10
  218.5 2.0 fusion.20
  220.4 3.1 fusion.4
  223.5 2.0 fusion.6
  233.1 5.7 %fusion = (f32[16,128]{1,0:T(8,128)S(1)}, f32[16,5,128,128]{3,2,1,0:T(8,128)}) fusion(f32[16,128]{1,0:T(8,128)S(1)} %fusion.17, f32[16,128]{1,0:T(8,128)S(1)} %get-tuple-element.130, f32[16,5,128,128]{3,2,1,0:T(8,128)S(1)} %get-tuple-element.131, pred[16,5]{1,0:T(8,128)(4,1)S(1)} %copy.197, bf16[16,5,128,128]{3,2,1,0:T(8,128)(2,1)} %copy-done.36, ...), kind=kOutput, calls=%fused_computation.10 | convolution fusion | flops 343406592 | bytes 13656144 | tf_op jit(solution)/shard_map/mip,mejp->meij/dot_general | solution.py:64
  238.8 3.9 fusion.2
  243.7 3.2 broadcast_multiply_fusion
  246.9 2.3 slice_bitcast_fusion.28
  249.3 8.1 %copy.199 = bf16[2048,1,128]{2,1,0:T(2,128)(2,1)S(1)} copy(bf16[2048,1,128]{2,0,1:T(8,128)(2,1)S(1)} %bitcast.429) | data formatting | bytes 1048576 | tf_op jit(solution)/shard_map/stack;reshape | solution.py:183
  257.4 2.4 slice_bitcast_fusion.33
  259.8 2.4 slice_bitcast_fusion.18
  262.2 8.3 %copy.200 = bf16[2048,1,128]{2,1,0:T(2,128)(2,1)S(1)} copy(bf16[2048,1,128]{2,0,1:T(8,128)(2,1)S(1)} %bitcast.430) | data formatting | bytes 1048576 | tf_op jit(solution)/shard_map/stack;reshape | solution.py:183
  270.5 2.4 slice_bitcast_fusion.23
  272.9 2.3 slice_bitcast_fusion.8
  275.2 8.1 %copy.201 = bf16[2048,1,128]{2,1,0:T(2,128)(2,1)S(1)} copy(bf16[2048,1,128]{2,0,1:T(8,128)(2,1)S(1)} %bitcast.431) | data formatting | bytes 1048576 | tf_op jit(solution)/shard_map/stack;reshape | solution.py:183
  283.3 4.5 pad_maximum_fusion.7
  287.9 9.8 %all-to-all-start.2 = ((bf16[2048,3,128]{2,1,0:T(4,128)(2,1)}), bf16[2048,3,128]{2,1,0:T(4,128)(2,1)S(1)}, u32[]{:S(2)}, u32[]{:S(2)}) async-start(bf16[2048,3,128]{2,1,0:T(4,128)(2,1)} %pad_maximum_fusion.7), calls=%async_computation.2 | async-start | bytes 4194304 | tf_op jit(solution)/shard_map/all_to_all | solution.py:193
  297.8 3.3 slice_bitcast_fusion.13
  313.3 7.2 %fusion.49 = bf16[2560,2,3,128]{3,2,0,1:T(4,128)(2,1)S(1)} fusion(f32[2560,2,1,128]{3,2,0,1:T(1,128)S(1)} %bitcast.368, f32[2560,2,1,128]{3,2,0,1:T(1,128)S(1)} %bitcast.366, f32[2560,2,1,128]{3,2,0,1:T(1,128)S(1)} %bitcast.364), kind=kLoop, calls=%fused_computation.194 | loop fusion | flops 11796480 | bytes 11796480 | tf_op jit(solution)/shard_map/convert.1
  320.8 3.8 collective-permute-start.3
  324.6 3.1 collective-permute-start.2
  327.7 7.2 %pad_maximum_fusion = f32[2560,2,3,128]{3,2,0,1:T(4,128)S(1)} fusion(f32[2560,2,1,128]{3,2,0,1:T(1,128)S(1)} %bitcast.369, f32[2560,2,1,128]{3,2,0,1:T(1,128)S(1)} %bitcast.367, f32[2560,2,1,128]{3,2,0,1:T(1,128)S(1)} %bitcast.365), kind=kLoop, calls=%fused_computation.7 | loop fusion | flops 3932160 | bytes 15728640 | tf_op jit(solution)/shard_map/stack | solution.py:184
  338.7 2.8 slice_bitcast_fusion
  341.6 4.2 all-to-all-done.2
  345.8 53.7 %all_to_all.90 = bf16[2048,3,128]{2,1,0:T(4,128)(2,1)} all-to-all(bf16[2048,3,128]{2,1,0:T(4,128)(2,1)} %get-tuple-element.70), channel_id=1, replica_groups=mesh['ctx'=16,'uly'=16] {'uly'}, dimensions={0} | all-to-all | bytes 3145728 | tf_op jit(solution)/shard_map/all_to_all | solution.py:195
  399.5 36.7 %all-to-all-start.3 = ((bf16[2048,3,128]{2,1,0:T(4,128)(2,1)}), bf16[2048,3,128]{2,1,0:T(4,128)(2,1)}, u32[]{:S(2)}, u32[]{:S(2)}) async-start(bf16[2048,3,128]{2,1,0:T(4,128)(2,1)} %get-tuple-element.71), calls=%async_computation.3 | async-start | bytes 4194304 | tf_op jit(solution)/shard_map/all_to_all | solution.py:194
  438.0 3.3 gather_fusion.4
  441.6 1.8 gather_fusion.6
  443.4 34.2 %all-to-all-done.3 = bf16[2048,3,128]{2,1,0:T(4,128)(2,1)} async-done(((bf16[2048,3,128]{2,1,0:T(4,128)(2,1)}), bf16[2048,3,128]{2,1,0:T(4,128)(2,1)}, u32[]{:S(2)}, u32[]{:S(2)}) %all-to-all-start.3) | async-done | bytes 1572896 | tf_op jit(solution)/shard_map/all_to_all | solution.py:194
  481.4 4.0 select_bitcast_fusion
  (190 shorter events, 66.9 us)
Async XLA Ops:
  1.3 117.3 %copy-start.38 = (s32[48]{0:T(128)}, s32[48]{0:T(128)S(1)}, u32[]{:S(2)}) copy-start(s32[48]{0:T(128)S(1)} %get-tuple-element.143) | copy-start | bytes 580
  10.0 2.0 copy-start.30
  13.5 2.0 copy-start.31
  17.0 3.9 copy-start.2
  27.0 84.0 %all-to-all-start.1 = ((bf16[128,48,256]{2,0,1:T(8,128)(2,1)}), bf16[128,48,256]{2,0,1:T(8,128)(2,1)S(1)}, u32[]{:S(2)}, u32[]{:S(2)}) async-start(bf16[128,48,256]{2,0,1:T(8,128)(2,1)} %pad_maximum_fusion.3), calls=%async_computation.1 | async-start | bytes 6291456 | tf_op jit(solution)/shard_map/all_to_all | solution.py:14
  111.0 1.7 copy-start
  112.7 77.6 %all-to-all-start = ((bf16[128,48,256]{2,0,1:T(8,128)(2,1)}), bf16[128,48,256]{2,0,1:T(8,128)(2,1)S(1)}, u32[]{:S(2)}, u32[]{:S(2)}) async-start(bf16[128,48,256]{2,0,1:T(8,128)(2,1)} %pad_maximum_fusion.2), calls=%async_computation | async-start | bytes 6291456 | tf_op jit(solution)/shard_map/all_to_all | solution.py:14
  191.2 9.6 %collective-permute-start.1 = (bf16[256,2,3,128]{3,0,2,1:T(8,128)(2,1)S(1)}, bf16[256,2,3,128]{3,0,2,1:T(8,128)(2,1)S(1)}, u32[]{:S(2)}, u32[]{:S(2)}) collective-permute-start(bf16[256,2,3,128]{3,0,2,1:T(8,128)(2,1)S(1)} %get-tuple-element.104), channel_id=1, source_target_pairs={{16,0},{32,16},{48,32},{64,48},{80,64},{96,80},{112,96},{128,112},... | collective-permute-start | bytes 1179656 | tf_op jit(solution)/shard_map/ppermute | solution.py:32
  193.9 7.8 %collective-permute-start = (bf16[256,2,3,128]{3,0,2,1:T(8,128)(2,1)S(1)}, bf16[256,2,3,128]{3,0,2,1:T(8,128)(2,1)S(1)}, u32[]{:S(2)}, u32[]{:S(2)}) collective-permute-start(bf16[256,2,3,128]{3,0,2,1:T(8,128)(2,1)S(1)} %get-tuple-element.105), channel_id=1, source_target_pairs={{0,16},{16,32},{32,48},{48,64},{64,80},{80,96},{96,112},{112,128},... | collective-permute-start | bytes 1179656 | tf_op jit(solution)/shard_map/ppermute | solution.py:31
  204.4 1.0 copy-start.5
  206.3 1.3 copy-start.34
  215.1 1.2 copy-start.4
  215.2 1.9 copy-start.35
  217.2 1.3 copy-start.33
  227.8 1.6 copy-start.3
  227.9 1.5 copy-start.36
  230.3 1.3 copy-start.32
  287.9 57.9 %all-to-all-start.2 = ((bf16[2048,3,128]{2,1,0:T(4,128)(2,1)}), bf16[2048,3,128]{2,1,0:T(4,128)(2,1)S(1)}, u32[]{:S(2)}, u32[]{:S(2)}) async-start(bf16[2048,3,128]{2,1,0:T(4,128)(2,1)} %pad_maximum_fusion.7), calls=%async_computation.2 | async-start | bytes 4194304 | tf_op jit(solution)/shard_map/all_to_all | solution.py:193
  297.7 3.3 copy-start.15
  297.7 3.3 copy-start.16
  297.7 3.4 copy-start.17
  297.7 3.7 copy-start.18
  297.7 4.0 copy-start.19
  301.8 1.2 copy-start.25
  301.8 1.5 copy-start.26
  301.8 1.9 copy-start.27
  301.8 2.2 copy-start.28
  301.8 2.5 copy-start.29
  304.7 1.2 copy-start.10
  304.7 1.5 copy-start.11
  304.7 1.8 copy-start.12
  304.7 2.1 copy-start.13
  304.7 2.5 copy-start.14
  307.2 1.2 copy-start.20
  307.2 1.5 copy-start.21
  307.2 1.9 copy-start.22
  307.2 2.2 copy-start.23
  307.2 2.5 copy-start.24
  310.1 1.2 copy-start.6
  310.1 1.5 copy-start.7
  310.1 1.8 copy-start.8
  310.1 2.1 copy-start.9
  320.8 16.0 %collective-permute-start.3 = (bf16[256,2,3,128]{3,2,0,1:T(4,128)(2,1)S(1)}, bf16[256,2,3,128]{3,2,0,1:T(4,128)(2,1)S(1)}, u32[]{:S(2)}, u32[]{:S(2)}) collective-permute-start(bf16[256,2,3,128]{3,2,0,1:T(4,128)(2,1)S(1)} %get-tuple-element.38), channel_id=1, source_target_pairs={{16,0},{32,16},{48,32},{64,48},{80,64},{96,80},{112,96},{128,112},... | collective-permute-start | bytes 1179656 | tf_op jit(solution)/shard_map/ppermute | solution.py:40
  324.6 11.9 %collective-permute-start.2 = (bf16[256,2,3,128]{3,2,0,1:T(4,128)(2,1)S(1)}, bf16[256,2,3,128]{3,2,0,1:T(4,128)(2,1)S(1)}, u32[]{:S(2)}, u32[]{:S(2)}) collective-permute-start(bf16[256,2,3,128]{3,2,0,1:T(4,128)(2,1)S(1)} %get-tuple-element.39), channel_id=1, source_target_pairs={{0,16},{16,32},{32,48},{48,64},{64,80},{80,96},{96,112},{112,128},... | collective-permute-start | bytes 1179656 | tf_op jit(solution)/shard_map/ppermute | solution.py:40
  399.5 36.7 %copy-start.37 = (pred[48]{0:T(512)(128)(4,1)S(1)}, pred[48]{0:T(512)(128)(4,1)}, u32[]{:S(2)}) copy-start(pred[48]{0:T(512)(128)(4,1)} %get-tuple-element.145) | copy-start | bytes 148
  399.5 36.8 %copy-start.39 = (s32[48]{0:T(128)S(1)}, s32[48]{0:T(128)}, u32[]{:S(2)}) copy-start(s32[48]{0:T(128)} %copy-done.38) | copy-start | bytes 580
  399.5 78.1 %all-to-all-start.3 = ((bf16[2048,3,128]{2,1,0:T(4,128)(2,1)}), bf16[2048,3,128]{2,1,0:T(4,128)(2,1)}, u32[]{:S(2)}, u32[]{:S(2)}) async-start(bf16[2048,3,128]{2,1,0:T(4,128)(2,1)} %get-tuple-element.71), calls=%async_computation.3 | async-start | bytes 4194304 | tf_op jit(solution)/shard_map/all_to_all | solution.py:194
  436.6 4.6 copy-start.1
where the time goes:
time: 501 us; the launch traced here: 495 us
  waiting for transfers between devices  173 us (35%)
  local copies, waits for them, and re-layouts  107 us (21%)
  starting transfers between devices  74.5 us (15%)
  blocking collectives  53.7 us (11%)
  other arithmetic  51.3 us (10%)
  matrix products  26.1 us (5%)
  between operations  8.1 us (2%)
    all_to_all x2, waiting for transfers between devices, side_by_side(): lax.all_to_all(both, axis, split_axis=split_dim, concat_axis=concat_dim,...  131 us
    all_to_all x1, blocking collectives, shards(): lax.all_to_all(summed[:, 1], 'uly', split_axis=0, concat_axis=1, tiled=True)  53.7 us
    all_to_all x1, starting transfers between devices, shards(): lax.all_to_all(summed[:, 0], 'uly', split_axis=0, concat_axis=1, tiled=True)  36.7 us
    all_to_all x1, waiting for transfers between devices, shards(): lax.all_to_all(summed[:, 0], 'uly', split_axis=0, concat_axis=1, tiled=True)  34.2 us
    unnamed x114, local copies, waits for them, and re-layouts  25.7 us
    another operation x3, local copies, waits for them, and re-layouts, shards(): query_grads = jnp.stack(query_list, 1).astype(jnp.bfloat16)  24.5 us
    all_to_all x2, starting transfers between devices, side_by_side(): lax.all_to_all(both, axis, split_axis=split_dim, concat_axis=concat_dim,...  15 us
    dot_general x3, matrix products, attend_grad(): jnp.einsum('mip,mejp->meij', output_gradient, windowed_values, preferred_...  10.5 us
  transfers between devices with their start and end apart: 8, of which 6 were waited for; matrix products, arithmetic and copies ran while one was open for 9% of the time, Pallas kernels for 0%

commit v1 on v0

v1 whole, which is shorter than its diff:
```python
import math

import jax
import jax.numpy as jnp
from jax import lax
from jax.experimental import pallas as pl
from jax.experimental.pallas import tpu as pltpu
from jax.sharding import PartitionSpec as P


BLK = 128
HD = 128
NZ = 4
CHUNKS = ((0, 6), (6, 4))
CW = 256
SCALE = 1.0 / math.sqrt(HD)
EXP2_SCALE = SCALE / math.log(2.0)
BF = jnp.bfloat16
F32 = jnp.float32


MIB = 1 << 20


def grant(mib):
    return pltpu.CompilerParams(vmem_limit_bytes=mib * MIB)


def cost(flops, nbytes):
    return pl.CostEstimate(flops=flops, bytes_accessed=nbytes, transcendentals=0)


def pack_body(zh, a1, a2, a3, b1, b2, b3, o1, o2, o3):
    for a, b, o in ((a1, b1, o1), (a2, b2, o2), (a3, b3, o3)):
        o[0] = a[...]
        o[1] = b[...]


def pack(zh, a, b, first, heads, group):
    per, off, steps = group * HD // CW, first * HD // CW, heads * HD // CW

    def src(s):
        return pl.BlockSpec((BLK, CW), lambda i, z: (0, lax.rem(z[0] + s, NZ) * per + off + i))

    out = pl.BlockSpec((2, BLK, CW), lambda i, z: (0, 0, i))
    n = heads * HD
    return pl.pallas_call(
        pack_body,
        grid_spec=pltpu.PrefetchScalarGridSpec(
            num_scalar_prefetch=1,
            grid=(steps,),
            in_specs=[src(1), src(2), src(3), src(1), src(2), src(3)],
            out_specs=[out, out, out],
        ),
        out_shape=[jax.ShapeDtypeStruct((2, BLK, n), BF)] * 3,
        cost_estimate=cost(0, 12 * BLK * n * 2),
        compiler_params=grant(8),
    )(zh, a, a, a, b, b, b)


def unpack_body(zh, k, v, r1, r2, r3, lo, hi):
    z = zh[0]
    for s, (kk, vv) in enumerate(((k, v), (r1.at[0], r1.at[1]), (r2.at[0], r2.at[1]), (r3.at[0], r3.at[1]))):
        b = lax.rem(z + NZ - s, NZ)

        @pl.when(b < 2)
        def _():
            lo[b, 0] = kk[...]
            lo[b, 1] = vv[...]

        @pl.when(b >= 2)
        def _():
            hi[b - 2, 0] = kk[...]
            hi[b - 2, 1] = vv[...]


def unpack(zh, k, v, recv, group):
    n = group * HD
    per = n // CW
    own = pl.BlockSpec((BLK, CW), lambda i, z: (0, z[0] * per + i))
    got = pl.BlockSpec((2, BLK, CW), lambda i, z: (0, 0, i))
    half = pl.BlockSpec((2, 2, BLK, CW), lambda i, z: (0, 0, 0, i))
    return pl.pallas_call(
        unpack_body,
        grid_spec=pltpu.PrefetchScalarGridSpec(
            num_scalar_prefetch=1, grid=(per,), in_specs=[own, own, got, got, got], out_specs=[half, half]
        ),
        out_shape=[jax.ShapeDtypeStruct((2, 2, BLK, n), BF)] * 2,
        cost_estimate=cost(0, 16 * BLK * n * 2),
        compiler_params=grant(10),
        name="unpack",
    )(zh, k, v, *recv)


def attend_body(zh, q0, g0, x1, x2, x3, before, lo, hi, after, bias,
                dq0, dq1, dq2, dq3, rim_before, rim_after, own,
                qs, gs, ks, vs, dqs, dk, dv):
    z = zh[0]
    for s, (qq, gg) in enumerate(((q0, g0), (x1.at[0], x1.at[1]), (x2.at[0], x2.at[1]), (x3.at[0], x3.at[1]))):
        row = pl.multiple_of(lax.rem(z + NZ - s, NZ) * BLK, BLK)
        qs[pl.ds(row, BLK), :] = qq[...]
        gs[pl.ds(row, BLK), :] = gg[...]
    for i, (ref, j) in enumerate(
        ((before, 0), (before, 1), (lo, 0), (lo, 1), (hi, 0), (hi, 1), (after, 0), (after, 1))
    ):
        ks[i * BLK : (i + 1) * BLK, :] = ref[j, 0]
        vs[i * BLK : (i + 1) * BLK, :] = ref[j, 1]
    nt = (((1,), (1,)), ((), ()))
    tn = (((0,), (0,)), ((), ()))
    nn = (((1,), (0,)), ((), ()))
    for pair in range(2):
        r0 = pair * 2 * BLK
        kw, vw = ks[r0 : r0 + 6 * BLK, :], vs[r0 : r0 + 6 * BLK, :]
        q, g = qs[r0 : r0 + 2 * BLK, :], gs[r0 : r0 + 2 * BLK, :]
        st = lax.dot_general(kw, q, nt, preferred_element_type=F32)
        st = st.reshape(6, BLK, 2 * BLK) + bias[0, pair][:, None, :]
        top = jnp.max(jnp.max(st, axis=0), axis=0, keepdims=True)[None]
        e = jnp.exp2((st - top) * EXP2_SCALE)
        total = jnp.sum(jnp.sum(e, axis=0), axis=0, keepdims=True)[None]
        p = e * (1.0 / total)
        dp = lax.dot_general(vw, g, nt, preferred_element_type=F32).reshape(6, BLK, 2 * BLK)
        delta = jnp.sum(jnp.sum(p * dp, axis=0), axis=0, keepdims=True)[None]
        ds = (p * (dp - delta)).astype(BF).reshape(6 * BLK, 2 * BLK)
        pb = p.astype(BF).reshape(6 * BLK, 2 * BLK)
        dvw = lax.dot_general(pb, g, nn, preferred_element_type=F32)
        dkw = lax.dot_general(ds, q, nn, preferred_element_type=F32)
        dqw = lax.dot_general(ds, kw, tn, preferred_element_type=F32) * SCALE
        dqs[2 * pair] = dqw[:BLK].astype(BF)
        dqs[2 * pair + 1] = dqw[BLK:].astype(BF)
        if pair == 0:
            dk[: 6 * BLK, :] = dkw
            dv[: 6 * BLK, :] = dvw
        else:
            dk[2 * BLK : 6 * BLK, :] += dkw[: 4 * BLK]
            dv[2 * BLK : 6 * BLK, :] += dvw[: 4 * BLK]
            dk[6 * BLK :, :] = dkw[4 * BLK :]
            dv[6 * BLK :, :] = dvw[4 * BLK :]
    for s, o in enumerate((dq0, dq1, dq2, dq3)):
        o[...] = dqs[lax.rem(z + s, NZ)]
    for j in range(2):
        rim_before[j, 0] = (dk[j * BLK : (j + 1) * BLK, :] * SCALE).astype(BF)
        rim_before[j, 1] = dv[j * BLK : (j + 1) * BLK, :].astype(BF)
        rim_after[j, 0] = (dk[(6 + j) * BLK : (7 + j) * BLK, :] * SCALE).astype(BF)
        rim_after[j, 1] = dv[(6 + j) * BLK : (7 + j) * BLK, :].astype(BF)
    for j in range(4):
        own[j, 0] = dk[(2 + j) * BLK : (3 + j) * BLK, :] * SCALE
        own[j, 1] = dv[(2 + j) * BLK : (3 + j) * BLK, :]


def attend(zh, q, g, recv, before, lo, hi, after, bias, first, heads, group):
    n = heads * HD
    mine = pl.BlockSpec((BLK, HD), lambda h, z: (0, z[0] * group + first + h))
    got = pl.BlockSpec((2, BLK, HD), lambda h, z: (0, 0, h))
    keys = pl.BlockSpec((2, 2, BLK, HD), lambda h, z: (0, 0, 0, first + h))
    flat = pl.BlockSpec((BLK, HD), lambda h, z: (0, h))
    rim = pl.BlockSpec((2, 2, BLK, HD), lambda h, z: (0, 0, 0, h))
    own = pl.BlockSpec((4, 2, BLK, HD), lambda h, z: (0, 0, 0, h))
    shape = jax.ShapeDtypeStruct
    return pl.pallas_call(
        attend_body,
        grid_spec=pltpu.PrefetchScalarGridSpec(
            num_scalar_prefetch=1,
            grid=(heads,),
            in_specs=[mine, mine, got, got, got, keys, keys, keys, keys,
                      pl.BlockSpec((1, 2, 6, 2 * BLK), lambda h, z: (first + h, 0, 0, 0))],
            out_specs=[flat] * 4 + [rim, rim, own],
            scratch_shapes=[
                pltpu.VMEM((4 * BLK, HD), BF),
                pltpu.VMEM((4 * BLK, HD), BF),
                pltpu.VMEM((8 * BLK, HD), BF),
                pltpu.VMEM((8 * BLK, HD), BF),
                pltpu.VMEM((4, BLK, HD), BF),
                pltpu.VMEM((8 * BLK, HD), F32),
                pltpu.VMEM((8 * BLK, HD), F32),
            ],
        ),
        out_shape=[shape((BLK, n), BF)] * 4
        + [shape((2, 2, BLK, n), BF)] * 2
        + [shape((4, 2, BLK, n), F32)],
        cost_estimate=cost(heads * 2 * 5 * 2 * 768 * 256 * 128, 40 * BLK * n * 2),
        compiler_params=grant(24),
    )(zh, q, g, *recv, before, lo, hi, after, bias)


def finish_body(zh, own, from_before, from_after, o0, o1, o2, o3):
    z = zh[0]
    for s, o in enumerate((o0, o1, o2, o3)):
        b = lax.rem(z + s, NZ)

        @pl.when(b < 2)
        def _():
            o[...] = (own[b] + from_before[b].astype(F32)).astype(BF)

        @pl.when(b >= 2)
        def _():
            o[...] = (own[b] + from_after[b - 2].astype(F32)).astype(BF)


def finish(zh, own, from_before, from_after):
    n = own.shape[-1]
    rim = pl.BlockSpec((2, 2, BLK, CW), lambda i, z: (0, 0, 0, i))
    out = pl.BlockSpec((2, BLK, CW), lambda i, z: (0, 0, i))
    return pl.pallas_call(
        finish_body,
        grid_spec=pltpu.PrefetchScalarGridSpec(
            num_scalar_prefetch=1,
            grid=(n // CW,),
            in_specs=[pl.BlockSpec((4, 2, BLK, CW), lambda i, z: (0, 0, 0, i)), rim, rim],
            out_specs=[out] * 4,
        ),
        out_shape=[jax.ShapeDtypeStruct((2, BLK, n), BF)] * 4,
        cost_estimate=cost(0, 32 * BLK * n * 2),
        compiler_params=grant(12),
    )(zh, own, from_before, from_after)


def assemble_body(zh, *refs):
    n_chunks = len(CHUNKS)
    ins, outs = refs[: 8 * n_chunks], refs[8 * n_chunks :]
    t = pl.program_id(0)
    for s in range(NZ):

        @pl.when(t == s)
        def _():
            for c, (first, heads) in enumerate(CHUNKS):
                cols = slice(first * HD, (first + heads) * HD)
                outs[0][:, cols] = ins[8 * c + s][...]
                outs[1][:, cols] = ins[8 * c + 4 + s][0]
                outs[2][:, cols] = ins[8 * c + 4 + s][1]


def assemble(zh, parts, group, width):
    specs, args = [], []
    for dq, dkv in parts:
        for a in (*dq, *dkv):
            specs.append(pl.BlockSpec(a.shape, lambda t, z, nd=a.ndim: (0,) * nd))
            args.append(a)
    out = pl.BlockSpec((BLK, group * HD), lambda t, z: (0, lax.rem(z[0] + NZ - t, NZ)))
    return pl.pallas_call(
        assemble_body,
        grid_spec=pltpu.PrefetchScalarGridSpec(
            num_scalar_prefetch=1, grid=(NZ,), in_specs=specs, out_specs=[out] * 3
        ),
        out_shape=[jax.ShapeDtypeStruct((BLK, width), BF)] * 3,
        cost_estimate=cost(0, 6 * BLK * width * 2),
        compiler_params=grant(24),
        name="assemble",
    )(zh, *args)


def tile_bias(tile_mask, zh, slab, group):
    all_blocks, span = tile_mask.shape[1], tile_mask.shape[2]
    local = lax.dynamic_slice(tile_mask, (zh * group, slab * NZ, 0), (group, NZ, span))
    key_block = slab * NZ + jnp.arange(NZ, dtype=jnp.int32)[:, None] + jnp.arange(span, dtype=jnp.int32)[None] - span // 2
    active = (local != 0) & (key_block >= 0) & (key_block < all_blocks)
    active = active.reshape(group, 2, 2, span)
    left = jnp.pad(active[:, :, 0], ((0, 0), (0, 0), (0, 1)))
    right = jnp.pad(active[:, :, 1], ((0, 0), (0, 0), (1, 0)))
    rows = jnp.stack([left, right], -1)
    return jnp.repeat(jnp.where(rows, 0.0, -jnp.inf).astype(F32), BLK, axis=-1)


def shards(query, key, value, dout, tile_mask):
    n_ctx, n_uly = lax.axis_size("ctx"), lax.axis_size("uly")
    width = query.shape[1]
    group = tile_mask.shape[0] // NZ
    me = lax.axis_index("uly")
    zh_s = lax.rem(me, NZ)
    slab = lax.axis_index("ctx") * (n_uly // NZ) + me // NZ
    zh = zh_s.astype(jnp.int32).reshape(1)
    n_slabs = n_ctx * n_uly // NZ
    rings = [
        [(NZ * i + j, NZ * i + (j + s) % NZ) for i in range(n_uly // NZ) for j in range(NZ)] for s in range(NZ)
    ]
    up = [(NZ * i + j, NZ * (i + 1) + j) for i in range(n_slabs - 1) for j in range(NZ)]
    down = [(b, a) for a, b in up]

    def around(arrays):
        out = []
        for s, a in enumerate(arrays, 1):
            out.append(lax.ppermute(a, "uly", rings[s]))
        return out

    def to_next(a):
        return lax.ppermute(a, ("ctx", "uly"), up)

    def to_prev(a):
        return lax.ppermute(a, ("ctx", "uly"), down)

    bias = tile_bias(tile_mask, zh_s, slab, group)
    kv = around(pack(zh, key, value, 0, group, group))
    qg = []
    behind = kv
    for first, heads in CHUNKS:
        packed = list(pack(zh, query, dout, first, heads, group))
        for s in range(3):
            packed[s], _ = lax.optimization_barrier((packed[s], behind[s]))
        behind = around(packed)
        qg.append(behind)
    lo, hi = unpack(zh, key, value, kv, group)
    before, after = to_next(hi), to_prev(lo)
    parts = []
    for (first, heads), recv in zip(CHUNKS, qg):
        *dq, rim_before, rim_after, own = attend(
            zh, query, dout, recv, before, lo, hi, after, bias, first, heads, group
        )
        from_after, from_before = to_prev(rim_before), to_next(rim_after)
        back_q = [dq[0], *around(dq[1:])]
        dkv = finish(zh, own, from_before, from_after)
        back_kv = [dkv[0], *around(dkv[1:])]
        parts.append((back_q, back_kv))
    return assemble(zh, parts, group, width)


def solution(mesh):
    rows = P(("ctx", "uly"), None)
    return jax.shard_map(
        shards,
        mesh=mesh,
        in_specs=(rows, rows, rows, rows, P()),
        out_specs=(rows, rows, rows),
        check_vma=False,
    )
```

time: 501 us -> 277 us (0.55)
  the two profiles are of different devices: /device:TPU:105 before, /device:TPU:70 now
where the time goes in v1:
time: 277 us
  waiting for transfers between devices  161 us (58%)
  starting transfers between devices  70.5 us (25%)
  Pallas kernels  34.5 us (12%)
  local copies, waits for them, and re-layouts  9.17 us (3%)
    ppermute x21, waiting for transfers between devices, around(): out.append(lax.ppermute(a, 'uly', rings[s]))  160 us
    ppermute x21, starting transfers between devices, around(): out.append(lax.ppermute(a, 'uly', rings[s]))  52.8 us
    pallas_call x2, Pallas kernels, attend(): pl.pallas_call(attend_body, grid_spec=pltpu.PrefetchScalarGridSpec(num_sc...  25.4 us
    ppermute x3, starting transfers between devices, to_prev(): return lax.ppermute(a, ('ctx', 'uly'), down)  11 us
    ppermute x3, starting transfers between devices, to_next(): return lax.ppermute(a, ('ctx', 'uly'), up)  6.68 us
  transfers between devices with their start and end apart: 27, of which 10 were waited for; matrix products, arithmetic and copies ran while one was open for 2% of the time, Pallas kernels for 10%

profile of v1, /device:TPU:70, one launch (start us, length us, event | category | flops | bytes accessed | tf_op | source)
XLA Modules:
  0.0 277.0 jit_solution(594883053423810602)
XLA Ops:
  0.6 1.3 copy-done.2
  2.0 1.3 copy-done.4
  3.3 1.1 shard_map.77
  4.4 4.6 %collective-permute-start = (bf16[2,128,1280]{2,1,0:T(8,128)(2,1)S(1)}, bf16[2,128,1280]{2,1,0:T(8,128)(2,1)S(1)}, u32[]{:S(2)}, u32[]{:S(2)}) collective-permute-start(bf16[2,128,1280]{2,1,0:T(8,128)(2,1)S(1)} %get-tuple-element.43), channel_id=1, source_target_pairs={{0,1},{1,2},{2,3},{3,0},{4,5},{5,6},{6,7},{7,4},{8,9},{9,10},{10,1... | collective-permute-start | bytes 1966088 | tf_op jit(solution)/shard_map/ppermute | solution.py:281
  8.9 1.0 collective-permute-start.2
  9.9 2.8 %collective-permute-start.4 = (bf16[2,128,1280]{2,1,0:T(8,128)(2,1)S(1)}, bf16[2,128,1280]{2,1,0:T(8,128)(2,1)S(1)}, u32[]{:S(2)}, u32[]{:S(2)}) collective-permute-start(bf16[2,128,1280]{2,1,0:T(8,128)(2,1)S(1)} %get-tuple-element.49), channel_id=1, source_target_pairs={{0,3},{1,0},{2,1},{3,2},{4,7},{5,4},{6,5},{7,6},{8,11},{9,8},{10,9... | collective-permute-start | bytes 1966088 | tf_op jit(solution)/shard_map/ppermute | solution.py:281
  12.8 38.7 %collective-permute-done.r1 = bf16[2,128,1280]{2,1,0:T(8,128)(2,1)S(1)} collective-permute-done((bf16[2,128,1280]{2,1,0:T(8,128)(2,1)S(1)}, bf16[2,128,1280]{2,1,0:T(8,128)(2,1)S(1)}, u32[]{:S(2)}, u32[]{:S(2)}) %collective-permute-start) | collective-permute-done | bytes 655392 | tf_op jit(solution)/shard_map/ppermute | solution.py:281
  51.5 15.3 %collective-permute-done.2.r2 = bf16[2,128,1280]{2,1,0:T(8,128)(2,1)S(1)} collective-permute-done((bf16[2,128,1280]{2,1,0:T(8,128)(2,1)S(1)}, bf16[2,128,1280]{2,1,0:T(8,128)(2,1)S(1)}, u32[]{:S(2)}, u32[]{:S(2)}) %collective-permute-start.2) | collective-permute-done | bytes 655392 | tf_op jit(solution)/shard_map/ppermute | solution.py:281
  66.7 1.9 collective-permute-done.4.r3
  68.6 2.9 %unpack.1 = (bf16[2,2,128,1280]{3,2,1,0:T(8,128)(2,1)}, bf16[2,2,128,1280]{3,2,1,0:T(8,128)(2,1)}) custom-call(s32[1]{0:T(128)} %bitcast.zh, bf16[128,5120]{1,0:T(8,128)(2,1)S(1)} %copy-done.3, bf16[128,5120]{1,0:T(8,128)(2,1)S(1)} %copy-done.5, bf16[2,128,1280]{2,1,0:T(8,128)(2,1)S(1)} %collective-permute-done.r1, ...), custom_call_target="tpu_custom_call" | custom-call | bytes 5242880 | tf_op jit(solution)/shard_map/unpack/pallas_call | solution.py:83
  71.5 1.9 collective-permute-start.6
  73.4 3.9 %collective-permute-start.7 = (bf16[2,2,128,1280]{3,2,1,0:T(8,128)(2,1)}, bf16[2,2,128,1280]{3,2,1,0:T(8,128)(2,1)}, u32[]{:S(2)}, u32[]{:S(2)}) collective-permute-start(bf16[2,2,128,1280]{3,2,1,0:T(8,128)(2,1)} %get-tuple-element.52.lo), channel_id=1, source_target_pairs={{4,0},{5,1},{6,2},{7,3},{8,4},{9,5},{10,6},{11,7},{12,8},{13,9},{1... | collective-permute-start | bytes 3932168 | tf_op jit(solution)/shard_map/ppermute | solution.py:288
  81.4 0.9 fusion.1
  82.5 4.4 %collective-permute-start.3 = (bf16[2,128,768]{2,1,0:T(8,128)(2,1)}, bf16[2,128,768]{2,1,0:T(8,128)(2,1)}, u32[]{:S(2)}, u32[]{:S(2)}) collective-permute-start(bf16[2,128,768]{2,1,0:T(8,128)(2,1)} %copy-done.6), channel_id=1, source_target_pairs={{0,2},{1,3},{2,0},{3,1},{4,6},{5,7},{6,4},{7,5},{8,10},{9,11},{10,... | collective-permute-start | bytes 1179656 | tf_op jit(solution)/shard_map/ppermute | solution.py:281
  87.0 1.3 collective-permute-start.5
  88.3 2.8 %collective-permute-start.1 = (bf16[2,128,768]{2,1,0:T(8,128)(2,1)S(1)}, bf16[2,128,768]{2,1,0:T(8,128)(2,1)}, u32[]{:S(2)}, u32[]{:S(2)}) collective-permute-start(bf16[2,128,768]{2,1,0:T(8,128)(2,1)S(1)} %get-tuple-element.44), channel_id=1, source_target_pairs={{0,1},{1,2},{2,3},{3,0},{4,5},{5,6},{6,7},{7,4},{8,9},{9,10},{10,1... | collective-permute-start | bytes 1179656 | tf_op jit(solution)/shard_map/ppermute | solution.py:281
  91.9 1.0 broadcast_in_dim.17
  92.9 0.8 reshape.61
  93.7 0.9 copy.12.bias
  94.6 8.5 %collective-permute-done.3.x2 = bf16[2,128,768]{2,1,0:T(8,128)(2,1)} collective-permute-done((bf16[2,128,768]{2,1,0:T(8,128)(2,1)}, bf16[2,128,768]{2,1,0:T(8,128)(2,1)}, u32[]{:S(2)}, u32[]{:S(2)}) %collective-permute-start.3) | collective-permute-done | bytes 393248 | tf_op jit(solution)/shard_map/ppermute | solution.py:281
  103.2 8.2 %collective-permute-start.17 = (bf16[2,128,512]{2,1,0:T(8,128)(2,1)}, bf16[2,128,512]{2,1,0:T(8,128)(2,1)S(1)}, u32[]{:S(2)}, u32[]{:S(2)}) collective-permute-start(bf16[2,128,512]{2,1,0:T(8,128)(2,1)} %copy-done.9), channel_id=1, source_target_pairs={{0,2},{1,3},{2,0},{3,1},{4,6},{5,7},{6,4},{7,5},{8,10},{9,11},{10,... | collective-permute-start | bytes 786440 | tf_op jit(solution)/shard_map/ppermute | solution.py:281
  111.3 15.5 %collective-permute-done.5.x3 = bf16[2,128,768]{2,1,0:T(8,128)(2,1)} collective-permute-done((bf16[2,128,768]{2,1,0:T(8,128)(2,1)S(1)}, bf16[2,128,768]{2,1,0:T(8,128)(2,1)}, u32[]{:S(2)}, u32[]{:S(2)}) %collective-permute-start.5) | collective-permute-done | bytes 393248 | tf_op jit(solution)/shard_map/ppermute | solution.py:281
  126.8 2.0 collective-permute-start.18
  128.8 2.1 collective-permute-start.16
  130.9 14.9 %shard_map.78 = (bf16[128,768]{1,0:T(8,128)(2,1)S(1)}, bf16[128,768]{1,0:T(8,128)(2,1)S(1)}, bf16[128,768]{1,0:T(8,128)(2,1)S(1)}, bf16[128,768]{1,0:T(8,128)(2,...) custom-call(s32[1]{0:T(128)} %bitcast.zh, ...), custom_call_target="tpu_custom_call" | custom-call | flops 3019898880 | bytes 7864320 | tf_op jit(solution)/shard_map/pallas_call | solution.py:159
  145.9 1.9 collective-permute-start.11
  147.8 4.1 %collective-permute-start.12 = (bf16[2,2,128,768]{3,2,1,0:T(8,128)(2,1)S(1)}, bf16[2,2,128,768]{3,2,1,0:T(8,128)(2,1)S(1)}, u32[]{:S(2)}, u32[]{:S(2)}) collective-permute-start(bf16[2,2,128,768]{3,2,1,0:T(8,128)(2,1)S(1)} %get-tuple-element.59), channel_id=1, source_target_pairs={{4,0},{5,1},{6,2},{7,3},{8,4},{9,5},{10,6},{11,7},{12,8},{13,9},{1... | collective-permute-start | bytes 2359304 | tf_op jit(solution)/shard_map/ppermute | solution.py:288
  152.0 10.5 %shard_map.81 = (bf16[128,512]{1,0:T(8,128)(2,1)S(1)}, bf16[128,512]{1,0:T(8,128)(2,1)S(1)}, bf16[128,512]{1,0:T(8,128)(2,1)S(1)}, bf16[128,512]{1,0:T(8,128)(2,...) custom-call(s32[1]{0:T(128)} %bitcast.zh, ...), custom_call_target="tpu_custom_call" | custom-call | flops 2013265920 | bytes 5242880 | tf_op jit(solution)/shard_map/pallas_call | solution.py:159
  162.5 2.9 %collective-permute-start.22 = (bf16[2,2,128,512]{3,2,1,0:T(8,128)(2,1)S(1)}, bf16[2,2,128,512]{3,2,1,0:T(8,128)(2,1)S(1)}, u32[]{:S(2)}, u32[]{:S(2)}) collective-permute-start(bf16[2,2,128,512]{3,2,1,0:T(8,128)(2,1)S(1)} %get-tuple-element.75), channel_id=1, source_target_pairs={{0,4},{1,5},{2,6},{3,7},{4,8},{5,9},{6,10},{7,11},{8,12},{9,13},{1... | collective-permute-start | bytes 1572872 | tf_op jit(solution)/shard_map/ppermute | solution.py:285
  165.3 3.0 %collective-permute-start.23 = (bf16[2,2,128,512]{3,2,1,0:T(8,128)(2,1)S(1)}, bf16[2,2,128,512]{3,2,1,0:T(8,128)(2,1)S(1)}, u32[]{:S(2)}, u32[]{:S(2)}) collective-permute-start(bf16[2,2,128,512]{3,2,1,0:T(8,128)(2,1)S(1)} %get-tuple-element.76), channel_id=1, source_target_pairs={{4,0},{5,1},{6,2},{7,3},{8,4},{9,5},{10,6},{11,7},{12,8},{13,9},{1... | collective-permute-start | bytes 1572872 | tf_op jit(solution)/shard_map/ppermute | solution.py:288
  168.3 0.8 collective-permute-start.19
  169.1 8.9 %collective-permute-done.19.refs_9_ = bf16[128,512]{1,0:T(8,128)(2,1)S(1)} collective-permute-done((bf16[128,512]{1,0:T(8,128)(2,1)S(1)}, bf16[128,512]{1,0:T(8,128)(2,1)S(1)}, u32[]{:S(2)}, u32[]{:S(2)}) %collective-permute-start.19) | collective-permute-done | bytes 131104 | tf_op jit(solution)/shard_map/ppermute | solution.py:281
  178.0 2.1 collective-permute-start.20
  180.2 2.0 collective-permute-start.10
  182.2 1.0 collective-permute-done.23.from_after
  183.1 1.2 collective-permute-start.8
  185.0 12.3 %collective-permute-done.20.refs_10_ = bf16[128,512]{1,0:T(8,128)(2,1)S(1)} collective-permute-done((bf16[128,512]{1,0:T(8,128)(2,1)S(1)}, bf16[128,512]{1,0:T(8,128)(2,1)S(1)}, u32[]{:S(2)}, u32[]{:S(2)}) %collective-permute-start.20) | collective-permute-done | bytes 131104 | tf_op jit(solution)/shard_map/ppermute | solution.py:281
  197.3 4.1 %collective-permute-start.24 = (bf16[2,128,512]{2,1,0:T(8,128)(2,1)S(1)}, bf16[2,128,512]{2,1,0:T(8,128)(2,1)S(1)}, u32[]{:S(2)}, u32[]{:S(2)}) collective-permute-start(bf16[2,128,512]{2,1,0:T(8,128)(2,1)S(1)} %get-tuple-element.78), channel_id=1, source_target_pairs={{0,1},{1,2},{2,3},{3,0},{4,5},{5,6},{6,7},{7,4},{8,9},{9,10},{10,1... | collective-permute-start | bytes 786440 | tf_op jit(solution)/shard_map/ppermute | solution.py:281
  201.4 2.9 %collective-permute-start.9 = (bf16[128,768]{1,0:T(8,128)(2,1)S(1)}, bf16[128,768]{1,0:T(8,128)(2,1)S(1)}, u32[]{:S(2)}, u32[]{:S(2)}) collective-permute-start(bf16[128,768]{1,0:T(8,128)(2,1)S(1)} %get-tuple-element.55), channel_id=1, source_target_pairs={{0,2},{1,3},{2,0},{3,1},{4,6},{5,7},{6,4},{7,5},{8,10},{9,11},{10,... | collective-permute-start | bytes 589832 | tf_op jit(solution)/shard_map/ppermute | solution.py:281
  204.3 0.9 shard_map.79
  205.2 28.3 %collective-permute-done.21.refs_11_ = bf16[128,512]{1,0:T(8,128)(2,1)S(1)} collective-permute-done((bf16[128,512]{1,0:T(8,128)(2,1)S(1)}, bf16[128,512]{1,0:T(8,128)(2,1)S(1)}, u32[]{:S(2)}, u32[]{:S(2)}) %collective-permute-start.21) | collective-permute-done | bytes 131104 | tf_op jit(solution)/shard_map/ppermute | solution.py:281
  233.5 1.9 collective-permute-start.13
  235.4 2.0 collective-permute-start.14
  237.4 2.1 collective-permute-start.15
  239.6 2.8 %collective-permute-start.25 = (bf16[2,128,512]{2,1,0:T(8,128)(2,1)S(1)}, bf16[2,128,512]{2,1,0:T(8,128)(2,1)S(1)}, u32[]{:S(2)}, u32[]{:S(2)}) collective-permute-start(bf16[2,128,512]{2,1,0:T(8,128)(2,1)S(1)} %get-tuple-element.79), channel_id=1, source_target_pairs={{0,2},{1,3},{2,0},{3,1},{4,6},{5,7},{6,4},{7,5},{8,10},{9,11},{10,... | collective-permute-start | bytes 786440 | tf_op jit(solution)/shard_map/ppermute | solution.py:281
  242.4 1.6 collective-permute-start.26
  243.9 30.6 %collective-permute-done.25.refs_14_ = bf16[2,128,512]{2,1,0:T(8,128)(2,1)S(1)} collective-permute-done((bf16[2,128,512]{2,1,0:T(8,128)(2,1)S(1)}, bf16[2,128,512]{2,1,0:T(8,128)(2,1)S(1)}, u32[]{:S(2)}, u32[]{:S(2)}) %collective-permute-start.25) | collective-permute-done | bytes 262176 | tf_op jit(solution)/shard_map/ppermute | solution.py:281
  274.5 2.4 assemble.1
  (46 shorter events, 5.7 us)
Async XLA Ops:
  0.6 1.3 copy-start.2
  2.0 1.3 copy-start.4
  3.3 65.3 %copy-start.3 = (bf16[128,5120]{1,0:T(8,128)(2,1)S(1)}, bf16[128,5120]{1,0:T(8,128)(2,1)}, u32[]{:S(2)}) copy-start(bf16[128,5120]{1,0:T(8,128)(2,1)} %k.1) | copy-start | bytes 3932164
  3.3 65.3 %copy-start.5 = (bf16[128,5120]{1,0:T(8,128)(2,1)S(1)}, bf16[128,5120]{1,0:T(8,128)(2,1)}, u32[]{:S(2)}) copy-start(bf16[128,5120]{1,0:T(8,128)(2,1)} %v.1) | copy-start | bytes 3932164
  4.4 47.1 %collective-permute-start = (bf16[2,128,1280]{2,1,0:T(8,128)(2,1)S(1)}, bf16[2,128,1280]{2,1,0:T(8,128)(2,1)S(1)}, u32[]{:S(2)}, u32[]{:S(2)}) collective-permute-start(bf16[2,128,1280]{2,1,0:T(8,128)(2,1)S(1)} %get-tuple-element.43), channel_id=1, source_target_pairs={{0,1},{1,2},{2,3},{3,0},{4,5},{5,6},{6,7},{7,4},{8,9},{9,10},{10,1... | collective-permute-start | bytes 1966088 | tf_op jit(solution)/shard_map/ppermute | solution.py:281
  8.9 57.8 %collective-permute-start.2 = (bf16[2,128,1280]{2,1,0:T(8,128)(2,1)S(1)}, bf16[2,128,1280]{2,1,0:T(8,128)(2,1)S(1)}, u32[]{:S(2)}, u32[]{:S(2)}) collective-permute-start(bf16[2,128,1280]{2,1,0:T(8,128)(2,1)S(1)} %get-tuple-element.46), channel_id=1, source_target_pairs={{0,2},{1,3},{2,0},{3,1},{4,6},{5,7},{6,4},{7,5},{8,10},{9,11},{10,... | collective-permute-start | bytes 1966088 | tf_op jit(solution)/shard_map/ppermute | solution.py:281
  9.9 67.4 %copy-start = (bf16[128,5120]{1,0:T(8,128)(2,1)S(1)}, bf16[128,5120]{1,0:T(8,128)(2,1)}, u32[]{:S(2)}) copy-start(bf16[128,5120]{1,0:T(8,128)(2,1)} %q0.3) | copy-start | bytes 3932164
  9.9 67.4 %copy-start.1 = (bf16[128,5120]{1,0:T(8,128)(2,1)S(1)}, bf16[128,5120]{1,0:T(8,128)(2,1)}, u32[]{:S(2)}) copy-start(bf16[128,5120]{1,0:T(8,128)(2,1)} %g0.3) | copy-start | bytes 3932164
  9.9 58.7 %collective-permute-start.4 = (bf16[2,128,1280]{2,1,0:T(8,128)(2,1)S(1)}, bf16[2,128,1280]{2,1,0:T(8,128)(2,1)S(1)}, u32[]{:S(2)}, u32[]{:S(2)}) collective-permute-start(bf16[2,128,1280]{2,1,0:T(8,128)(2,1)S(1)} %get-tuple-element.49), channel_id=1, source_target_pairs={{0,3},{1,0},{2,1},{3,2},{4,7},{5,4},{6,5},{7,6},{8,11},{9,8},{10,9... | collective-permute-start | bytes 1966088 | tf_op jit(solution)/shard_map/ppermute | solution.py:281
  71.5 59.5 %collective-permute-start.6 = (bf16[2,2,128,1280]{3,2,1,0:T(8,128)(2,1)}, bf16[2,2,128,1280]{3,2,1,0:T(8,128)(2,1)}, u32[]{:S(2)}, u32[]{:S(2)}) collective-permute-start(bf16[2,2,128,1280]{3,2,1,0:T(8,128)(2,1)} %get-tuple-element.51.hi), channel_id=1, source_target_pairs={{0,4},{1,5},{2,6},{3,7},{4,8},{5,9},{6,10},{7,11},{8,12},{9,13},{1... | collective-permute-start | bytes 3932168 | tf_op jit(solution)/shard_map/ppermute | solution.py:285
  73.4 57.6 %collective-permute-start.7 = (bf16[2,2,128,1280]{3,2,1,0:T(8,128)(2,1)}, bf16[2,2,128,1280]{3,2,1,0:T(8,128)(2,1)}, u32[]{:S(2)}, u32[]{:S(2)}) collective-permute-start(bf16[2,2,128,1280]{3,2,1,0:T(8,128)(2,1)} %get-tuple-element.52.lo), channel_id=1, source_target_pairs={{4,0},{5,1},{6,2},{7,3},{8,4},{9,5},{10,6},{11,7},{12,8},{13,9},{1... | collective-permute-start | bytes 3932168 | tf_op jit(solution)/shard_map/ppermute | solution.py:288
  78.1 0.7 copy-start.6
  79.3 0.7 copy-start.7
  80.0 0.7 copy-start.8
  80.7 0.7 copy-start.9
  82.5 20.7 %collective-permute-start.3 = (bf16[2,128,768]{2,1,0:T(8,128)(2,1)}, bf16[2,128,768]{2,1,0:T(8,128)(2,1)}, u32[]{:S(2)}, u32[]{:S(2)}) collective-permute-start(bf16[2,128,768]{2,1,0:T(8,128)(2,1)} %copy-done.6), channel_id=1, source_target_pairs={{0,2},{1,3},{2,0},{3,1},{4,6},{5,7},{6,4},{7,5},{8,10},{9,11},{10,... | collective-permute-start | bytes 1179656 | tf_op jit(solution)/shard_map/ppermute | solution.py:281
  87.0 39.8 %collective-permute-start.5 = (bf16[2,128,768]{2,1,0:T(8,128)(2,1)S(1)}, bf16[2,128,768]{2,1,0:T(8,128)(2,1)}, u32[]{:S(2)}, u32[]{:S(2)}) collective-permute-start(bf16[2,128,768]{2,1,0:T(8,128)(2,1)S(1)} %get-tuple-element.50), channel_id=1, source_target_pairs={{0,3},{1,0},{2,1},{3,2},{4,7},{5,4},{6,5},{7,6},{8,11},{9,8},{10,9... | collective-permute-start | bytes 1179656 | tf_op jit(solution)/shard_map/ppermute | solution.py:281
  88.3 40.5 %collective-permute-start.1 = (bf16[2,128,768]{2,1,0:T(8,128)(2,1)S(1)}, bf16[2,128,768]{2,1,0:T(8,128)(2,1)}, u32[]{:S(2)}, u32[]{:S(2)}) collective-permute-start(bf16[2,128,768]{2,1,0:T(8,128)(2,1)S(1)} %get-tuple-element.44), channel_id=1, source_target_pairs={{0,1},{1,2},{2,3},{3,0},{4,5},{5,6},{6,7},{7,4},{8,9},{9,10},{10,1... | collective-permute-start | bytes 1179656 | tf_op jit(solution)/shard_map/ppermute | solution.py:281
  103.2 48.7 %collective-permute-start.17 = (bf16[2,128,512]{2,1,0:T(8,128)(2,1)}, bf16[2,128,512]{2,1,0:T(8,128)(2,1)S(1)}, u32[]{:S(2)}, u32[]{:S(2)}) collective-permute-start(bf16[2,128,512]{2,1,0:T(8,128)(2,1)} %copy-done.9), channel_id=1, source_target_pairs={{0,2},{1,3},{2,0},{3,1},{4,6},{5,7},{6,4},{7,5},{8,10},{9,11},{10,... | collective-permute-start | bytes 786440 | tf_op jit(solution)/shard_map/ppermute | solution.py:281
  126.8 25.1 %collective-permute-start.18 = (bf16[2,128,512]{2,1,0:T(8,128)(2,1)}, bf16[2,128,512]{2,1,0:T(8,128)(2,1)S(1)}, u32[]{:S(2)}, u32[]{:S(2)}) collective-permute-start(bf16[2,128,512]{2,1,0:T(8,128)(2,1)} %copy-done.8), channel_id=1, source_target_pairs={{0,3},{1,0},{2,1},{3,2},{4,7},{5,4},{6,5},{7,6},{8,11},{9,8},{10,9... | collective-permute-start | bytes 786440 | tf_op jit(solution)/shard_map/ppermute | solution.py:281
  128.8 23.1 %collective-permute-start.16 = (bf16[2,128,512]{2,1,0:T(8,128)(2,1)}, bf16[2,128,512]{2,1,0:T(8,128)(2,1)S(1)}, u32[]{:S(2)}, u32[]{:S(2)}) collective-permute-start(bf16[2,128,512]{2,1,0:T(8,128)(2,1)} %copy-done.7), channel_id=1, source_target_pairs={{0,1},{1,2},{2,3},{3,0},{4,5},{5,6},{6,7},{7,4},{8,9},{9,10},{10,1... | collective-permute-start | bytes 786440 | tf_op jit(solution)/shard_map/ppermute | solution.py:281
  145.9 51.4 %collective-permute-start.11 = (bf16[2,2,128,768]{3,2,1,0:T(8,128)(2,1)S(1)}, bf16[2,2,128,768]{3,2,1,0:T(8,128)(2,1)S(1)}, u32[]{:S(2)}, u32[]{:S(2)}) collective-permute-start(bf16[2,2,128,768]{3,2,1,0:T(8,128)(2,1)S(1)} %get-tuple-element.58), channel_id=1, source_target_pairs={{0,4},{1,5},{2,6},{3,7},{4,8},{5,9},{6,10},{7,11},{8,12},{9,13},{1... | collective-permute-start | bytes 2359304 | tf_op jit(solution)/shard_map/ppermute | solution.py:285
  147.8 53.6 %collective-permute-start.12 = (bf16[2,2,128,768]{3,2,1,0:T(8,128)(2,1)S(1)}, bf16[2,2,128,768]{3,2,1,0:T(8,128)(2,1)S(1)}, u32[]{:S(2)}, u32[]{:S(2)}) collective-permute-start(bf16[2,2,128,768]{3,2,1,0:T(8,128)(2,1)S(1)} %get-tuple-element.59), channel_id=1, source_target_pairs={{4,0},{5,1},{6,2},{7,3},{8,4},{9,5},{10,6},{11,7},{12,8},{13,9},{1... | collective-permute-start | bytes 2359304 | tf_op jit(solution)/shard_map/ppermute | solution.py:288
  162.5 17.7 %collective-permute-start.22 = (bf16[2,2,128,512]{3,2,1,0:T(8,128)(2,1)S(1)}, bf16[2,2,128,512]{3,2,1,0:T(8,128)(2,1)S(1)}, u32[]{:S(2)}, u32[]{:S(2)}) collective-permute-start(bf16[2,2,128,512]{3,2,1,0:T(8,128)(2,1)S(1)} %get-tuple-element.75), channel_id=1, source_target_pairs={{0,4},{1,5},{2,6},{3,7},{4,8},{5,9},{6,10},{7,11},{8,12},{9,13},{1... | collective-permute-start | bytes 1572872 | tf_op jit(solution)/shard_map/ppermute | solution.py:285
  165.3 17.8 %collective-permute-start.23 = (bf16[2,2,128,512]{3,2,1,0:T(8,128)(2,1)S(1)}, bf16[2,2,128,512]{3,2,1,0:T(8,128)(2,1)S(1)}, u32[]{:S(2)}, u32[]{:S(2)}) collective-permute-start(bf16[2,2,128,512]{3,2,1,0:T(8,128)(2,1)S(1)} %get-tuple-element.76), channel_id=1, source_target_pairs={{4,0},{5,1},{6,2},{7,3},{8,4},{9,5},{10,6},{11,7},{12,8},{13,9},{1... | collective-permute-start | bytes 1572872 | tf_op jit(solution)/shard_map/ppermute | solution.py:288
  168.3 9.7 %collective-permute-start.19 = (bf16[128,512]{1,0:T(8,128)(2,1)S(1)}, bf16[128,512]{1,0:T(8,128)(2,1)S(1)}, u32[]{:S(2)}, u32[]{:S(2)}) collective-permute-start(bf16[128,512]{1,0:T(8,128)(2,1)S(1)} %get-tuple-element.71), channel_id=1, source_target_pairs={{0,1},{1,2},{2,3},{3,0},{4,5},{5,6},{6,7},{7,4},{8,9},{9,10},{10,1... | collective-permute-start | bytes 393224 | tf_op jit(solution)/shard_map/ppermute | solution.py:281
  178.0 19.2 %collective-permute-start.20 = (bf16[128,512]{1,0:T(8,128)(2,1)S(1)}, bf16[128,512]{1,0:T(8,128)(2,1)S(1)}, u32[]{:S(2)}, u32[]{:S(2)}) collective-permute-start(bf16[128,512]{1,0:T(8,128)(2,1)S(1)} %get-tuple-element.72), channel_id=1, source_target_pairs={{0,2},{1,3},{2,0},{3,1},{4,6},{5,7},{6,4},{7,5},{8,10},{9,11},{10,... | collective-permute-start | bytes 393224 | tf_op jit(solution)/shard_map/ppermute | solution.py:281
  180.2 55.2 %collective-permute-start.10 = (bf16[128,768]{1,0:T(8,128)(2,1)S(1)}, bf16[128,768]{1,0:T(8,128)(2,1)S(1)}, u32[]{:S(2)}, u32[]{:S(2)}) collective-permute-start(bf16[128,768]{1,0:T(8,128)(2,1)S(1)} %get-tuple-element.56), channel_id=1, source_target_pairs={{0,3},{1,0},{2,1},{3,2},{4,7},{5,4},{6,5},{7,6},{8,11},{9,8},{10,9... | collective-permute-start | bytes 589832 | tf_op jit(solution)/shard_map/ppermute | solution.py:281
  183.1 54.3 %collective-permute-start.8 = (bf16[128,768]{1,0:T(8,128)(2,1)S(1)}, bf16[128,768]{1,0:T(8,128)(2,1)S(1)}, u32[]{:S(2)}, u32[]{:S(2)}) collective-permute-start(bf16[128,768]{1,0:T(8,128)(2,1)S(1)} %get-tuple-element.54), channel_id=1, source_target_pairs={{0,1},{1,2},{2,3},{3,0},{4,5},{5,6},{6,7},{7,4},{8,9},{9,10},{10,1... | collective-permute-start | bytes 589832 | tf_op jit(solution)/shard_map/ppermute | solution.py:281
  197.3 36.2 %collective-permute-start.21 = (bf16[128,512]{1,0:T(8,128)(2,1)S(1)}, bf16[128,512]{1,0:T(8,128)(2,1)S(1)}, u32[]{:S(2)}, u32[]{:S(2)}) collective-permute-start(bf16[128,512]{1,0:T(8,128)(2,1)S(1)} %get-tuple-element.73), channel_id=1, source_target_pairs={{0,3},{1,0},{2,1},{3,2},{4,7},{5,4},{6,5},{7,6},{8,11},{9,8},{10,9... | collective-permute-start | bytes 393224 | tf_op jit(solution)/shard_map/ppermute | solution.py:281
  197.3 45.1 %collective-permute-start.24 = (bf16[2,128,512]{2,1,0:T(8,128)(2,1)S(1)}, bf16[2,128,512]{2,1,0:T(8,128)(2,1)S(1)}, u32[]{:S(2)}, u32[]{:S(2)}) collective-permute-start(bf16[2,128,512]{2,1,0:T(8,128)(2,1)S(1)} %get-tuple-element.78), channel_id=1, source_target_pairs={{0,1},{1,2},{2,3},{3,0},{4,5},{5,6},{6,7},{7,4},{8,9},{9,10},{10,1... | collective-permute-start | bytes 786440 | tf_op jit(solution)/shard_map/ppermute | solution.py:281
  201.4 38.1 %collective-permute-start.9 = (bf16[128,768]{1,0:T(8,128)(2,1)S(1)}, bf16[128,768]{1,0:T(8,128)(2,1)S(1)}, u32[]{:S(2)}, u32[]{:S(2)}) collective-permute-start(bf16[128,768]{1,0:T(8,128)(2,1)S(1)} %get-tuple-element.55), channel_id=1, source_target_pairs={{0,2},{1,3},{2,0},{3,1},{4,6},{5,7},{6,4},{7,5},{8,10},{9,11},{10,... | collective-permute-start | bytes 589832 | tf_op jit(solution)/shard_map/ppermute | solution.py:281
  233.5 41.0 %collective-permute-start.13 = (bf16[2,128,768]{2,1,0:T(8,128)(2,1)S(1)}, bf16[2,128,768]{2,1,0:T(8,128)(2,1)S(1)}, u32[]{:S(2)}, u32[]{:S(2)}) collective-permute-start(bf16[2,128,768]{2,1,0:T(8,128)(2,1)S(1)} %get-tuple-element.61), channel_id=1, source_target_pairs={{0,1},{1,2},{2,3},{3,0},{4,5},{5,6},{6,7},{7,4},{8,9},{9,10},{10,1... | collective-permute-start | bytes 1179656 | tf_op jit(solution)/shard_map/ppermute | solution.py:281
  235.4 39.1 %collective-permute-start.14 = (bf16[2,128,768]{2,1,0:T(8,128)(2,1)S(1)}, bf16[2,128,768]{2,1,0:T(8,128)(2,1)S(1)}, u32[]{:S(2)}, u32[]{:S(2)}) collective-permute-start(bf16[2,128,768]{2,1,0:T(8,128)(2,1)S(1)} %get-tuple-element.62), channel_id=1, source_target_pairs={{0,2},{1,3},{2,0},{3,1},{4,6},{5,7},{6,4},{7,5},{8,10},{9,11},{10,... | collective-permute-start | bytes 1179656 | tf_op jit(solution)/shard_map/ppermute | solution.py:281
  237.4 37.1 %collective-permute-start.15 = (bf16[2,128,768]{2,1,0:T(8,128)(2,1)S(1)}, bf16[2,128,768]{2,1,0:T(8,128)(2,1)S(1)}, u32[]{:S(2)}, u32[]{:S(2)}) collective-permute-start(bf16[2,128,768]{2,1,0:T(8,128)(2,1)S(1)} %get-tuple-element.63), channel_id=1, source_target_pairs={{0,3},{1,0},{2,1},{3,2},{4,7},{5,4},{6,5},{7,6},{8,11},{9,8},{10,9... | collective-permute-start | bytes 1179656 | tf_op jit(solution)/shard_map/ppermute | solution.py:281
  239.6 35.0 %collective-permute-start.25 = (bf16[2,128,512]{2,1,0:T(8,128)(2,1)S(1)}, bf16[2,128,512]{2,1,0:T(8,128)(2,1)S(1)}, u32[]{:S(2)}, u32[]{:S(2)}) collective-permute-start(bf16[2,128,512]{2,1,0:T(8,128)(2,1)S(1)} %get-tuple-element.79), channel_id=1, source_target_pairs={{0,2},{1,3},{2,0},{3,1},{4,6},{5,7},{6,4},{7,5},{8,10},{9,11},{10,... | collective-permute-start | bytes 786440 | tf_op jit(solution)/shard_map/ppermute | solution.py:281
  242.4 32.2 %collective-permute-start.26 = (bf16[2,128,512]{2,1,0:T(8,128)(2,1)S(1)}, bf16[2,128,512]{2,1,0:T(8,128)(2,1)S(1)}, u32[]{:S(2)}, u32[]{:S(2)}) collective-permute-start(bf16[2,128,512]{2,1,0:T(8,128)(2,1)S(1)} %get-tuple-element.80), channel_id=1, source_target_pairs={{0,3},{1,0},{2,1},{3,2},{4,7},{5,4},{6,5},{7,6},{8,11},{9,8},{10,9... | collective-permute-start | bytes 786440 | tf_op jit(solution)/shard_map/ppermute | solution.py:281

commit v2 on v1

--- a/solution.py
+++ b/solution.py
@@ -289,14 +289,7 @@
 
     bias = tile_bias(tile_mask, zh_s, slab, group)
     kv = around(pack(zh, key, value, 0, group, group))
-    qg = []
-    behind = kv
-    for first, heads in CHUNKS:
-        packed = list(pack(zh, query, dout, first, heads, group))
-        for s in range(3):
-            packed[s], _ = lax.optimization_barrier((packed[s], behind[s]))
-        behind = around(packed)
-        qg.append(behind)
+    qg = [around(pack(zh, query, dout, first, heads, group)) for first, heads in CHUNKS]
     lo, hi = unpack(zh, key, value, kv, group)
     before, after = to_next(hi), to_prev(lo)
     parts = []

time: 277 us -> 294 us (1.061)
  the two profiles are of different devices: /device:TPU:70 before, /device:TPU:32 now
where the time goes in v2:
time: 294 us; the launch traced here: 293 us
  waiting for transfers between devices  139 us (47%)
  starting transfers between devices  108 us (37%)
  Pallas kernels  35.8 us (12%)
  local copies, waits for them, and re-layouts  8.48 us (3%)
    ppermute x21, waiting for transfers between devices, around(): out.append(lax.ppermute(a, 'uly', rings[s]))  139 us
    ppermute x21, starting transfers between devices, around(): out.append(lax.ppermute(a, 'uly', rings[s]))  64.9 us
    ppermute x3, starting transfers between devices, to_prev(): return lax.ppermute(a, ('ctx', 'uly'), down)  36.3 us
    pallas_call x2, Pallas kernels, attend(): pl.pallas_call(attend_body, grid_spec=pltpu.PrefetchScalarGridSpec(num_sc...  25.5 us
    ppermute x3, starting transfers between devices, to_next(): return lax.ppermute(a, ('ctx', 'uly'), up)  7.23 us
  transfers between devices with their start and end apart: 27, of which 9 were waited for; matrix products, arithmetic and copies ran while one was open for 2% of the time, Pallas kernels for 10%

profile of v2, /device:TPU:32, one launch (start us, length us, event | category | flops | bytes accessed | tf_op | source)
XLA Modules:
  0.0 293.2 jit_solution(4336792951524852420)
XLA Ops:
  0.6 1.3 copy-done.2
  2.0 1.3 copy-done.4
  3.3 1.1 shard_map.77
  4.4 3.3 %collective-permute-start.3 = (bf16[2,128,1280]{2,1,0:T(8,128)(2,1)S(1)}, bf16[2,128,1280]{2,1,0:T(8,128)(2,1)S(1)}, u32[]{:S(2)}, u32[]{:S(2)}) collective-permute-start(bf16[2,128,1280]{2,1,0:T(8,128)(2,1)S(1)} %get-tuple-element.39), channel_id=1, source_target_pairs={{0,1},{1,2},{2,3},{3,0},{4,5},{5,6},{6,7},{7,4},{8,9},{9,10},{10,1... | collective-permute-start | bytes 1966088 | tf_op jit(solution)/shard_map/ppermute | solution.py:281
  7.7 4.5 %collective-permute-start.4 = (bf16[2,128,1280]{2,1,0:T(8,128)(2,1)S(1)}, bf16[2,128,1280]{2,1,0:T(8,128)(2,1)S(1)}, u32[]{:S(2)}, u32[]{:S(2)}) collective-permute-start(bf16[2,128,1280]{2,1,0:T(8,128)(2,1)S(1)} %get-tuple-element.40), channel_id=1, source_target_pairs={{0,2},{1,3},{2,0},{3,1},{4,6},{5,7},{6,4},{7,5},{8,10},{9,11},{10,... | collective-permute-start | bytes 1966088 | tf_op jit(solution)/shard_map/ppermute | solution.py:281
  12.2 2.7 collective-permute-start.5
  14.9 39.5 %collective-permute-done.3.r1 = bf16[2,128,1280]{2,1,0:T(8,128)(2,1)S(1)} collective-permute-done((bf16[2,128,1280]{2,1,0:T(8,128)(2,1)S(1)}, bf16[2,128,1280]{2,1,0:T(8,128)(2,1)S(1)}, u32[]{:S(2)}, u32[]{:S(2)}) %collective-permute-start.3) | collective-permute-done | bytes 655392 | tf_op jit(solution)/shard_map/ppermute | solution.py:281
  54.4 2.7 collective-permute-done.5.r3
  57.1 2.9 unpack.1
  60.0 3.4 %collective-permute-start.6 = (bf16[2,2,128,1280]{3,2,1,0:T(8,128)(2,1)}, bf16[2,2,128,1280]{3,2,1,0:T(8,128)(2,1)}, u32[]{:S(2)}, u32[]{:S(2)}) collective-permute-start(bf16[2,2,128,1280]{3,2,1,0:T(8,128)(2,1)} %get-tuple-element.42.hi), channel_id=1, source_target_pairs={{0,4},{1,5},{2,6},{3,7},{4,8},{5,9},{6,10},{7,11},{8,12},{9,13},{1... | collective-permute-start | bytes 3932168 | tf_op jit(solution)/shard_map/ppermute | solution.py:285
  63.4 18.2 %collective-permute-start.7 = (bf16[2,2,128,1280]{3,2,1,0:T(8,128)(2,1)}, bf16[2,2,128,1280]{3,2,1,0:T(8,128)(2,1)}, u32[]{:S(2)}, u32[]{:S(2)}) collective-permute-start(bf16[2,2,128,1280]{3,2,1,0:T(8,128)(2,1)} %get-tuple-element.43.lo), channel_id=1, source_target_pairs={{4,0},{5,1},{6,2},{7,3},{8,4},{9,5},{10,6},{11,7},{12,8},{13,9},{1... | collective-permute-start | bytes 3932168 | tf_op jit(solution)/shard_map/ppermute | solution.py:288
  81.6 1.9 shard_map.76
  83.4 1.0 collective-permute-start
  84.4 4.8 %collective-permute-start.1 = (bf16[2,128,768]{2,1,0:T(8,128)(2,1)}, bf16[2,128,768]{2,1,0:T(8,128)(2,1)S(1)}, u32[]{:S(2)}, u32[]{:S(2)}) collective-permute-start(bf16[2,128,768]{2,1,0:T(8,128)(2,1)} %get-tuple-element.37), channel_id=1, source_target_pairs={{0,2},{1,3},{2,0},{3,1},{4,6},{5,7},{6,4},{7,5},{8,10},{9,11},{10,... | collective-permute-start | bytes 1179656 | tf_op jit(solution)/shard_map/ppermute | solution.py:281
  89.3 2.0 collective-permute-start.2
  92.5 0.7 copy-done.7
  93.2 0.7 copy-done.8
  94.0 0.9 fusion.1
  95.1 0.8 copy.11
  95.9 1.0 broadcast_in_dim.17
  96.9 0.8 reshape.61
  97.7 0.9 copy.12.bias
  98.6 27.2 %collective-permute-done.x1 = bf16[2,128,768]{2,1,0:T(8,128)(2,1)S(1)} collective-permute-done((bf16[2,128,768]{2,1,0:T(8,128)(2,1)}, bf16[2,128,768]{2,1,0:T(8,128)(2,1)S(1)}, u32[]{:S(2)}, u32[]{:S(2)}) %collective-permute-start) | collective-permute-done | bytes 393248 | tf_op jit(solution)/shard_map/ppermute | solution.py:281
  125.8 2.3 collective-permute-start.16
  128.1 3.6 %collective-permute-start.17 = (bf16[2,128,512]{2,1,0:T(8,128)(2,1)}, bf16[2,128,512]{2,1,0:T(8,128)(2,1)S(1)}, u32[]{:S(2)}, u32[]{:S(2)}) collective-permute-start(bf16[2,128,512]{2,1,0:T(8,128)(2,1)} %copy-done.7), channel_id=1, source_target_pairs={{0,2},{1,3},{2,0},{3,1},{4,6},{5,7},{6,4},{7,5},{8,10},{9,11},{10,... | collective-permute-start | bytes 786440 | tf_op jit(solution)/shard_map/ppermute | solution.py:281
  132.0 3.6 %collective-permute-start.18 = (bf16[2,128,512]{2,1,0:T(8,128)(2,1)}, bf16[2,128,512]{2,1,0:T(8,128)(2,1)S(1)}, u32[]{:S(2)}, u32[]{:S(2)}) collective-permute-start(bf16[2,128,512]{2,1,0:T(8,128)(2,1)} %copy-done.6), channel_id=1, source_target_pairs={{0,3},{1,0},{2,1},{3,2},{4,7},{5,4},{6,5},{7,6},{8,11},{9,8},{10,9... | collective-permute-start | bytes 786440 | tf_op jit(solution)/shard_map/ppermute | solution.py:281
  135.7 15.0 %shard_map.78 = (bf16[128,768]{1,0:T(8,128)(2,1)S(1)}, bf16[128,768]{1,0:T(8,128)(2,1)S(1)}, bf16[128,768]{1,0:T(8,128)(2,1)S(1)}, bf16[128,768]{1,0:T(8,128)(2,...) custom-call(s32[1]{0:T(128)} %bitcast.zh, ...), custom_call_target="tpu_custom_call" | custom-call | flops 3019898880 | bytes 7864320 | tf_op jit(solution)/shard_map/pallas_call | solution.py:159
  150.7 1.9 collective-permute-start.11
  152.6 10.3 %collective-permute-start.12 = (bf16[2,2,128,768]{3,2,1,0:T(8,128)(2,1)S(1)}, bf16[2,2,128,768]{3,2,1,0:T(8,128)(2,1)S(1)}, u32[]{:S(2)}, u32[]{:S(2)}) collective-permute-start(bf16[2,2,128,768]{3,2,1,0:T(8,128)(2,1)S(1)} %get-tuple-element.50), channel_id=1, source_target_pairs={{4,0},{5,1},{6,2},{7,3},{8,4},{9,5},{10,6},{11,7},{12,8},{13,9},{1... | collective-permute-start | bytes 2359304 | tf_op jit(solution)/shard_map/ppermute | solution.py:288
  162.9 10.5 %shard_map.81 = (bf16[128,512]{1,0:T(8,128)(2,1)S(1)}, bf16[128,512]{1,0:T(8,128)(2,1)S(1)}, bf16[128,512]{1,0:T(8,128)(2,1)S(1)}, bf16[128,512]{1,0:T(8,128)(2,...) custom-call(s32[1]{0:T(128)} %bitcast.zh, ...), custom_call_target="tpu_custom_call" | custom-call | flops 2013265920 | bytes 5242880 | tf_op jit(solution)/shard_map/pallas_call | solution.py:159
  173.4 1.9 collective-permute-start.22
  175.3 7.9 %collective-permute-start.23 = (bf16[2,2,128,512]{3,2,1,0:T(8,128)(2,1)S(1)}, bf16[2,2,128,512]{3,2,1,0:T(8,128)(2,1)S(1)}, u32[]{:S(2)}, u32[]{:S(2)}) collective-permute-start(bf16[2,2,128,512]{3,2,1,0:T(8,128)(2,1)S(1)} %get-tuple-element.64), channel_id=1, source_target_pairs={{4,0},{5,1},{6,2},{7,3},{8,4},{9,5},{10,6},{11,7},{12,8},{13,9},{1... | collective-permute-start | bytes 1572872 | tf_op jit(solution)/shard_map/ppermute | solution.py:288
  183.2 2.7 collective-permute-start.19
  185.9 45.0 %collective-permute-done.19.refs_9_ = bf16[128,512]{1,0:T(8,128)(2,1)S(1)} collective-permute-done((bf16[128,512]{1,0:T(8,128)(2,1)S(1)}, bf16[128,512]{1,0:T(8,128)(2,1)S(1)}, u32[]{:S(2)}, u32[]{:S(2)}) %collective-permute-start.19) | collective-permute-done | bytes 131104 | tf_op jit(solution)/shard_map/ppermute | solution.py:281
  230.9 17.4 %collective-permute-start.20 = (bf16[128,512]{1,0:T(8,128)(2,1)S(1)}, bf16[128,512]{1,0:T(8,128)(2,1)S(1)}, u32[]{:S(2)}, u32[]{:S(2)}) collective-permute-start(bf16[128,512]{1,0:T(8,128)(2,1)S(1)} %get-tuple-element.60), channel_id=1, source_target_pairs={{0,2},{1,3},{2,0},{3,1},{4,6},{5,7},{6,4},{7,5},{8,10},{9,11},{10,... | collective-permute-start | bytes 393224 | tf_op jit(solution)/shard_map/ppermute | solution.py:281
  249.1 2.2 collective-permute-done.20.refs_10_
  251.3 1.9 collective-permute-start.21
  253.2 2.5 collective-permute-start.24
  255.7 2.3 collective-permute-start.10
  257.9 0.9 shard_map.79
  258.9 2.7 collective-permute-done.21.refs_11_
  261.6 1.3 collective-permute-start.13
  262.8 1.6 collective-permute-start.14
  264.4 4.0 %collective-permute-start.15 = (bf16[2,128,768]{2,1,0:T(8,128)(2,1)S(1)}, bf16[2,128,768]{2,1,0:T(8,128)(2,1)S(1)}, u32[]{:S(2)}, u32[]{:S(2)}) collective-permute-start(bf16[2,128,768]{2,1,0:T(8,128)(2,1)S(1)} %get-tuple-element.54), channel_id=1, source_target_pairs={{0,3},{1,0},{2,1},{3,2},{4,7},{5,4},{6,5},{7,6},{8,11},{9,8},{10,9... | collective-permute-start | bytes 1179656 | tf_op jit(solution)/shard_map/ppermute | solution.py:281
  268.4 3.2 %collective-permute-start.25 = (bf16[2,128,512]{2,1,0:T(8,128)(2,1)S(1)}, bf16[2,128,512]{2,1,0:T(8,128)(2,1)S(1)}, u32[]{:S(2)}, u32[]{:S(2)}) collective-permute-start(bf16[2,128,512]{2,1,0:T(8,128)(2,1)S(1)} %get-tuple-element.67), channel_id=1, source_target_pairs={{0,2},{1,3},{2,0},{3,1},{4,6},{5,7},{6,4},{7,5},{8,10},{9,11},{10,... | collective-permute-start | bytes 786440 | tf_op jit(solution)/shard_map/ppermute | solution.py:281
  271.7 14.2 %collective-permute-done.25.refs_14_ = bf16[2,128,512]{2,1,0:T(8,128)(2,1)S(1)} collective-permute-done((bf16[2,128,512]{2,1,0:T(8,128)(2,1)S(1)}, bf16[2,128,512]{2,1,0:T(8,128)(2,1)S(1)}, u32[]{:S(2)}, u32[]{:S(2)}) %collective-permute-start.25) | collective-permute-done | bytes 262176 | tf_op jit(solution)/shard_map/ppermute | solution.py:281
  285.9 4.8 %collective-permute-done.26.refs_15_ = bf16[2,128,512]{2,1,0:T(8,128)(2,1)S(1)} collective-permute-done((bf16[2,128,512]{2,1,0:T(8,128)(2,1)S(1)}, bf16[2,128,512]{2,1,0:T(8,128)(2,1)S(1)}, u32[]{:S(2)}, u32[]{:S(2)}) %collective-permute-start.26) | collective-permute-done | bytes 262176 | tf_op jit(solution)/shard_map/ppermute | solution.py:281
  290.7 2.4 assemble.1
  (44 shorter events, 2.6 us)
Async XLA Ops:
  0.6 1.3 copy-start.2
  2.0 1.3 copy-start.4
  3.3 53.8 %copy-start.3 = (bf16[128,5120]{1,0:T(8,128)(2,1)S(1)}, bf16[128,5120]{1,0:T(8,128)(2,1)}, u32[]{:S(2)}) copy-start(bf16[128,5120]{1,0:T(8,128)(2,1)} %k.1) | copy-start | bytes 3932164
  3.3 53.8 %copy-start.5 = (bf16[128,5120]{1,0:T(8,128)(2,1)S(1)}, bf16[128,5120]{1,0:T(8,128)(2,1)}, u32[]{:S(2)}) copy-start(bf16[128,5120]{1,0:T(8,128)(2,1)} %v.1) | copy-start | bytes 3932164
  4.4 50.0 %collective-permute-start.3 = (bf16[2,128,1280]{2,1,0:T(8,128)(2,1)S(1)}, bf16[2,128,1280]{2,1,0:T(8,128)(2,1)S(1)}, u32[]{:S(2)}, u32[]{:S(2)}) collective-permute-start(bf16[2,128,1280]{2,1,0:T(8,128)(2,1)S(1)} %get-tuple-element.39), channel_id=1, source_target_pairs={{0,1},{1,2},{2,3},{3,0},{4,5},{5,6},{6,7},{7,4},{8,9},{9,10},{10,1... | collective-permute-start | bytes 1966088 | tf_op jit(solution)/shard_map/ppermute | solution.py:281
  7.7 46.7 %collective-permute-start.4 = (bf16[2,128,1280]{2,1,0:T(8,128)(2,1)S(1)}, bf16[2,128,1280]{2,1,0:T(8,128)(2,1)S(1)}, u32[]{:S(2)}, u32[]{:S(2)}) collective-permute-start(bf16[2,128,1280]{2,1,0:T(8,128)(2,1)S(1)} %get-tuple-element.40), channel_id=1, source_target_pairs={{0,2},{1,3},{2,0},{3,1},{4,6},{5,7},{6,4},{7,5},{8,10},{9,11},{10,... | collective-permute-start | bytes 1966088 | tf_op jit(solution)/shard_map/ppermute | solution.py:281
  12.2 69.3 %copy-start = (bf16[128,5120]{1,0:T(8,128)(2,1)S(1)}, bf16[128,5120]{1,0:T(8,128)(2,1)}, u32[]{:S(2)}) copy-start(bf16[128,5120]{1,0:T(8,128)(2,1)} %q0.3) | copy-start | bytes 3932164
  12.2 69.3 %copy-start.1 = (bf16[128,5120]{1,0:T(8,128)(2,1)S(1)}, bf16[128,5120]{1,0:T(8,128)(2,1)}, u32[]{:S(2)}) copy-start(bf16[128,5120]{1,0:T(8,128)(2,1)} %g0.3) | copy-start | bytes 3932164
  12.2 44.9 %collective-permute-start.5 = (bf16[2,128,1280]{2,1,0:T(8,128)(2,1)S(1)}, bf16[2,128,1280]{2,1,0:T(8,128)(2,1)S(1)}, u32[]{:S(2)}, u32[]{:S(2)}) collective-permute-start(bf16[2,128,1280]{2,1,0:T(8,128)(2,1)S(1)} %get-tuple-element.41), channel_id=1, source_target_pairs={{0,3},{1,0},{2,1},{3,2},{4,7},{5,4},{6,5},{7,6},{8,11},{9,8},{10,9... | collective-permute-start | bytes 1966088 | tf_op jit(solution)/shard_map/ppermute | solution.py:281
  60.0 75.7 %collective-permute-start.6 = (bf16[2,2,128,1280]{3,2,1,0:T(8,128)(2,1)}, bf16[2,2,128,1280]{3,2,1,0:T(8,128)(2,1)}, u32[]{:S(2)}, u32[]{:S(2)}) collective-permute-start(bf16[2,2,128,1280]{3,2,1,0:T(8,128)(2,1)} %get-tuple-element.42.hi), channel_id=1, source_target_pairs={{0,4},{1,5},{2,6},{3,7},{4,8},{5,9},{6,10},{7,11},{8,12},{9,13},{1... | collective-permute-start | bytes 3932168 | tf_op jit(solution)/shard_map/ppermute | solution.py:285
  63.4 72.3 %collective-permute-start.7 = (bf16[2,2,128,1280]{3,2,1,0:T(8,128)(2,1)}, bf16[2,2,128,1280]{3,2,1,0:T(8,128)(2,1)}, u32[]{:S(2)}, u32[]{:S(2)}) collective-permute-start(bf16[2,2,128,1280]{3,2,1,0:T(8,128)(2,1)} %get-tuple-element.43.lo), channel_id=1, source_target_pairs={{4,0},{5,1},{6,2},{7,3},{8,4},{9,5},{10,6},{11,7},{12,8},{13,9},{1... | collective-permute-start | bytes 3932168 | tf_op jit(solution)/shard_map/ppermute | solution.py:288
  83.4 42.4 %collective-permute-start = (bf16[2,128,768]{2,1,0:T(8,128)(2,1)}, bf16[2,128,768]{2,1,0:T(8,128)(2,1)S(1)}, u32[]{:S(2)}, u32[]{:S(2)}) collective-permute-start(bf16[2,128,768]{2,1,0:T(8,128)(2,1)} %get-tuple-element.36), channel_id=1, source_target_pairs={{0,1},{1,2},{2,3},{3,0},{4,5},{5,6},{6,7},{7,4},{8,9},{9,10},{10,1... | collective-permute-start | bytes 1179656 | tf_op jit(solution)/shard_map/ppermute | solution.py:281
  84.4 43.7 %collective-permute-start.1 = (bf16[2,128,768]{2,1,0:T(8,128)(2,1)}, bf16[2,128,768]{2,1,0:T(8,128)(2,1)S(1)}, u32[]{:S(2)}, u32[]{:S(2)}) collective-permute-start(bf16[2,128,768]{2,1,0:T(8,128)(2,1)} %get-tuple-element.37), channel_id=1, source_target_pairs={{0,2},{1,3},{2,0},{3,1},{4,6},{5,7},{6,4},{7,5},{8,10},{9,11},{10,... | collective-permute-start | bytes 1179656 | tf_op jit(solution)/shard_map/ppermute | solution.py:281
  89.3 42.8 %collective-permute-start.2 = (bf16[2,128,768]{2,1,0:T(8,128)(2,1)}, bf16[2,128,768]{2,1,0:T(8,128)(2,1)}, u32[]{:S(2)}, u32[]{:S(2)}) collective-permute-start(bf16[2,128,768]{2,1,0:T(8,128)(2,1)} %get-tuple-element.38), channel_id=1, source_target_pairs={{0,3},{1,0},{2,1},{3,2},{4,7},{5,4},{6,5},{7,6},{8,11},{9,8},{10,9... | collective-permute-start | bytes 1179656 | tf_op jit(solution)/shard_map/ppermute | solution.py:281
  91.8 0.7 copy-start.6
  92.5 0.7 copy-start.7
  93.2 0.7 copy-start.8
  125.8 37.1 %collective-permute-start.16 = (bf16[2,128,512]{2,1,0:T(8,128)(2,1)}, bf16[2,128,512]{2,1,0:T(8,128)(2,1)S(1)}, u32[]{:S(2)}, u32[]{:S(2)}) collective-permute-start(bf16[2,128,512]{2,1,0:T(8,128)(2,1)} %copy-done.8), channel_id=1, source_target_pairs={{0,1},{1,2},{2,3},{3,0},{4,5},{5,6},{6,7},{7,4},{8,9},{9,10},{10,1... | collective-permute-start | bytes 786440 | tf_op jit(solution)/shard_map/ppermute | solution.py:281
  128.1 34.8 %collective-permute-start.17 = (bf16[2,128,512]{2,1,0:T(8,128)(2,1)}, bf16[2,128,512]{2,1,0:T(8,128)(2,1)S(1)}, u32[]{:S(2)}, u32[]{:S(2)}) collective-permute-start(bf16[2,128,512]{2,1,0:T(8,128)(2,1)} %copy-done.7), channel_id=1, source_target_pairs={{0,2},{1,3},{2,0},{3,1},{4,6},{5,7},{6,4},{7,5},{8,10},{9,11},{10,... | collective-permute-start | bytes 786440 | tf_op jit(solution)/shard_map/ppermute | solution.py:281
  132.0 30.9 %collective-permute-start.18 = (bf16[2,128,512]{2,1,0:T(8,128)(2,1)}, bf16[2,128,512]{2,1,0:T(8,128)(2,1)S(1)}, u32[]{:S(2)}, u32[]{:S(2)}) collective-permute-start(bf16[2,128,512]{2,1,0:T(8,128)(2,1)} %copy-done.6), channel_id=1, source_target_pairs={{0,3},{1,0},{2,1},{3,2},{4,7},{5,4},{6,5},{7,6},{8,11},{9,8},{10,9... | collective-permute-start | bytes 786440 | tf_op jit(solution)/shard_map/ppermute | solution.py:281
  150.7 102.5 %collective-permute-start.11 = (bf16[2,2,128,768]{3,2,1,0:T(8,128)(2,1)S(1)}, bf16[2,2,128,768]{3,2,1,0:T(8,128)(2,1)S(1)}, u32[]{:S(2)}, u32[]{:S(2)}) collective-permute-start(bf16[2,2,128,768]{3,2,1,0:T(8,128)(2,1)S(1)} %get-tuple-element.49), channel_id=1, source_target_pairs={{0,4},{1,5},{2,6},{3,7},{4,8},{5,9},{6,10},{7,11},{8,12},{9,13},{1... | collective-permute-start | bytes 2359304 | tf_op jit(solution)/shard_map/ppermute | solution.py:285
  152.6 103.1 %collective-permute-start.12 = (bf16[2,2,128,768]{3,2,1,0:T(8,128)(2,1)S(1)}, bf16[2,2,128,768]{3,2,1,0:T(8,128)(2,1)S(1)}, u32[]{:S(2)}, u32[]{:S(2)}) collective-permute-start(bf16[2,2,128,768]{3,2,1,0:T(8,128)(2,1)S(1)} %get-tuple-element.50), channel_id=1, source_target_pairs={{4,0},{5,1},{6,2},{7,3},{8,4},{9,5},{10,6},{11,7},{12,8},{13,9},{1... | collective-permute-start | bytes 2359304 | tf_op jit(solution)/shard_map/ppermute | solution.py:288
  173.4 74.9 %collective-permute-start.22 = (bf16[2,2,128,512]{3,2,1,0:T(8,128)(2,1)S(1)}, bf16[2,2,128,512]{3,2,1,0:T(8,128)(2,1)S(1)}, u32[]{:S(2)}, u32[]{:S(2)}) collective-permute-start(bf16[2,2,128,512]{3,2,1,0:T(8,128)(2,1)S(1)} %get-tuple-element.63), channel_id=1, source_target_pairs={{0,4},{1,5},{2,6},{3,7},{4,8},{5,9},{6,10},{7,11},{8,12},{9,13},{1... | collective-permute-start | bytes 1572872 | tf_op jit(solution)/shard_map/ppermute | solution.py:285
  175.3 73.0 %collective-permute-start.23 = (bf16[2,2,128,512]{3,2,1,0:T(8,128)(2,1)S(1)}, bf16[2,2,128,512]{3,2,1,0:T(8,128)(2,1)S(1)}, u32[]{:S(2)}, u32[]{:S(2)}) collective-permute-start(bf16[2,2,128,512]{3,2,1,0:T(8,128)(2,1)S(1)} %get-tuple-element.64), channel_id=1, source_target_pairs={{4,0},{5,1},{6,2},{7,3},{8,4},{9,5},{10,6},{11,7},{12,8},{13,9},{1... | collective-permute-start | bytes 1572872 | tf_op jit(solution)/shard_map/ppermute | solution.py:288
  183.2 47.7 %collective-permute-start.19 = (bf16[128,512]{1,0:T(8,128)(2,1)S(1)}, bf16[128,512]{1,0:T(8,128)(2,1)S(1)}, u32[]{:S(2)}, u32[]{:S(2)}) collective-permute-start(bf16[128,512]{1,0:T(8,128)(2,1)S(1)} %get-tuple-element.59), channel_id=1, source_target_pairs={{0,1},{1,2},{2,3},{3,0},{4,5},{5,6},{6,7},{7,4},{8,9},{9,10},{10,1... | collective-permute-start | bytes 393224 | tf_op jit(solution)/shard_map/ppermute | solution.py:281
  230.9 20.3 %collective-permute-start.20 = (bf16[128,512]{1,0:T(8,128)(2,1)S(1)}, bf16[128,512]{1,0:T(8,128)(2,1)S(1)}, u32[]{:S(2)}, u32[]{:S(2)}) collective-permute-start(bf16[128,512]{1,0:T(8,128)(2,1)S(1)} %get-tuple-element.60), channel_id=1, source_target_pairs={{0,2},{1,3},{2,0},{3,1},{4,6},{5,7},{6,4},{7,5},{8,10},{9,11},{10,... | collective-permute-start | bytes 393224 | tf_op jit(solution)/shard_map/ppermute | solution.py:281
  248.3 14.5 %collective-permute-start.8 = (bf16[128,768]{1,0:T(8,128)(2,1)S(1)}, bf16[128,768]{1,0:T(8,128)(2,1)S(1)}, u32[]{:S(2)}, u32[]{:S(2)}) collective-permute-start(bf16[128,768]{1,0:T(8,128)(2,1)S(1)} %get-tuple-element.45), channel_id=1, source_target_pairs={{0,1},{1,2},{2,3},{3,0},{4,5},{5,6},{6,7},{7,4},{8,9},{9,10},{10,1... | collective-permute-start | bytes 589832 | tf_op jit(solution)/shard_map/ppermute | solution.py:281
  248.3 16.1 %collective-permute-start.9 = (bf16[128,768]{1,0:T(8,128)(2,1)S(1)}, bf16[128,768]{1,0:T(8,128)(2,1)S(1)}, u32[]{:S(2)}, u32[]{:S(2)}) collective-permute-start(bf16[128,768]{1,0:T(8,128)(2,1)S(1)} %get-tuple-element.46), channel_id=1, source_target_pairs={{0,2},{1,3},{2,0},{3,1},{4,6},{5,7},{6,4},{7,5},{8,10},{9,11},{10,... | collective-permute-start | bytes 589832 | tf_op jit(solution)/shard_map/ppermute | solution.py:281
  251.3 10.3 %collective-permute-start.21 = (bf16[128,512]{1,0:T(8,128)(2,1)S(1)}, bf16[128,512]{1,0:T(8,128)(2,1)S(1)}, u32[]{:S(2)}, u32[]{:S(2)}) collective-permute-start(bf16[128,512]{1,0:T(8,128)(2,1)S(1)} %get-tuple-element.61), channel_id=1, source_target_pairs={{0,3},{1,0},{2,1},{3,2},{4,7},{5,4},{6,5},{7,6},{8,11},{9,8},{10,9... | collective-permute-start | bytes 393224 | tf_op jit(solution)/shard_map/ppermute | solution.py:281
  253.2 18.4 %collective-permute-start.24 = (bf16[2,128,512]{2,1,0:T(8,128)(2,1)S(1)}, bf16[2,128,512]{2,1,0:T(8,128)(2,1)S(1)}, u32[]{:S(2)}, u32[]{:S(2)}) collective-permute-start(bf16[2,128,512]{2,1,0:T(8,128)(2,1)S(1)} %get-tuple-element.66), channel_id=1, source_target_pairs={{0,1},{1,2},{2,3},{3,0},{4,5},{5,6},{6,7},{7,4},{8,9},{9,10},{10,1... | collective-permute-start | bytes 786440 | tf_op jit(solution)/shard_map/ppermute | solution.py:281
  255.7 12.8 %collective-permute-start.10 = (bf16[128,768]{1,0:T(8,128)(2,1)S(1)}, bf16[128,768]{1,0:T(8,128)(2,1)S(1)}, u32[]{:S(2)}, u32[]{:S(2)}) collective-permute-start(bf16[128,768]{1,0:T(8,128)(2,1)S(1)} %get-tuple-element.47), channel_id=1, source_target_pairs={{0,3},{1,0},{2,1},{3,2},{4,7},{5,4},{6,5},{7,6},{8,11},{9,8},{10,9... | collective-permute-start | bytes 589832 | tf_op jit(solution)/shard_map/ppermute | solution.py:281
  261.6 29.2 %collective-permute-start.13 = (bf16[2,128,768]{2,1,0:T(8,128)(2,1)S(1)}, bf16[2,128,768]{2,1,0:T(8,128)(2,1)S(1)}, u32[]{:S(2)}, u32[]{:S(2)}) collective-permute-start(bf16[2,128,768]{2,1,0:T(8,128)(2,1)S(1)} %get-tuple-element.52), channel_id=1, source_target_pairs={{0,1},{1,2},{2,3},{3,0},{4,5},{5,6},{6,7},{7,4},{8,9},{9,10},{10,1... | collective-permute-start | bytes 1179656 | tf_op jit(solution)/shard_map/ppermute | solution.py:281
  262.8 27.9 %collective-permute-start.14 = (bf16[2,128,768]{2,1,0:T(8,128)(2,1)S(1)}, bf16[2,128,768]{2,1,0:T(8,128)(2,1)S(1)}, u32[]{:S(2)}, u32[]{:S(2)}) collective-permute-start(bf16[2,128,768]{2,1,0:T(8,128)(2,1)S(1)} %get-tuple-element.53), channel_id=1, source_target_pairs={{0,2},{1,3},{2,0},{3,1},{4,6},{5,7},{6,4},{7,5},{8,10},{9,11},{10,... | collective-permute-start | bytes 1179656 | tf_op jit(solution)/shard_map/ppermute | solution.py:281
  264.4 26.3 %collective-permute-start.15 = (bf16[2,128,768]{2,1,0:T(8,128)(2,1)S(1)}, bf16[2,128,768]{2,1,0:T(8,128)(2,1)S(1)}, u32[]{:S(2)}, u32[]{:S(2)}) collective-permute-start(bf16[2,128,768]{2,1,0:T(8,128)(2,1)S(1)} %get-tuple-element.54), channel_id=1, source_target_pairs={{0,3},{1,0},{2,1},{3,2},{4,7},{5,4},{6,5},{7,6},{8,11},{9,8},{10,9... | collective-permute-start | bytes 1179656 | tf_op jit(solution)/shard_map/ppermute | solution.py:281
  268.4 17.5 %collective-permute-start.25 = (bf16[2,128,512]{2,1,0:T(8,128)(2,1)S(1)}, bf16[2,128,512]{2,1,0:T(8,128)(2,1)S(1)}, u32[]{:S(2)}, u32[]{:S(2)}) collective-permute-start(bf16[2,128,512]{2,1,0:T(8,128)(2,1)S(1)} %get-tuple-element.67), channel_id=1, source_target_pairs={{0,2},{1,3},{2,0},{3,1},{4,6},{5,7},{6,4},{7,5},{8,10},{9,11},{10,... | collective-permute-start | bytes 786440 | tf_op jit(solution)/shard_map/ppermute | solution.py:281
  271.7 19.1 %collective-permute-start.26 = (bf16[2,128,512]{2,1,0:T(8,128)(2,1)S(1)}, bf16[2,128,512]{2,1,0:T(8,128)(2,1)S(1)}, u32[]{:S(2)}, u32[]{:S(2)}) collective-permute-start(bf16[2,128,512]{2,1,0:T(8,128)(2,1)S(1)} %get-tuple-element.68), channel_id=1, source_target_pairs={{0,3},{1,0},{2,1},{3,2},{4,7},{5,4},{6,5},{7,6},{8,11},{9,8},{10,9... | collective-permute-start | bytes 786440 | tf_op jit(solution)/shard_map/ppermute | solution.py:281

commit v3 on v2

--- a/solution.py
+++ b/solution.py
@@ -30,37 +30,39 @@
     return pl.CostEstimate(flops=flops, bytes_accessed=nbytes, transcendentals=0)
 
 
-def pack_body(zh, a1, a2, a3, b1, b2, b3, o1, o2, o3):
-    for a, b, o in ((a1, b1, o1), (a2, b2, o2), (a3, b3, o3)):
-        o[0] = a[...]
-        o[1] = b[...]
-
-
-def pack(zh, a, b, first, heads, group):
+def pack_body(zh, *refs):
+    ins, (plus, minus) = refs[:-2], refs[-2:]
+    m = len(ins) // 2
+    for i in range(m):
+        plus[i] = ins[i][...]
+        minus[i] = ins[m + i][...]
+
+
+def pack(zh, plus, minus, first, heads, group):
     per, off, steps = group * HD // CW, first * HD // CW, heads * HD // CW
+    n, m = heads * HD, len(plus)
 
     def src(s):
         return pl.BlockSpec((BLK, CW), lambda i, z: (0, lax.rem(z[0] + s, NZ) * per + off + i))
 
-    out = pl.BlockSpec((2, BLK, CW), lambda i, z: (0, 0, i))
-    n = heads * HD
+    out = pl.BlockSpec((m, BLK, CW), lambda i, z: (0, 0, i))
     return pl.pallas_call(
         pack_body,
         grid_spec=pltpu.PrefetchScalarGridSpec(
             num_scalar_prefetch=1,
             grid=(steps,),
-            in_specs=[src(1), src(2), src(3), src(1), src(2), src(3)],
-            out_specs=[out, out, out],
-        ),
-        out_shape=[jax.ShapeDtypeStruct((2, BLK, n), BF)] * 3,
-        cost_estimate=cost(0, 12 * BLK * n * 2),
-        compiler_params=grant(8),
-    )(zh, a, a, a, b, b, b)
-
-
-def unpack_body(zh, k, v, r1, r2, r3, lo, hi):
+            in_specs=[src(s) for _, s in (*plus, *minus)],
+            out_specs=[out, out],
+        ),
+        out_shape=[jax.ShapeDtypeStruct((m, BLK, n), BF)] * 2,
+        cost_estimate=cost(0, 4 * m * BLK * n * 2),
+        compiler_params=grant(56),
+    )(zh, *[a for a, _ in (*plus, *minus)])
+
+
+def unpack_body(zh, k, v, mp, mm, fp, fm, lo, hi):
     z = zh[0]
-    for s, (kk, vv) in enumerate(((k, v), (r1.at[0], r1.at[1]), (r2.at[0], r2.at[1]), (r3.at[0], r3.at[1]))):
+    for s, (kk, vv) in enumerate(((k, v), (mp.at[0], mp.at[1]), (fp.at[0], fm.at[0]), (mm.at[0], mm.at[1]))):
         b = lax.rem(z + NZ - s, NZ)
 
         @pl.when(b < 2)
@@ -74,29 +76,29 @@
             hi[b - 2, 1] = vv[...]
 
 
-def unpack(zh, k, v, recv, group):
-    n = group * HD
-    per = n // CW
-    own = pl.BlockSpec((BLK, CW), lambda i, z: (0, z[0] * per + i))
-    got = pl.BlockSpec((2, BLK, CW), lambda i, z: (0, 0, i))
+def unpack(zh, k, v, recv, first, heads, group):
+    n = heads * HD
+    per, off = group * HD // CW, first * HD // CW
+    own = pl.BlockSpec((BLK, CW), lambda i, z: (0, z[0] * per + off + i))
+    two = pl.BlockSpec((2, BLK, CW), lambda i, z: (0, 0, i))
+    one = pl.BlockSpec((1, BLK, CW), lambda i, z: (0, 0, i))
     half = pl.BlockSpec((2, 2, BLK, CW), lambda i, z: (0, 0, 0, i))
     return pl.pallas_call(
         unpack_body,
         grid_spec=pltpu.PrefetchScalarGridSpec(
-            num_scalar_prefetch=1, grid=(per,), in_specs=[own, own, got, got, got], out_specs=[half, half]
+            num_scalar_prefetch=1, grid=(n // CW,), in_specs=[own, own, two, two, one, one], out_specs=[half, half]
         ),
         out_shape=[jax.ShapeDtypeStruct((2, 2, BLK, n), BF)] * 2,
         cost_estimate=cost(0, 16 * BLK * n * 2),
-        compiler_params=grant(10),
-        name="unpack",
+        compiler_params=grant(8),
     )(zh, k, v, *recv)
 
 
-def attend_body(zh, q0, g0, x1, x2, x3, before, lo, hi, after, bias,
+def attend_body(zh, q0, g0, mp, mm, fp, fm, before, lo, hi, after, bias,
                 dq0, dq1, dq2, dq3, rim_before, rim_after, own,
                 qs, gs, ks, vs, dqs, dk, dv):
     z = zh[0]
-    for s, (qq, gg) in enumerate(((q0, g0), (x1.at[0], x1.at[1]), (x2.at[0], x2.at[1]), (x3.at[0], x3.at[1]))):
+    for s, (qq, gg) in enumerate(((q0, g0), (mp.at[0], mp.at[1]), (fp.at[0], fm.at[0]), (mm.at[0], mm.at[1]))):
         row = pl.multiple_of(lax.rem(z + NZ - s, NZ) * BLK, BLK)
         qs[pl.ds(row, BLK), :] = qq[...]
         gs[pl.ds(row, BLK), :] = gg[...]
@@ -150,8 +152,8 @@
 def attend(zh, q, g, recv, before, lo, hi, after, bias, first, heads, group):
     n = heads * HD
     mine = pl.BlockSpec((BLK, HD), lambda h, z: (0, z[0] * group + first + h))
-    got = pl.BlockSpec((2, BLK, HD), lambda h, z: (0, 0, h))
-    keys = pl.BlockSpec((2, 2, BLK, HD), lambda h, z: (0, 0, 0, first + h))
+    two = pl.BlockSpec((2, BLK, HD), lambda h, z: (1, 0, h))
+    one = pl.BlockSpec((1, BLK, HD), lambda h, z: (1, 0, h))
     flat = pl.BlockSpec((BLK, HD), lambda h, z: (0, h))
     rim = pl.BlockSpec((2, 2, BLK, HD), lambda h, z: (0, 0, 0, h))
     own = pl.BlockSpec((4, 2, BLK, HD), lambda h, z: (0, 0, 0, h))
@@ -161,7 +163,7 @@
         grid_spec=pltpu.PrefetchScalarGridSpec(
             num_scalar_prefetch=1,
             grid=(heads,),
-            in_specs=[mine, mine, got, got, got, keys, keys, keys, keys,
+            in_specs=[mine, mine, two, two, one, one, rim, rim, rim, rim,
                       pl.BlockSpec((1, 2, 6, 2 * BLK), lambda h, z: (first + h, 0, 0, 0))],
             out_specs=[flat] * 4 + [rim, rim, own],
             scratch_shapes=[
@@ -275,25 +277,32 @@
     up = [(NZ * i + j, NZ * (i + 1) + j) for i in range(n_slabs - 1) for j in range(NZ)]
     down = [(b, a) for a, b in up]
 
+    def move(axes, perm, a):
+        return lax.ppermute(a, axes, perm)
+
     def around(arrays):
-        out = []
-        for s, a in enumerate(arrays, 1):
-            out.append(lax.ppermute(a, "uly", rings[s]))
-        return out
+        return [move("uly", rings[s], a) for s, a in enumerate(arrays, 1)]
 
     def to_next(a):
-        return lax.ppermute(a, ("ctx", "uly"), up)
+        return move(("ctx", "uly"), up, a)
 
     def to_prev(a):
-        return lax.ppermute(a, ("ctx", "uly"), down)
+        return move(("ctx", "uly"), down, a)
 
     bias = tile_bias(tile_mask, zh_s, slab, group)
-    kv = around(pack(zh, key, value, 0, group, group))
-    qg = [around(pack(zh, query, dout, first, heads, group)) for first, heads in CHUNKS]
-    lo, hi = unpack(zh, key, value, kv, group)
-    before, after = to_next(hi), to_prev(lo)
     parts = []
-    for (first, heads), recv in zip(CHUNKS, qg):
+    for first, heads in CHUNKS:
+        rp, rm = pack(zh, ((key, 2), (query, 2)), ((value, 2), (dout, 2)), first, heads, group)
+        mp, mm = pack(
+            zh, tuple((a, 1) for a in (key, value, query, dout)),
+            tuple((a, 3) for a in (key, value, query, dout)), first, heads, group,
+        )
+        rp, rm = move("uly", rings[1], rp), move("uly", rings[3], rm)
+        mp, mm = move("uly", rings[1], mp), move("uly", rings[3], mm)
+        fp, fm = move("uly", rings[1], rp), move("uly", rings[3], rm)
+        recv = (mp, mm, fp, fm)
+        lo, hi = unpack(zh, key, value, recv, first, heads, group)
+        before, after = to_next(hi), to_prev(lo)
         *dq, rim_before, rim_after, own = attend(
             zh, query, dout, recv, before, lo, hi, after, bias, first, heads, group
         )

time: 294 us -> 335 us (1.14)
  the two profiles are of different devices: /device:TPU:32 before, /device:TPU:57 now
where the time goes in v3:
time: 335 us; the launch traced here: 334 us
  waiting for transfers between devices  191 us (57%)
  starting transfers between devices  92 us (27%)
  Pallas kernels  45 us (13%)
  local copies, waits for them, and re-layouts  4.03 us (1%)
    ppermute x32, waiting for transfers between devices, move(): return lax.ppermute(a, axes, perm)  191 us
    ppermute x32, starting transfers between devices, move(): return lax.ppermute(a, axes, perm)  92 us
    pallas_call x2, Pallas kernels, attend(): pl.pallas_call(attend_body, grid_spec=pltpu.PrefetchScalarGridSpec(num_sc...  25.4 us
    pallas_call x4, Pallas kernels, pack(): pl.pallas_call(pack_body, grid_spec=pltpu.PrefetchScalarGridSpec(num_scal...  10.2 us
  transfers between devices with their start and end apart: 32, of which 9 were waited for; matrix products, arithmetic and copies ran while one was open for 0% of the time, Pallas kernels for 12%

profile of v3, /device:TPU:57, one launch (start us, length us, event | category | flops | bytes accessed | tf_op | source)
XLA Modules:
  0.0 333.5 jit_solution(4952934163675352918)
XLA Ops:
  0.6 1.8 shard_map.82
  2.5 3.0 collective-permute-start.18
  5.5 3.4 %shard_map.76 = (bf16[4,128,768]{2,1,0:T(8,128)(2,1)}, bf16[4,128,768]{2,1,0:T(8,128)(2,1)}) custom-call(s32[1]{0:T(128)} %bitcast.zh, bf16[128,5120]{1,0:T(8,128)(2,1)} %k.3, bf16[128,5120]{1,0:T(8,128)(2,1)} %v.3, bf16[128,5120]{1,0:T(8,128)(2,1)} %q0.3, bf16[128,5120]{1,0:T(8,128)(2,1)} %g0.3, bf16[128,5120]{1,0:T(8,128)(2,1)} %k.3, bf16[128,5120]{1,0:T(8,128)(2,1)} %v.3, ...), custom_call_target="tpu_custom_call" | custom-call | bytes 3145728 | tf_op jit(solution)/shard_map/pallas_call | solution.py:49
  8.9 3.3 collective-permute-start
  12.5 2.9 shard_map.77
  15.3 2.1 collective-permute-start.2
  17.4 1.5 collective-permute-start.4
  18.9 5.2 %collective-permute-done.18 = bf16[2,128,512]{2,1,0:T(8,128)(2,1)S(1)} collective-permute-done((bf16[2,128,512]{2,1,0:T(8,128)(2,1)}, bf16[2,128,512]{2,1,0:T(8,128)(2,1)S(1)}, u32[]{:S(2)}, u32[]{:S(2)}) %collective-permute-start.18) | collective-permute-done | bytes 262176 | tf_op jit(solution)/shard_map/ppermute | solution.py:281
  24.1 2.6 collective-permute-start.20
  26.7 2.1 shard_map.81
  28.8 32.4 %collective-permute-done.20 = bf16[2,128,512]{2,1,0:T(8,128)(2,1)S(1)} collective-permute-done((bf16[2,128,512]{2,1,0:T(8,128)(2,1)S(1)}, bf16[2,128,512]{2,1,0:T(8,128)(2,1)S(1)}, u32[]{:S(2)}, u32[]{:S(2)}) %collective-permute-start.20) | collective-permute-done | bytes 262176 | tf_op jit(solution)/shard_map/ppermute | solution.py:281
  61.2 0.7 copy-done.5
  61.9 17.6 %collective-permute-start.16 = (bf16[4,128,512]{2,1,0:T(8,128)(2,1)}, bf16[4,128,512]{2,1,0:T(8,128)(2,1)}, u32[]{:S(2)}, u32[]{:S(2)}) collective-permute-start(bf16[4,128,512]{2,1,0:T(8,128)(2,1)} %get-tuple-element.54), channel_id=1, source_target_pairs={{0,1},{1,2},{2,3},{3,0},{4,5},{5,6},{6,7},{7,4},{8,9},{9,10},{10,1... | collective-permute-start | bytes 1572872 | tf_op jit(solution)/shard_map/ppermute | solution.py:281
  79.6 3.6 %collective-permute-start.5 = (bf16[2,128,768]{2,1,0:T(8,128)(2,1)}, bf16[2,128,768]{2,1,0:T(8,128)(2,1)}, u32[]{:S(2)}, u32[]{:S(2)}) collective-permute-start(bf16[2,128,768]{2,1,0:T(8,128)(2,1)} %collective-permute-done.4), channel_id=1, source_target_pairs={{0,3},{1,0},{2,1},{3,2},{4,7},{5,4},{6,5},{7,6},{8,11},{9,8},{10,9... | collective-permute-start | bytes 1179656 | tf_op jit(solution)/shard_map/ppermute | solution.py:281
  83.2 2.3 collective-permute-start.19
  85.5 38.9 %collective-permute-done.3.fp = bf16[2,128,768]{2,1,0:T(8,128)(2,1)} collective-permute-done((bf16[2,128,768]{2,1,0:T(8,128)(2,1)}, bf16[2,128,768]{2,1,0:T(8,128)(2,1)}, u32[]{:S(2)}, u32[]{:S(2)}) %collective-permute-start.3) | collective-permute-done | bytes 393248 | tf_op jit(solution)/shard_map/ppermute | solution.py:281
  124.4 3.3 shard_map.78
  127.6 3.1 collective-permute-start.6
  130.8 6.4 %collective-permute-start.7 = (bf16[2,2,128,768]{3,2,1,0:T(8,128)(2,1)}, bf16[2,2,128,768]{3,2,1,0:T(8,128)(2,1)}, u32[]{:S(2)}, u32[]{:S(2)}) collective-permute-start(bf16[2,2,128,768]{3,2,1,0:T(8,128)(2,1)} %get-tuple-element.42.lo), channel_id=1, source_target_pairs={{4,0},{5,1},{6,2},{7,3},{8,4},{9,5},{10,6},{11,7},{12,8},{13,9},{1... | collective-permute-start | bytes 2359304 | tf_op jit(solution)/shard_map/ppermute | solution.py:281
  137.2 0.9 fusion.1
  138.3 2.1 shard_map.83
  140.4 1.9 collective-permute-start.22
  142.3 5.0 %collective-permute-start.23 = (bf16[2,2,128,512]{3,2,1,0:T(8,128)(2,1)}, bf16[2,2,128,512]{3,2,1,0:T(8,128)(2,1)S(1)}, u32[]{:S(2)}, u32[]{:S(2)}) collective-permute-start(bf16[2,2,128,512]{3,2,1,0:T(8,128)(2,1)} %get-tuple-element.59.lo), channel_id=1, source_target_pairs={{4,0},{5,1},{6,2},{7,3},{8,4},{9,5},{10,6},{11,7},{12,8},{13,9},{1... | collective-permute-start | bytes 1572872 | tf_op jit(solution)/shard_map/ppermute | solution.py:281
  147.9 11.5 %collective-permute-done.6.before = bf16[2,2,128,768]{3,2,1,0:T(8,128)(2,1)} collective-permute-done((bf16[2,2,128,768]{3,2,1,0:T(8,128)(2,1)}, bf16[2,2,128,768]{3,2,1,0:T(8,128)(2,1)}, u32[]{:S(2)}, u32[]{:S(2)}) %collective-permute-start.6) | collective-permute-done | bytes 786464 | tf_op jit(solution)/shard_map/ppermute | solution.py:281
  159.4 1.3 copy-done.2
  160.7 1.3 copy-done.3
  162.0 15.0 %shard_map.79 = (bf16[128,768]{1,0:T(8,128)(2,1)S(1)}, bf16[128,768]{1,0:T(8,128)(2,1)S(1)}, bf16[128,768]{1,0:T(8,128)(2,1)S(1)}, bf16[128,768]{1,0:T(8,128)(2,...) custom-call(s32[1]{0:T(128)} %bitcast.zh, ...), custom_call_target="tpu_custom_call" | custom-call | flops 3019898880 | bytes 7864320 | tf_op jit(solution)/shard_map/pallas_call | solution.py:161
  177.0 1.9 collective-permute-start.11
  178.9 4.9 %collective-permute-start.12 = (bf16[2,2,128,768]{3,2,1,0:T(8,128)(2,1)S(1)}, bf16[2,2,128,768]{3,2,1,0:T(8,128)(2,1)S(1)}, u32[]{:S(2)}, u32[]{:S(2)}) collective-permute-start(bf16[2,2,128,768]{3,2,1,0:T(8,128)(2,1)S(1)} %get-tuple-element.49), channel_id=1, source_target_pairs={{4,0},{5,1},{6,2},{7,3},{8,4},{9,5},{10,6},{11,7},{12,8},{13,9},{1... | collective-permute-start | bytes 2359304 | tf_op jit(solution)/shard_map/ppermute | solution.py:281
  183.8 10.4 %shard_map.84 = (bf16[128,512]{1,0:T(8,128)(2,1)S(1)}, bf16[128,512]{1,0:T(8,128)(2,1)S(1)}, bf16[128,512]{1,0:T(8,128)(2,1)S(1)}, bf16[128,512]{1,0:T(8,128)(2,...) custom-call(s32[1]{0:T(128)} %bitcast.zh, ...), custom_call_target="tpu_custom_call" | custom-call | flops 2013265920 | bytes 5242880 | tf_op jit(solution)/shard_map/pallas_call | solution.py:161
  194.3 1.9 collective-permute-start.27
  196.2 4.9 %collective-permute-start.28 = (bf16[2,2,128,512]{3,2,1,0:T(8,128)(2,1)S(1)}, bf16[2,2,128,512]{3,2,1,0:T(8,128)(2,1)S(1)}, u32[]{:S(2)}, u32[]{:S(2)}) collective-permute-start(bf16[2,2,128,512]{3,2,1,0:T(8,128)(2,1)S(1)} %get-tuple-element.66), channel_id=1, source_target_pairs={{4,0},{5,1},{6,2},{7,3},{8,4},{9,5},{10,6},{11,7},{12,8},{13,9},{1... | collective-permute-start | bytes 1572872 | tf_op jit(solution)/shard_map/ppermute | solution.py:281
  201.1 2.3 collective-permute-start.24
  203.3 52.4 %collective-permute-done.24.refs_9_ = bf16[128,512]{1,0:T(8,128)(2,1)S(1)} collective-permute-done((bf16[128,512]{1,0:T(8,128)(2,1)S(1)}, bf16[128,512]{1,0:T(8,128)(2,1)S(1)}, u32[]{:S(2)}, u32[]{:S(2)}) %collective-permute-start.24) | collective-permute-done | bytes 131104 | tf_op jit(solution)/shard_map/ppermute | solution.py:281
  255.7 8.8 %collective-permute-start.25 = (bf16[128,512]{1,0:T(8,128)(2,1)S(1)}, bf16[128,512]{1,0:T(8,128)(2,1)S(1)}, u32[]{:S(2)}, u32[]{:S(2)}) collective-permute-start(bf16[128,512]{1,0:T(8,128)(2,1)S(1)} %get-tuple-element.62), channel_id=1, source_target_pairs={{0,2},{1,3},{2,0},{3,1},{4,6},{5,7},{6,4},{7,5},{8,10},{9,11},{10,... | collective-permute-start | bytes 393224 | tf_op jit(solution)/shard_map/ppermute | solution.py:281
  264.7 0.6 shard_map.85
  265.3 2.7 collective-permute-done.25.refs_10_
  268.0 0.8 collective-permute-start.26
  268.9 2.2 collective-permute-start.29
  271.0 2.4 collective-permute-start.10
  273.5 0.9 shard_map.80
  274.4 8.0 %collective-permute-done.26.refs_11_ = bf16[128,512]{1,0:T(8,128)(2,1)S(1)} collective-permute-done((bf16[128,512]{1,0:T(8,128)(2,1)S(1)}, bf16[128,512]{1,0:T(8,128)(2,1)S(1)}, u32[]{:S(2)}, u32[]{:S(2)}) %collective-permute-start.26) | collective-permute-done | bytes 131104 | tf_op jit(solution)/shard_map/ppermute | solution.py:281
  282.4 2.7 collective-permute-start.14
  285.1 3.6 %collective-permute-start.15 = (bf16[2,128,768]{2,1,0:T(8,128)(2,1)S(1)}, bf16[2,128,768]{2,1,0:T(8,128)(2,1)S(1)}, u32[]{:S(2)}, u32[]{:S(2)}) collective-permute-start(bf16[2,128,768]{2,1,0:T(8,128)(2,1)S(1)} %get-tuple-element.53), channel_id=1, source_target_pairs={{0,3},{1,0},{2,1},{3,2},{4,7},{5,4},{6,5},{7,6},{8,11},{9,8},{10,9... | collective-permute-start | bytes 1179656 | tf_op jit(solution)/shard_map/ppermute | solution.py:281
  288.7 2.7 collective-permute-start.30
  291.5 26.4 %collective-permute-done.30.refs_14_ = bf16[2,128,512]{2,1,0:T(8,128)(2,1)S(1)} collective-permute-done((bf16[2,128,512]{2,1,0:T(8,128)(2,1)S(1)}, bf16[2,128,512]{2,1,0:T(8,128)(2,1)S(1)}, u32[]{:S(2)}, u32[]{:S(2)}) %collective-permute-start.30) | collective-permute-done | bytes 262176 | tf_op jit(solution)/shard_map/ppermute | solution.py:281
  317.9 13.2 %collective-permute-done.31.refs_15_ = bf16[2,128,512]{2,1,0:T(8,128)(2,1)S(1)} collective-permute-done((bf16[2,128,512]{2,1,0:T(8,128)(2,1)S(1)}, bf16[2,128,512]{2,1,0:T(8,128)(2,1)S(1)}, u32[]{:S(2)}, u32[]{:S(2)}) %collective-permute-start.31) | collective-permute-done | bytes 262176 | tf_op jit(solution)/shard_map/ppermute | solution.py:281
  331.1 2.4 assemble.1
  (52 shorter events, 1.3 us)
Async XLA Ops:
  2.5 21.6 %collective-permute-start.18 = (bf16[2,128,512]{2,1,0:T(8,128)(2,1)}, bf16[2,128,512]{2,1,0:T(8,128)(2,1)S(1)}, u32[]{:S(2)}, u32[]{:S(2)}) collective-permute-start(bf16[2,128,512]{2,1,0:T(8,128)(2,1)} %get-tuple-element.56), channel_id=1, source_target_pairs={{0,1},{1,2},{2,3},{3,0},{4,5},{5,6},{6,7},{7,4},{8,9},{9,10},{10,1... | collective-permute-start | bytes 786440 | tf_op jit(solution)/shard_map/ppermute | solution.py:281
  8.9 74.3 %collective-permute-start = (bf16[4,128,768]{2,1,0:T(8,128)(2,1)}, bf16[4,128,768]{2,1,0:T(8,128)(2,1)S(1)}, u32[]{:S(2)}, u32[]{:S(2)}) collective-permute-start(bf16[4,128,768]{2,1,0:T(8,128)(2,1)} %get-tuple-element.37), channel_id=1, source_target_pairs={{0,1},{1,2},{2,3},{3,0},{4,5},{5,6},{6,7},{7,4},{8,9},{9,10},{10,1... | collective-permute-start | bytes 2359304 | tf_op jit(solution)/shard_map/ppermute | solution.py:281
  12.2 11.9 %copy-start.6 = (bf16[2,128,512]{2,1,0:T(8,128)(2,1)S(1)}, bf16[2,128,512]{2,1,0:T(8,128)(2,1)}, u32[]{:S(2)}) copy-start(bf16[2,128,512]{2,1,0:T(8,128)(2,1)} %get-tuple-element.57) | copy-start | bytes 786436
  12.2 71.0 %collective-permute-start.1 = (bf16[4,128,768]{2,1,0:T(8,128)(2,1)}, bf16[4,128,768]{2,1,0:T(8,128)(2,1)}, u32[]{:S(2)}, u32[]{:S(2)}) collective-permute-start(bf16[4,128,768]{2,1,0:T(8,128)(2,1)} %get-tuple-element.38), channel_id=1, source_target_pairs={{0,3},{1,0},{2,1},{3,2},{4,7},{5,4},{6,5},{7,6},{8,11},{9,8},{10,9... | collective-permute-start | bytes 2359304 | tf_op jit(solution)/shard_map/ppermute | solution.py:281
  15.3 64.2 %collective-permute-start.2 = (bf16[2,128,768]{2,1,0:T(8,128)(2,1)}, bf16[2,128,768]{2,1,0:T(8,128)(2,1)}, u32[]{:S(2)}, u32[]{:S(2)}) collective-permute-start(bf16[2,128,768]{2,1,0:T(8,128)(2,1)} %get-tuple-element.39), channel_id=1, source_target_pairs={{0,1},{1,2},{2,3},{3,0},{4,5},{5,6},{6,7},{7,4},{8,9},{9,10},{10,1... | collective-permute-start | bytes 1179656 | tf_op jit(solution)/shard_map/ppermute | solution.py:281
  17.4 62.1 %collective-permute-start.4 = (bf16[2,128,768]{2,1,0:T(8,128)(2,1)}, bf16[2,128,768]{2,1,0:T(8,128)(2,1)}, u32[]{:S(2)}, u32[]{:S(2)}) collective-permute-start(bf16[2,128,768]{2,1,0:T(8,128)(2,1)} %get-tuple-element.40), channel_id=1, source_target_pairs={{0,3},{1,0},{2,1},{3,2},{4,7},{5,4},{6,5},{7,6},{8,11},{9,8},{10,9... | collective-permute-start | bytes 1179656 | tf_op jit(solution)/shard_map/ppermute | solution.py:281
  24.1 4.8 %copy-start.4 = (bf16[2,128,512]{2,1,0:T(8,128)(2,1)}, bf16[2,128,512]{2,1,0:T(8,128)(2,1)S(1)}, u32[]{:S(2)}) copy-start(bf16[2,128,512]{2,1,0:T(8,128)(2,1)S(1)} %collective-permute-done.18) | copy-start | bytes 786436
  24.1 100.3 %copy-start = (bf16[128,5120]{1,0:T(8,128)(2,1)S(1)}, bf16[128,5120]{1,0:T(8,128)(2,1)}, u32[]{:S(2)}) copy-start(bf16[128,5120]{1,0:T(8,128)(2,1)} %k.3) | copy-start | bytes 3932164
  24.1 100.3 %copy-start.1 = (bf16[128,5120]{1,0:T(8,128)(2,1)S(1)}, bf16[128,5120]{1,0:T(8,128)(2,1)}, u32[]{:S(2)}) copy-start(bf16[128,5120]{1,0:T(8,128)(2,1)} %v.3) | copy-start | bytes 3932164
  24.1 37.1 %collective-permute-start.20 = (bf16[2,128,512]{2,1,0:T(8,128)(2,1)S(1)}, bf16[2,128,512]{2,1,0:T(8,128)(2,1)S(1)}, u32[]{:S(2)}, u32[]{:S(2)}) collective-permute-start(bf16[2,128,512]{2,1,0:T(8,128)(2,1)S(1)} %copy-done.6), channel_id=1, source_target_pairs={{0,3},{1,0},{2,1},{3,2},{4,7},{5,4},{6,5},{7,6},{8,11},{9,8},{10,9... | collective-permute-start | bytes 786440 | tf_op jit(solution)/shard_map/ppermute | solution.py:281
  61.2 0.7 copy-start.5
  61.9 68.8 %collective-permute-start.16 = (bf16[4,128,512]{2,1,0:T(8,128)(2,1)}, bf16[4,128,512]{2,1,0:T(8,128)(2,1)}, u32[]{:S(2)}, u32[]{:S(2)}) collective-permute-start(bf16[4,128,512]{2,1,0:T(8,128)(2,1)} %get-tuple-element.54), channel_id=1, source_target_pairs={{0,1},{1,2},{2,3},{3,0},{4,5},{5,6},{6,7},{7,4},{8,9},{9,10},{10,1... | collective-permute-start | bytes 1572872 | tf_op jit(solution)/shard_map/ppermute | solution.py:281
  79.5 44.8 %collective-permute-start.3 = (bf16[2,128,768]{2,1,0:T(8,128)(2,1)}, bf16[2,128,768]{2,1,0:T(8,128)(2,1)}, u32[]{:S(2)}, u32[]{:S(2)}) collective-permute-start(bf16[2,128,768]{2,1,0:T(8,128)(2,1)} %collective-permute-done.2), channel_id=1, source_target_pairs={{0,1},{1,2},{2,3},{3,0},{4,5},{5,6},{6,7},{7,4},{8,9},{9,10},{10,1... | collective-permute-start | bytes 1179656 | tf_op jit(solution)/shard_map/ppermute | solution.py:281
  79.6 44.8 %collective-permute-start.5 = (bf16[2,128,768]{2,1,0:T(8,128)(2,1)}, bf16[2,128,768]{2,1,0:T(8,128)(2,1)}, u32[]{:S(2)}, u32[]{:S(2)}) collective-permute-start(bf16[2,128,768]{2,1,0:T(8,128)(2,1)} %collective-permute-done.4), channel_id=1, source_target_pairs={{0,3},{1,0},{2,1},{3,2},{4,7},{5,4},{6,5},{7,6},{8,11},{9,8},{10,9... | collective-permute-start | bytes 1179656 | tf_op jit(solution)/shard_map/ppermute | solution.py:281
  83.1 55.1 %collective-permute-start.17 = (bf16[4,128,512]{2,1,0:T(8,128)(2,1)}, bf16[4,128,512]{2,1,0:T(8,128)(2,1)}, u32[]{:S(2)}, u32[]{:S(2)}) collective-permute-start(bf16[4,128,512]{2,1,0:T(8,128)(2,1)} %get-tuple-element.55), channel_id=1, source_target_pairs={{0,3},{1,0},{2,1},{3,2},{4,7},{5,4},{6,5},{7,6},{8,11},{9,8},{10,9... | collective-permute-start | bytes 1572872 | tf_op jit(solution)/shard_map/ppermute | solution.py:281
  83.2 55.1 %collective-permute-start.19 = (bf16[2,128,512]{2,1,0:T(8,128)(2,1)}, bf16[2,128,512]{2,1,0:T(8,128)(2,1)}, u32[]{:S(2)}, u32[]{:S(2)}) collective-permute-start(bf16[2,128,512]{2,1,0:T(8,128)(2,1)} %copy-done.4), channel_id=1, source_target_pairs={{0,1},{1,2},{2,3},{3,0},{4,5},{5,6},{6,7},{7,4},{8,9},{9,10},{10,1... | collective-permute-start | bytes 786440 | tf_op jit(solution)/shard_map/ppermute | solution.py:281
  124.3 13.9 %collective-permute-start.21 = (bf16[2,128,512]{2,1,0:T(8,128)(2,1)}, bf16[2,128,512]{2,1,0:T(8,128)(2,1)}, u32[]{:S(2)}, u32[]{:S(2)}) collective-permute-start(bf16[2,128,512]{2,1,0:T(8,128)(2,1)} %copy-done.5), channel_id=1, source_target_pairs={{0,3},{1,0},{2,1},{3,2},{4,7},{5,4},{6,5},{7,6},{8,11},{9,8},{10,9... | collective-permute-start | bytes 786440 | tf_op jit(solution)/shard_map/ppermute | solution.py:281
  127.6 31.8 %collective-permute-start.6 = (bf16[2,2,128,768]{3,2,1,0:T(8,128)(2,1)}, bf16[2,2,128,768]{3,2,1,0:T(8,128)(2,1)}, u32[]{:S(2)}, u32[]{:S(2)}) collective-permute-start(bf16[2,2,128,768]{3,2,1,0:T(8,128)(2,1)} %get-tuple-element.41.hi), channel_id=1, source_target_pairs={{0,4},{1,5},{2,6},{3,7},{4,8},{5,9},{6,10},{7,11},{8,12},{9,13},{1... | collective-permute-start | bytes 2359304 | tf_op jit(solution)/shard_map/ppermute | solution.py:281
  130.8 28.6 %collective-permute-start.7 = (bf16[2,2,128,768]{3,2,1,0:T(8,128)(2,1)}, bf16[2,2,128,768]{3,2,1,0:T(8,128)(2,1)}, u32[]{:S(2)}, u32[]{:S(2)}) collective-permute-start(bf16[2,2,128,768]{3,2,1,0:T(8,128)(2,1)} %get-tuple-element.42.lo), channel_id=1, source_target_pairs={{4,0},{5,1},{6,2},{7,3},{8,4},{9,5},{10,6},{11,7},{12,8},{13,9},{1... | collective-permute-start | bytes 2359304 | tf_op jit(solution)/shard_map/ppermute | solution.py:281
  140.4 43.4 %collective-permute-start.22 = (bf16[2,2,128,512]{3,2,1,0:T(8,128)(2,1)}, bf16[2,2,128,512]{3,2,1,0:T(8,128)(2,1)S(1)}, u32[]{:S(2)}, u32[]{:S(2)}) collective-permute-start(bf16[2,2,128,512]{3,2,1,0:T(8,128)(2,1)} %get-tuple-element.58.hi), channel_id=1, source_target_pairs={{0,4},{1,5},{2,6},{3,7},{4,8},{5,9},{6,10},{7,11},{8,12},{9,13},{1... | collective-permute-start | bytes 1572872 | tf_op jit(solution)/shard_map/ppermute | solution.py:281
  142.3 41.5 %collective-permute-start.23 = (bf16[2,2,128,512]{3,2,1,0:T(8,128)(2,1)}, bf16[2,2,128,512]{3,2,1,0:T(8,128)(2,1)S(1)}, u32[]{:S(2)}, u32[]{:S(2)}) collective-permute-start(bf16[2,2,128,512]{3,2,1,0:T(8,128)(2,1)} %get-tuple-element.59.lo), channel_id=1, source_target_pairs={{4,0},{5,1},{6,2},{7,3},{8,4},{9,5},{10,6},{11,7},{12,8},{13,9},{1... | collective-permute-start | bytes 1572872 | tf_op jit(solution)/shard_map/ppermute | solution.py:281
  159.4 1.3 copy-start.2
  160.7 1.3 copy-start.3
  177.0 91.9 %collective-permute-start.11 = (bf16[2,2,128,768]{3,2,1,0:T(8,128)(2,1)S(1)}, bf16[2,2,128,768]{3,2,1,0:T(8,128)(2,1)S(1)}, u32[]{:S(2)}, u32[]{:S(2)}) collective-permute-start(bf16[2,2,128,768]{3,2,1,0:T(8,128)(2,1)S(1)} %get-tuple-element.48), channel_id=1, source_target_pairs={{0,4},{1,5},{2,6},{3,7},{4,8},{5,9},{6,10},{7,11},{8,12},{9,13},{1... | collective-permute-start | bytes 2359304 | tf_op jit(solution)/shard_map/ppermute | solution.py:281
  178.9 92.1 %collective-permute-start.12 = (bf16[2,2,128,768]{3,2,1,0:T(8,128)(2,1)S(1)}, bf16[2,2,128,768]{3,2,1,0:T(8,128)(2,1)S(1)}, u32[]{:S(2)}, u32[]{:S(2)}) collective-permute-start(bf16[2,2,128,768]{3,2,1,0:T(8,128)(2,1)S(1)} %get-tuple-element.49), channel_id=1, source_target_pairs={{4,0},{5,1},{6,2},{7,3},{8,4},{9,5},{10,6},{11,7},{12,8},{13,9},{1... | collective-permute-start | bytes 2359304 | tf_op jit(solution)/shard_map/ppermute | solution.py:281
  194.3 70.3 %collective-permute-start.27 = (bf16[2,2,128,512]{3,2,1,0:T(8,128)(2,1)S(1)}, bf16[2,2,128,512]{3,2,1,0:T(8,128)(2,1)S(1)}, u32[]{:S(2)}, u32[]{:S(2)}) collective-permute-start(bf16[2,2,128,512]{3,2,1,0:T(8,128)(2,1)S(1)} %get-tuple-element.65), channel_id=1, source_target_pairs={{0,4},{1,5},{2,6},{3,7},{4,8},{5,9},{6,10},{7,11},{8,12},{9,13},{1... | collective-permute-start | bytes 1572872 | tf_op jit(solution)/shard_map/ppermute | solution.py:281
  196.2 68.4 %collective-permute-start.28 = (bf16[2,2,128,512]{3,2,1,0:T(8,128)(2,1)S(1)}, bf16[2,2,128,512]{3,2,1,0:T(8,128)(2,1)S(1)}, u32[]{:S(2)}, u32[]{:S(2)}) collective-permute-start(bf16[2,2,128,512]{3,2,1,0:T(8,128)(2,1)S(1)} %get-tuple-element.66), channel_id=1, source_target_pairs={{4,0},{5,1},{6,2},{7,3},{8,4},{9,5},{10,6},{11,7},{12,8},{13,9},{1... | collective-permute-start | bytes 1572872 | tf_op jit(solution)/shard_map/ppermute | solution.py:281
  201.1 54.7 %collective-permute-start.24 = (bf16[128,512]{1,0:T(8,128)(2,1)S(1)}, bf16[128,512]{1,0:T(8,128)(2,1)S(1)}, u32[]{:S(2)}, u32[]{:S(2)}) collective-permute-start(bf16[128,512]{1,0:T(8,128)(2,1)S(1)} %get-tuple-element.61), channel_id=1, source_target_pairs={{0,1},{1,2},{2,3},{3,0},{4,5},{5,6},{6,7},{7,4},{8,9},{9,10},{10,1... | collective-permute-start | bytes 393224 | tf_op jit(solution)/shard_map/ppermute | solution.py:281
  255.7 12.3 %collective-permute-start.25 = (bf16[128,512]{1,0:T(8,128)(2,1)S(1)}, bf16[128,512]{1,0:T(8,128)(2,1)S(1)}, u32[]{:S(2)}, u32[]{:S(2)}) collective-permute-start(bf16[128,512]{1,0:T(8,128)(2,1)S(1)} %get-tuple-element.62), channel_id=1, source_target_pairs={{0,2},{1,3},{2,0},{3,1},{4,6},{5,7},{6,4},{7,5},{8,10},{9,11},{10,... | collective-permute-start | bytes 393224 | tf_op jit(solution)/shard_map/ppermute | solution.py:281
  264.6 17.9 %collective-permute-start.8 = (bf16[128,768]{1,0:T(8,128)(2,1)S(1)}, bf16[128,768]{1,0:T(8,128)(2,1)S(1)}, u32[]{:S(2)}, u32[]{:S(2)}) collective-permute-start(bf16[128,768]{1,0:T(8,128)(2,1)S(1)} %get-tuple-element.44), channel_id=1, source_target_pairs={{0,1},{1,2},{2,3},{3,0},{4,5},{5,6},{6,7},{7,4},{8,9},{9,10},{10,1... | collective-permute-start | bytes 589832 | tf_op jit(solution)/shard_map/ppermute | solution.py:281
  264.6 20.6 %collective-permute-start.9 = (bf16[128,768]{1,0:T(8,128)(2,1)S(1)}, bf16[128,768]{1,0:T(8,128)(2,1)S(1)}, u32[]{:S(2)}, u32[]{:S(2)}) collective-permute-start(bf16[128,768]{1,0:T(8,128)(2,1)S(1)} %get-tuple-element.45), channel_id=1, source_target_pairs={{0,2},{1,3},{2,0},{3,1},{4,6},{5,7},{6,4},{7,5},{8,10},{9,11},{10,... | collective-permute-start | bytes 589832 | tf_op jit(solution)/shard_map/ppermute | solution.py:281
  268.0 14.4 %collective-permute-start.26 = (bf16[128,512]{1,0:T(8,128)(2,1)S(1)}, bf16[128,512]{1,0:T(8,128)(2,1)S(1)}, u32[]{:S(2)}, u32[]{:S(2)}) collective-permute-start(bf16[128,512]{1,0:T(8,128)(2,1)S(1)} %get-tuple-element.63), channel_id=1, source_target_pairs={{0,3},{1,0},{2,1},{3,2},{4,7},{5,4},{6,5},{7,6},{8,11},{9,8},{10,9... | collective-permute-start | bytes 393224 | tf_op jit(solution)/shard_map/ppermute | solution.py:281
  268.9 22.5 %collective-permute-start.29 = (bf16[2,128,512]{2,1,0:T(8,128)(2,1)S(1)}, bf16[2,128,512]{2,1,0:T(8,128)(2,1)S(1)}, u32[]{:S(2)}, u32[]{:S(2)}) collective-permute-start(bf16[2,128,512]{2,1,0:T(8,128)(2,1)S(1)} %get-tuple-element.68), channel_id=1, source_target_pairs={{0,1},{1,2},{2,3},{3,0},{4,5},{5,6},{6,7},{7,4},{8,9},{9,10},{10,1... | collective-permute-start | bytes 786440 | tf_op jit(solution)/shard_map/ppermute | solution.py:281
  271.0 17.7 %collective-permute-start.10 = (bf16[128,768]{1,0:T(8,128)(2,1)S(1)}, bf16[128,768]{1,0:T(8,128)(2,1)S(1)}, u32[]{:S(2)}, u32[]{:S(2)}) collective-permute-start(bf16[128,768]{1,0:T(8,128)(2,1)S(1)} %get-tuple-element.46), channel_id=1, source_target_pairs={{0,3},{1,0},{2,1},{3,2},{4,7},{5,4},{6,5},{7,6},{8,11},{9,8},{10,9... | collective-permute-start | bytes 589832 | tf_op jit(solution)/shard_map/ppermute | solution.py:281
  282.4 48.7 %collective-permute-start.13 = (bf16[2,128,768]{2,1,0:T(8,128)(2,1)S(1)}, bf16[2,128,768]{2,1,0:T(8,128)(2,1)S(1)}, u32[]{:S(2)}, u32[]{:S(2)}) collective-permute-start(bf16[2,128,768]{2,1,0:T(8,128)(2,1)S(1)} %get-tuple-element.51), channel_id=1, source_target_pairs={{0,1},{1,2},{2,3},{3,0},{4,5},{5,6},{6,7},{7,4},{8,9},{9,10},{10,1... | collective-permute-start | bytes 1179656 | tf_op jit(solution)/shard_map/ppermute | solution.py:281
  282.4 48.7 %collective-permute-start.14 = (bf16[2,128,768]{2,1,0:T(8,128)(2,1)S(1)}, bf16[2,128,768]{2,1,0:T(8,128)(2,1)S(1)}, u32[]{:S(2)}, u32[]{:S(2)}) collective-permute-start(bf16[2,128,768]{2,1,0:T(8,128)(2,1)S(1)} %get-tuple-element.52), channel_id=1, source_target_pairs={{0,2},{1,3},{2,0},{3,1},{4,6},{5,7},{6,4},{7,5},{8,10},{9,11},{10,... | collective-permute-start | bytes 1179656 | tf_op jit(solution)/shard_map/ppermute | solution.py:281
  285.1 46.0 %collective-permute-start.15 = (bf16[2,128,768]{2,1,0:T(8,128)(2,1)S(1)}, bf16[2,128,768]{2,1,0:T(8,128)(2,1)S(1)}, u32[]{:S(2)}, u32[]{:S(2)}) collective-permute-start(bf16[2,128,768]{2,1,0:T(8,128)(2,1)S(1)} %get-tuple-element.53), channel_id=1, source_target_pairs={{0,3},{1,0},{2,1},{3,2},{4,7},{5,4},{6,5},{7,6},{8,11},{9,8},{10,9... | collective-permute-start | bytes 1179656 | tf_op jit(solution)/shard_map/ppermute | solution.py:281
  288.7 29.2 %collective-permute-start.30 = (bf16[2,128,512]{2,1,0:T(8,128)(2,1)S(1)}, bf16[2,128,512]{2,1,0:T(8,128)(2,1)S(1)}, u32[]{:S(2)}, u32[]{:S(2)}) collective-permute-start(bf16[2,128,512]{2,1,0:T(8,128)(2,1)S(1)} %get-tuple-element.69), channel_id=1, source_target_pairs={{0,2},{1,3},{2,0},{3,1},{4,6},{5,7},{6,4},{7,5},{8,10},{9,11},{10,... | collective-permute-start | bytes 786440 | tf_op jit(solution)/shard_map/ppermute | solution.py:281
  291.4 39.7 %collective-permute-start.31 = (bf16[2,128,512]{2,1,0:T(8,128)(2,1)S(1)}, bf16[2,128,512]{2,1,0:T(8,128)(2,1)S(1)}, u32[]{:S(2)}, u32[]{:S(2)}) collective-permute-start(bf16[2,128,512]{2,1,0:T(8,128)(2,1)S(1)} %get-tuple-element.70), channel_id=1, source_target_pairs={{0,3},{1,0},{2,1},{3,2},{4,7},{5,4},{6,5},{7,6},{8,11},{9,8},{10,9... | collective-permute-start | bytes 786440 | tf_op jit(solution)/shard_map/ppermute | solution.py:281

commit v4 on v3

--- a/solution.py
+++ b/solution.py
@@ -38,14 +38,14 @@
         minus[i] = ins[m + i][...]
 
 
-def pack(zh, plus, minus, first, heads, group):
-    per, off, steps = group * HD // CW, first * HD // CW, heads * HD // CW
+def pack(zh, plus, minus, first, heads, group, wide=CW):
+    per, off, steps = group * HD // wide, first * HD // wide, heads * HD // wide
     n, m = heads * HD, len(plus)
 
     def src(s):
-        return pl.BlockSpec((BLK, CW), lambda i, z: (0, lax.rem(z[0] + s, NZ) * per + off + i))
-
-    out = pl.BlockSpec((m, BLK, CW), lambda i, z: (0, 0, i))
+        return pl.BlockSpec((BLK, wide), lambda i, z: (0, lax.rem(z[0] + s, NZ) * per + off + i))
+
+    out = pl.BlockSpec((m, BLK, wide), lambda i, z: (0, 0, i))
     return pl.pallas_call(
         pack_body,
         grid_spec=pltpu.PrefetchScalarGridSpec(
@@ -80,8 +80,8 @@
     n = heads * HD
     per, off = group * HD // CW, first * HD // CW
     own = pl.BlockSpec((BLK, CW), lambda i, z: (0, z[0] * per + off + i))
-    two = pl.BlockSpec((2, BLK, CW), lambda i, z: (0, 0, i))
-    one = pl.BlockSpec((1, BLK, CW), lambda i, z: (0, 0, i))
+    two = pl.BlockSpec((2, BLK, CW), lambda i, z: (0, 0, off + i))
+    one = pl.BlockSpec((1, BLK, CW), lambda i, z: (0, 0, off + i))
     half = pl.BlockSpec((2, 2, BLK, CW), lambda i, z: (0, 0, 0, i))
     return pl.pallas_call(
         unpack_body,
@@ -152,8 +152,8 @@
 def attend(zh, q, g, recv, before, lo, hi, after, bias, first, heads, group):
     n = heads * HD
     mine = pl.BlockSpec((BLK, HD), lambda h, z: (0, z[0] * group + first + h))
-    two = pl.BlockSpec((2, BLK, HD), lambda h, z: (1, 0, h))
-    one = pl.BlockSpec((1, BLK, HD), lambda h, z: (1, 0, h))
+    two = pl.BlockSpec((2, BLK, HD), lambda h, z: (0, 0, h))
+    one = pl.BlockSpec((1, BLK, HD), lambda h, z: (0, 0, h))
     flat = pl.BlockSpec((BLK, HD), lambda h, z: (0, h))
     rim = pl.BlockSpec((2, 2, BLK, HD), lambda h, z: (0, 0, 0, h))
     own = pl.BlockSpec((4, 2, BLK, HD), lambda h, z: (0, 0, 0, h))
@@ -290,18 +290,21 @@
         return move(("ctx", "uly"), down, a)
 
     bias = tile_bias(tile_mask, zh_s, slab, group)
-    parts = []
-    for first, heads in CHUNKS:
-        rp, rm = pack(zh, ((key, 2), (query, 2)), ((value, 2), (dout, 2)), first, heads, group)
-        mp, mm = pack(
-            zh, tuple((a, 1) for a in (key, value, query, dout)),
-            tuple((a, 3) for a in (key, value, query, dout)), first, heads, group,
-        )
+
+    def gather(a, b, first, heads, wide):
+        rp, rm = pack(zh, ((a, 2),), ((b, 2),), first, heads, group, wide)
+        mp, mm = pack(zh, ((a, 1), (b, 1)), ((a, 3), (b, 3)), first, heads, group, wide)
         rp, rm = move("uly", rings[1], rp), move("uly", rings[3], rm)
         mp, mm = move("uly", rings[1], mp), move("uly", rings[3], mm)
         fp, fm = move("uly", rings[1], rp), move("uly", rings[3], rm)
-        recv = (mp, mm, fp, fm)
-        lo, hi = unpack(zh, key, value, recv, first, heads, group)
+        return mp, mm, fp, fm
+
+    kv = gather(key, value, 0, group, group * HD // 2)
+    qg = [gather(query, dout, first, heads, CW) for first, heads in CHUNKS]
+    parts = []
+    for c, (first, heads) in enumerate(CHUNKS):
+        recv = qg[c]
+        lo, hi = unpack(zh, key, value, kv, first, heads, group)
         before, after = to_next(hi), to_prev(lo)
         *dq, rim_before, rim_after, own = attend(
             zh, query, dout, recv, before, lo, hi, after, bias, first, heads, group

time: 335 us -> 313 us (0.934)
  the two profiles are of different devices: /device:TPU:57 before, /device:TPU:32 now
where the time goes in v4:
time: 313 us; the launch traced here: 312 us
  waiting for transfers between devices  140 us (45%)
  starting transfers between devices  112 us (36%)
  Pallas kernels  47.9 us (15%)
  local copies, waits for them, and re-layouts  10.1 us (3%)
    ppermute x38, waiting for transfers between devices, move(): return lax.ppermute(a, axes, perm)  140 us
    ppermute x38, starting transfers between devices, move(): return lax.ppermute(a, axes, perm)  112 us
    pallas_call x2, Pallas kernels, attend(): pl.pallas_call(attend_body, grid_spec=pltpu.PrefetchScalarGridSpec(num_sc...  25.4 us
    pallas_call x6, Pallas kernels, pack(): pl.pallas_call(pack_body, grid_spec=pltpu.PrefetchScalarGridSpec(num_scal...  13.4 us
  transfers between devices with their start and end apart: 38, of which 9 were waited for; matrix products, arithmetic and copies ran while one was open for 2% of the time, Pallas kernels for 14%

profile of v4, /device:TPU:32, one launch (start us, length us, event | category | flops | bytes accessed | tf_op | source)
XLA Modules:
  0.0 311.7 jit_solution(13225200389445140797)
XLA Ops:
  0.6 2.0 shard_map.79
  2.6 3.3 %collective-permute-start.8 = (bf16[1,128,1280]{2,1,0:T(8,128)(2,1)}, bf16[1,128,1280]{2,1,0:T(8,128)(2,1)S(1)}, u32[]{:S(2)}, u32[]{:S(2)}) collective-permute-start(bf16[1,128,1280]{2,1,0:T(8,128)(2,1)} %get-tuple-element.47), channel_id=1, source_target_pairs={{0,1},{1,2},{2,3},{3,0},{4,5},{5,6},{6,7},{7,4},{8,9},{9,10},{10,1... | collective-permute-start | bytes 983048 | tf_op jit(solution)/shard_map/ppermute | solution.py:281
  5.9 2.2 collective-permute-start.10
  8.0 2.3 shard_map.78
  11.8 2.7 collective-permute-start.7
  14.5 19.3 %collective-permute-done.8 = bf16[1,128,1280]{2,1,0:T(8,128)(2,1)S(1)} collective-permute-done((bf16[1,128,1280]{2,1,0:T(8,128)(2,1)}, bf16[1,128,1280]{2,1,0:T(8,128)(2,1)S(1)}, u32[]{:S(2)}, u32[]{:S(2)}) %collective-permute-start.8) | collective-permute-done | bytes 327712 | tf_op jit(solution)/shard_map/ppermute | solution.py:281
  33.8 1.6 collective-permute-start.9
  35.4 2.6 collective-permute-start.11
  37.9 1.6 shard_map.84
  40.8 2.5 shard_map.77
  43.4 27.4 %collective-permute-done.24 = bf16[1,128,512]{2,1,0:T(8,128)(2,1)S(1)} collective-permute-done((bf16[1,128,512]{2,1,0:T(8,128)(2,1)}, bf16[1,128,512]{2,1,0:T(8,128)(2,1)S(1)}, u32[]{:S(2)}, u32[]{:S(2)}) %collective-permute-start.24) | collective-permute-done | bytes 131104 | tf_op jit(solution)/shard_map/ppermute | solution.py:281
  72.2 3.5 %collective-permute-start.26 = (bf16[1,128,512]{2,1,0:T(8,128)(2,1)}, bf16[1,128,512]{2,1,0:T(8,128)(2,1)}, u32[]{:S(2)}, u32[]{:S(2)}) collective-permute-start(bf16[1,128,512]{2,1,0:T(8,128)(2,1)} %get-tuple-element.65), channel_id=1, source_target_pairs={{0,3},{1,0},{2,1},{3,2},{4,7},{5,4},{6,5},{7,6},{8,11},{9,8},{10,9... | collective-permute-start | bytes 393224 | tf_op jit(solution)/shard_map/ppermute | solution.py:281
  75.7 3.0 shard_map.76
  79.9 1.8 collective-permute-start
  83.3 3.1 shard_map.80
  86.5 3.4 %collective-permute-start.12 = (bf16[2,2,128,768]{3,2,1,0:T(8,128)(2,1)}, bf16[2,2,128,768]{3,2,1,0:T(8,128)(2,1)}, u32[]{:S(2)}, u32[]{:S(2)}) collective-permute-start(bf16[2,2,128,768]{3,2,1,0:T(8,128)(2,1)} %get-tuple-element.49.hi), channel_id=1, source_target_pairs={{0,4},{1,5},{2,6},{3,7},{4,8},{5,9},{6,10},{7,11},{8,12},{9,13},{1... | collective-permute-start | bytes 2359304 | tf_op jit(solution)/shard_map/ppermute | solution.py:281
  89.9 6.4 %collective-permute-start.13 = (bf16[2,2,128,768]{3,2,1,0:T(8,128)(2,1)}, bf16[2,2,128,768]{3,2,1,0:T(8,128)(2,1)}, u32[]{:S(2)}, u32[]{:S(2)}) collective-permute-start(bf16[2,2,128,768]{3,2,1,0:T(8,128)(2,1)} %get-tuple-element.50.lo), channel_id=1, source_target_pairs={{4,0},{5,1},{6,2},{7,3},{8,4},{9,5},{10,6},{11,7},{12,8},{13,9},{1... | collective-permute-start | bytes 2359304 | tf_op jit(solution)/shard_map/ppermute | solution.py:281
  96.3 2.7 collective-permute-start.3
  99.0 10.3 %collective-permute-done.25.fp = bf16[1,128,512]{2,1,0:T(8,128)(2,1)} collective-permute-done((bf16[1,128,512]{2,1,0:T(8,128)(2,1)}, bf16[1,128,512]{2,1,0:T(8,128)(2,1)}, u32[]{:S(2)}, u32[]{:S(2)}) %collective-permute-start.25) | collective-permute-done | bytes 131104 | tf_op jit(solution)/shard_map/ppermute | solution.py:281
  112.4 2.0 shard_map.85
  117.3 3.4 %collective-permute-start.28 = (bf16[2,2,128,512]{3,2,1,0:T(8,128)(2,1)}, bf16[2,2,128,512]{3,2,1,0:T(8,128)(2,1)S(1)}, u32[]{:S(2)}, u32[]{:S(2)}) collective-permute-start(bf16[2,2,128,512]{3,2,1,0:T(8,128)(2,1)} %get-tuple-element.66.hi), channel_id=1, source_target_pairs={{0,4},{1,5},{2,6},{3,7},{4,8},{5,9},{6,10},{7,11},{8,12},{9,13},{1... | collective-permute-start | bytes 1572872 | tf_op jit(solution)/shard_map/ppermute | solution.py:281
  120.7 14.6 %collective-permute-start.29 = (bf16[2,2,128,512]{3,2,1,0:T(8,128)(2,1)}, bf16[2,2,128,512]{3,2,1,0:T(8,128)(2,1)}, u32[]{:S(2)}, u32[]{:S(2)}) collective-permute-start(bf16[2,2,128,512]{3,2,1,0:T(8,128)(2,1)} %get-tuple-element.67.lo), channel_id=1, source_target_pairs={{4,0},{5,1},{6,2},{7,3},{8,4},{9,5},{10,6},{11,7},{12,8},{13,9},{1... | collective-permute-start | bytes 1572872 | tf_op jit(solution)/shard_map/ppermute | solution.py:281
  135.4 2.0 shard_map.83
  138.2 1.7 broadcast_in_dim.17
  139.8 1.7 reshape.61
  143.1 3.6 %collective-permute-start.23 = (bf16[2,128,512]{2,1,0:T(8,128)(2,1)}, bf16[2,128,512]{2,1,0:T(8,128)(2,1)S(1)}, u32[]{:S(2)}, u32[]{:S(2)}) collective-permute-start(bf16[2,128,512]{2,1,0:T(8,128)(2,1)} %get-tuple-element.63), channel_id=1, source_target_pairs={{0,3},{1,0},{2,1},{3,2},{4,7},{5,4},{6,5},{7,6},{8,11},{9,8},{10,9... | collective-permute-start | bytes 786440 | tf_op jit(solution)/shard_map/ppermute | solution.py:281
  147.9 14.9 %shard_map.81 = (bf16[128,768]{1,0:T(8,128)(2,1)S(1)}, bf16[128,768]{1,0:T(8,128)(2,1)S(1)}, bf16[128,768]{1,0:T(8,128)(2,1)S(1)}, bf16[128,768]{1,0:T(8,128)(2,...) custom-call(s32[1]{0:T(128)} %bitcast.zh, ...), custom_call_target="tpu_custom_call" | custom-call | flops 3019898880 | bytes 7864320 | tf_op jit(solution)/shard_map/pallas_call | solution.py:161
  162.8 2.3 collective-permute-start.17
  165.1 7.5 %collective-permute-start.18 = (bf16[2,2,128,768]{3,2,1,0:T(8,128)(2,1)S(1)}, bf16[2,2,128,768]{3,2,1,0:T(8,128)(2,1)S(1)}, u32[]{:S(2)}, u32[]{:S(2)}) collective-permute-start(bf16[2,2,128,768]{3,2,1,0:T(8,128)(2,1)S(1)} %get-tuple-element.57), channel_id=1, source_target_pairs={{4,0},{5,1},{6,2},{7,3},{8,4},{9,5},{10,6},{11,7},{12,8},{13,9},{1... | collective-permute-start | bytes 2359304 | tf_op jit(solution)/shard_map/ppermute | solution.py:281
  172.6 10.5 %shard_map.86 = (bf16[128,512]{1,0:T(8,128)(2,1)S(1)}, bf16[128,512]{1,0:T(8,128)(2,1)S(1)}, bf16[128,512]{1,0:T(8,128)(2,1)S(1)}, bf16[128,512]{1,0:T(8,128)(2,...) custom-call(s32[1]{0:T(128)} %bitcast.zh, ...), custom_call_target="tpu_custom_call" | custom-call | flops 2013265920 | bytes 5242880 | tf_op jit(solution)/shard_map/pallas_call | solution.py:161
  183.1 1.9 collective-permute-start.33
  185.1 7.9 %collective-permute-start.34 = (bf16[2,2,128,512]{3,2,1,0:T(8,128)(2,1)S(1)}, bf16[2,2,128,512]{3,2,1,0:T(8,128)(2,1)S(1)}, u32[]{:S(2)}, u32[]{:S(2)}) collective-permute-start(bf16[2,2,128,512]{3,2,1,0:T(8,128)(2,1)S(1)} %get-tuple-element.74), channel_id=1, source_target_pairs={{4,0},{5,1},{6,2},{7,3},{8,4},{9,5},{10,6},{11,7},{12,8},{13,9},{1... | collective-permute-start | bytes 1572872 | tf_op jit(solution)/shard_map/ppermute | solution.py:281
  192.9 2.8 collective-permute-start.30
  195.7 55.3 %collective-permute-done.30.refs_9_ = bf16[128,512]{1,0:T(8,128)(2,1)S(1)} collective-permute-done((bf16[128,512]{1,0:T(8,128)(2,1)S(1)}, bf16[128,512]{1,0:T(8,128)(2,1)S(1)}, u32[]{:S(2)}, u32[]{:S(2)}) %collective-permute-start.30) | collective-permute-done | bytes 131104 | tf_op jit(solution)/shard_map/ppermute | solution.py:281
  251.0 1.9 collective-permute-start.31
  252.8 2.3 collective-permute-start.14
  255.1 4.2 %collective-permute-start.15 = (bf16[128,768]{1,0:T(8,128)(2,1)S(1)}, bf16[128,768]{1,0:T(8,128)(2,1)S(1)}, u32[]{:S(2)}, u32[]{:S(2)}) collective-permute-start(bf16[128,768]{1,0:T(8,128)(2,1)S(1)} %get-tuple-element.53), channel_id=1, source_target_pairs={{0,2},{1,3},{2,0},{3,1},{4,6},{5,7},{6,4},{7,5},{8,10},{9,11},{10,... | collective-permute-start | bytes 589832 | tf_op jit(solution)/shard_map/ppermute | solution.py:281
  261.4 5.2 %collective-permute-start.32 = (bf16[128,512]{1,0:T(8,128)(2,1)S(1)}, bf16[128,512]{1,0:T(8,128)(2,1)S(1)}, u32[]{:S(2)}, u32[]{:S(2)}) collective-permute-start(bf16[128,512]{1,0:T(8,128)(2,1)S(1)} %get-tuple-element.71), channel_id=1, source_target_pairs={{0,3},{1,0},{2,1},{3,2},{4,7},{5,4},{6,5},{7,6},{8,11},{9,8},{10,9... | collective-permute-start | bytes 393224 | tf_op jit(solution)/shard_map/ppermute | solution.py:281
  266.6 1.7 collective-permute-start.35
  268.3 2.5 collective-permute-start.16
  271.7 2.7 collective-permute-done.32.refs_11_
  274.4 3.7 %collective-permute-start.19 = (bf16[2,128,768]{2,1,0:T(8,128)(2,1)S(1)}, bf16[2,128,768]{2,1,0:T(8,128)(2,1)S(1)}, u32[]{:S(2)}, u32[]{:S(2)}) collective-permute-start(bf16[2,128,768]{2,1,0:T(8,128)(2,1)S(1)} %get-tuple-element.59), channel_id=1, source_target_pairs={{0,1},{1,2},{2,3},{3,0},{4,5},{5,6},{6,7},{7,4},{8,9},{9,10},{10,1... | collective-permute-start | bytes 1179656 | tf_op jit(solution)/shard_map/ppermute | solution.py:281
  278.0 2.4 collective-permute-start.20
  281.7 2.7 collective-permute-start.36
  284.4 2.5 collective-permute-start.37
  287.0 18.4 %collective-permute-done.36.refs_14_ = bf16[2,128,512]{2,1,0:T(8,128)(2,1)S(1)} collective-permute-done((bf16[2,128,512]{2,1,0:T(8,128)(2,1)S(1)}, bf16[2,128,512]{2,1,0:T(8,128)(2,1)S(1)}, u32[]{:S(2)}, u32[]{:S(2)}) %collective-permute-start.36) | collective-permute-done | bytes 262176 | tf_op jit(solution)/shard_map/ppermute | solution.py:281
  305.4 3.9 %collective-permute-done.37.refs_15_ = bf16[2,128,512]{2,1,0:T(8,128)(2,1)S(1)} collective-permute-done((bf16[2,128,512]{2,1,0:T(8,128)(2,1)S(1)}, bf16[2,128,512]{2,1,0:T(8,128)(2,1)S(1)}, u32[]{:S(2)}, u32[]{:S(2)}) %collective-permute-start.37) | collective-permute-done | bytes 262176 | tf_op jit(solution)/shard_map/ppermute | solution.py:281
  309.3 2.4 assemble.1
  (74 shorter events, 20.8 us)
Async XLA Ops:
  2.6 31.2 %collective-permute-start.8 = (bf16[1,128,1280]{2,1,0:T(8,128)(2,1)}, bf16[1,128,1280]{2,1,0:T(8,128)(2,1)S(1)}, u32[]{:S(2)}, u32[]{:S(2)}) collective-permute-start(bf16[1,128,1280]{2,1,0:T(8,128)(2,1)} %get-tuple-element.47), channel_id=1, source_target_pairs={{0,1},{1,2},{2,3},{3,0},{4,5},{5,6},{6,7},{7,4},{8,9},{9,10},{10,1... | collective-permute-start | bytes 983048 | tf_op jit(solution)/shard_map/ppermute | solution.py:281
  5.9 29.5 %collective-permute-start.10 = (bf16[1,128,1280]{2,1,0:T(8,128)(2,1)}, bf16[1,128,1280]{2,1,0:T(8,128)(2,1)}, u32[]{:S(2)}, u32[]{:S(2)}) collective-permute-start(bf16[1,128,1280]{2,1,0:T(8,128)(2,1)} %get-tuple-element.48), channel_id=1, source_target_pairs={{0,3},{1,0},{2,1},{3,2},{4,7},{5,4},{6,5},{7,6},{8,11},{9,8},{10,9... | collective-permute-start | bytes 983048 | tf_op jit(solution)/shard_map/ppermute | solution.py:281
  10.3 69.6 %collective-permute-start.6 = (bf16[2,128,1280]{2,1,0:T(8,128)(2,1)}, bf16[2,128,1280]{2,1,0:T(8,128)(2,1)S(1)}, u32[]{:S(2)}, u32[]{:S(2)}) collective-permute-start(bf16[2,128,1280]{2,1,0:T(8,128)(2,1)} %get-tuple-element.45), channel_id=1, source_target_pairs={{0,1},{1,2},{2,3},{3,0},{4,5},{5,6},{6,7},{7,4},{8,9},{9,10},{10,1... | collective-permute-start | bytes 1966088 | tf_op jit(solution)/shard_map/ppermute | solution.py:281
  11.8 70.0 %collective-permute-start.7 = (bf16[2,128,1280]{2,1,0:T(8,128)(2,1)}, bf16[2,128,1280]{2,1,0:T(8,128)(2,1)}, u32[]{:S(2)}, u32[]{:S(2)}) collective-permute-start(bf16[2,128,1280]{2,1,0:T(8,128)(2,1)} %get-tuple-element.46), channel_id=1, source_target_pairs={{0,3},{1,0},{2,1},{3,2},{4,7},{5,4},{6,5},{7,6},{8,11},{9,8},{10,9... | collective-permute-start | bytes 1966088 | tf_op jit(solution)/shard_map/ppermute | solution.py:281
  33.8 37.1 %collective-permute-start.9 = (bf16[1,128,1280]{2,1,0:T(8,128)(2,1)S(1)}, bf16[1,128,1280]{2,1,0:T(8,128)(2,1)S(1)}, u32[]{:S(2)}, u32[]{:S(2)}) collective-permute-start(bf16[1,128,1280]{2,1,0:T(8,128)(2,1)S(1)} %collective-permute-done.8), channel_id=1, source_target_pairs={{0,1},{1,2},{2,3},{3,0},{4,5},{5,6},{6,7},{7,4},{8,9},{9,10},{10,1... | collective-permute-start | bytes 983048 | tf_op jit(solution)/shard_map/ppermute | solution.py:281
  35.4 43.3 %collective-permute-start.11 = (bf16[1,128,1280]{2,1,0:T(8,128)(2,1)}, bf16[1,128,1280]{2,1,0:T(8,128)(2,1)}, u32[]{:S(2)}, u32[]{:S(2)}) collective-permute-start(bf16[1,128,1280]{2,1,0:T(8,128)(2,1)} %collective-permute-done.10), channel_id=1, source_target_pairs={{0,3},{1,0},{2,1},{3,2},{4,7},{5,4},{6,5},{7,6},{8,11},{9,8},{10,9... | collective-permute-start | bytes 983048 | tf_op jit(solution)/shard_map/ppermute | solution.py:281
  39.5 31.2 %collective-permute-start.24 = (bf16[1,128,512]{2,1,0:T(8,128)(2,1)}, bf16[1,128,512]{2,1,0:T(8,128)(2,1)S(1)}, u32[]{:S(2)}, u32[]{:S(2)}) collective-permute-start(bf16[1,128,512]{2,1,0:T(8,128)(2,1)} %get-tuple-element.64), channel_id=1, source_target_pairs={{0,1},{1,2},{2,3},{3,0},{4,5},{5,6},{6,7},{7,4},{8,9},{9,10},{10,1... | collective-permute-start | bytes 393224 | tf_op jit(solution)/shard_map/ppermute | solution.py:281
  70.8 19.1 %collective-permute-start.2 = (bf16[1,128,768]{2,1,0:T(8,128)(2,1)}, bf16[1,128,768]{2,1,0:T(8,128)(2,1)S(1)}, u32[]{:S(2)}, u32[]{:S(2)}) collective-permute-start(bf16[1,128,768]{2,1,0:T(8,128)(2,1)} %get-tuple-element.43), channel_id=1, source_target_pairs={{0,1},{1,2},{2,3},{3,0},{4,5},{5,6},{6,7},{7,4},{8,9},{9,10},{10,1... | collective-permute-start | bytes 589832 | tf_op jit(solution)/shard_map/ppermute | solution.py:281
  71.4 0.7 copy-start.4
  72.2 14.3 %collective-permute-start.26 = (bf16[1,128,512]{2,1,0:T(8,128)(2,1)}, bf16[1,128,512]{2,1,0:T(8,128)(2,1)}, u32[]{:S(2)}, u32[]{:S(2)}) collective-permute-start(bf16[1,128,512]{2,1,0:T(8,128)(2,1)} %get-tuple-element.65), channel_id=1, source_target_pairs={{0,3},{1,0},{2,1},{3,2},{4,7},{5,4},{6,5},{7,6},{8,11},{9,8},{10,9... | collective-permute-start | bytes 393224 | tf_op jit(solution)/shard_map/ppermute | solution.py:281
  75.6 6.7 %copy-start.2 = (bf16[128,5120]{1,0:T(8,128)(2,1)S(1)}, bf16[128,5120]{1,0:T(8,128)(2,1)}, u32[]{:S(2)}) copy-start(bf16[128,5120]{1,0:T(8,128)(2,1)} %k.3) | copy-start | bytes 3932164
  75.7 6.7 %copy-start.3 = (bf16[128,5120]{1,0:T(8,128)(2,1)S(1)}, bf16[128,5120]{1,0:T(8,128)(2,1)}, u32[]{:S(2)}) copy-start(bf16[128,5120]{1,0:T(8,128)(2,1)} %v.3) | copy-start | bytes 3932164
  78.7 17.6 %collective-permute-start.4 = (bf16[1,128,768]{2,1,0:T(8,128)(2,1)}, bf16[1,128,768]{2,1,0:T(8,128)(2,1)}, u32[]{:S(2)}, u32[]{:S(2)}) collective-permute-start(bf16[1,128,768]{2,1,0:T(8,128)(2,1)} %get-tuple-element.44), channel_id=1, source_target_pairs={{0,3},{1,0},{2,1},{3,2},{4,7},{5,4},{6,5},{7,6},{8,11},{9,8},{10,9... | collective-permute-start | bytes 589832 | tf_op jit(solution)/shard_map/ppermute | solution.py:281
  79.9 40.8 %collective-permute-start = (bf16[2,128,768]{2,1,0:T(8,128)(2,1)}, bf16[2,128,768]{2,1,0:T(8,128)(2,1)}, u32[]{:S(2)}, u32[]{:S(2)}) collective-permute-start(bf16[2,128,768]{2,1,0:T(8,128)(2,1)} %get-tuple-element.41), channel_id=1, source_target_pairs={{0,1},{1,2},{2,3},{3,0},{4,5},{5,6},{6,7},{7,4},{8,9},{9,10},{10,1... | collective-permute-start | bytes 1179656 | tf_op jit(solution)/shard_map/ppermute | solution.py:281
  81.7 27.6 %collective-permute-start.25 = (bf16[1,128,512]{2,1,0:T(8,128)(2,1)}, bf16[1,128,512]{2,1,0:T(8,128)(2,1)}, u32[]{:S(2)}, u32[]{:S(2)}) collective-permute-start(bf16[1,128,512]{2,1,0:T(8,128)(2,1)} %copy-done.10), channel_id=1, source_target_pairs={{0,1},{1,2},{2,3},{3,0},{4,5},{5,6},{6,7},{7,4},{8,9},{9,10},{10,1... | collective-permute-start | bytes 393224 | tf_op jit(solution)/shard_map/ppermute | solution.py:281
  82.4 1.0 copy-start.5
  86.5 56.6 %collective-permute-start.12 = (bf16[2,2,128,768]{3,2,1,0:T(8,128)(2,1)}, bf16[2,2,128,768]{3,2,1,0:T(8,128)(2,1)}, u32[]{:S(2)}, u32[]{:S(2)}) collective-permute-start(bf16[2,2,128,768]{3,2,1,0:T(8,128)(2,1)} %get-tuple-element.49.hi), channel_id=1, source_target_pairs={{0,4},{1,5},{2,6},{3,7},{4,8},{5,9},{6,10},{7,11},{8,12},{9,13},{1... | collective-permute-start | bytes 2359304 | tf_op jit(solution)/shard_map/ppermute | solution.py:281
  89.9 6.4 %copy-start.9 = (bf16[1,128,768]{2,1,0:T(8,128)(2,1)}, bf16[1,128,768]{2,1,0:T(8,128)(2,1)S(1)}, u32[]{:S(2)}) copy-start(bf16[1,128,768]{2,1,0:T(8,128)(2,1)S(1)} %collective-permute-done.2) | copy-start | bytes 589828
  89.9 56.8 %collective-permute-start.13 = (bf16[2,2,128,768]{3,2,1,0:T(8,128)(2,1)}, bf16[2,2,128,768]{3,2,1,0:T(8,128)(2,1)}, u32[]{:S(2)}, u32[]{:S(2)}) collective-permute-start(bf16[2,2,128,768]{3,2,1,0:T(8,128)(2,1)} %get-tuple-element.50.lo), channel_id=1, source_target_pairs={{4,0},{5,1},{6,2},{7,3},{8,4},{9,5},{10,6},{11,7},{12,8},{13,9},{1... | collective-permute-start | bytes 2359304 | tf_op jit(solution)/shard_map/ppermute | solution.py:281
  96.3 18.1 %collective-permute-start.3 = (bf16[1,128,768]{2,1,0:T(8,128)(2,1)}, bf16[1,128,768]{2,1,0:T(8,128)(2,1)S(1)}, u32[]{:S(2)}, u32[]{:S(2)}) collective-permute-start(bf16[1,128,768]{2,1,0:T(8,128)(2,1)} %copy-done.9), channel_id=1, source_target_pairs={{0,1},{1,2},{2,3},{3,0},{4,5},{5,6},{6,7},{7,4},{8,9},{9,10},{10,1... | collective-permute-start | bytes 589832 | tf_op jit(solution)/shard_map/ppermute | solution.py:281
  109.3 8.0 %collective-permute-start.5 = (bf16[1,128,768]{2,1,0:T(8,128)(2,1)}, bf16[1,128,768]{2,1,0:T(8,128)(2,1)}, u32[]{:S(2)}, u32[]{:S(2)}) collective-permute-start(bf16[1,128,768]{2,1,0:T(8,128)(2,1)} %collective-permute-done.4), channel_id=1, source_target_pairs={{0,3},{1,0},{2,1},{3,2},{4,7},{5,4},{6,5},{7,6},{8,11},{9,8},{10,9... | collective-permute-start | bytes 589832 | tf_op jit(solution)/shard_map/ppermute | solution.py:281
  111.4 1.0 copy-start.6
  114.4 0.7 copy-start.7
  115.1 27.4 %collective-permute-start.1 = (bf16[2,128,768]{2,1,0:T(8,128)(2,1)}, bf16[2,128,768]{2,1,0:T(8,128)(2,1)S(1)}, u32[]{:S(2)}, u32[]{:S(2)}) collective-permute-start(bf16[2,128,768]{2,1,0:T(8,128)(2,1)} %get-tuple-element.42), channel_id=1, source_target_pairs={{0,3},{1,0},{2,1},{3,2},{4,7},{5,4},{6,5},{7,6},{8,11},{9,8},{10,9... | collective-permute-start | bytes 1179656 | tf_op jit(solution)/shard_map/ppermute | solution.py:281
  117.3 55.3 %collective-permute-start.28 = (bf16[2,2,128,512]{3,2,1,0:T(8,128)(2,1)}, bf16[2,2,128,512]{3,2,1,0:T(8,128)(2,1)S(1)}, u32[]{:S(2)}, u32[]{:S(2)}) collective-permute-start(bf16[2,2,128,512]{3,2,1,0:T(8,128)(2,1)} %get-tuple-element.66.hi), channel_id=1, source_target_pairs={{0,4},{1,5},{2,6},{3,7},{4,8},{5,9},{6,10},{7,11},{8,12},{9,13},{1... | collective-permute-start | bytes 1572872 | tf_op jit(solution)/shard_map/ppermute | solution.py:281
  120.7 51.9 %collective-permute-start.29 = (bf16[2,2,128,512]{3,2,1,0:T(8,128)(2,1)}, bf16[2,2,128,512]{3,2,1,0:T(8,128)(2,1)}, u32[]{:S(2)}, u32[]{:S(2)}) collective-permute-start(bf16[2,2,128,512]{3,2,1,0:T(8,128)(2,1)} %get-tuple-element.67.lo), channel_id=1, source_target_pairs={{4,0},{5,1},{6,2},{7,3},{8,4},{9,5},{10,6},{11,7},{12,8},{13,9},{1... | collective-permute-start | bytes 1572872 | tf_op jit(solution)/shard_map/ppermute | solution.py:281
  135.3 11.6 %copy-start = (bf16[128,5120]{1,0:T(8,128)(2,1)S(1)}, bf16[128,5120]{1,0:T(8,128)(2,1)}, u32[]{:S(2)}) copy-start(bf16[128,5120]{1,0:T(8,128)(2,1)} %q0.3) | copy-start | bytes 3932164
  135.3 11.6 %copy-start.1 = (bf16[128,5120]{1,0:T(8,128)(2,1)S(1)}, bf16[128,5120]{1,0:T(8,128)(2,1)}, u32[]{:S(2)}) copy-start(bf16[128,5120]{1,0:T(8,128)(2,1)} %g0.3) | copy-start | bytes 3932164
  142.5 22.7 %collective-permute-start.22 = (bf16[2,128,512]{2,1,0:T(8,128)(2,1)}, bf16[2,128,512]{2,1,0:T(8,128)(2,1)S(1)}, u32[]{:S(2)}, u32[]{:S(2)}) collective-permute-start(bf16[2,128,512]{2,1,0:T(8,128)(2,1)} %get-tuple-element.62), channel_id=1, source_target_pairs={{0,1},{1,2},{2,3},{3,0},{4,5},{5,6},{6,7},{7,4},{8,9},{9,10},{10,1... | collective-permute-start | bytes 786440 | tf_op jit(solution)/shard_map/ppermute | solution.py:281
  143.1 29.5 %collective-permute-start.23 = (bf16[2,128,512]{2,1,0:T(8,128)(2,1)}, bf16[2,128,512]{2,1,0:T(8,128)(2,1)S(1)}, u32[]{:S(2)}, u32[]{:S(2)}) collective-permute-start(bf16[2,128,512]{2,1,0:T(8,128)(2,1)} %get-tuple-element.63), channel_id=1, source_target_pairs={{0,3},{1,0},{2,1},{3,2},{4,7},{5,4},{6,5},{7,6},{8,11},{9,8},{10,9... | collective-permute-start | bytes 786440 | tf_op jit(solution)/shard_map/ppermute | solution.py:281
  146.7 16.1 %collective-permute-start.27 = (bf16[1,128,512]{2,1,0:T(8,128)(2,1)}, bf16[1,128,512]{2,1,0:T(8,128)(2,1)S(1)}, u32[]{:S(2)}, u32[]{:S(2)}) collective-permute-start(bf16[1,128,512]{2,1,0:T(8,128)(2,1)} %collective-permute-done.26), channel_id=1, source_target_pairs={{0,3},{1,0},{2,1},{3,2},{4,7},{5,4},{6,5},{7,6},{8,11},{9,8},{10,9... | collective-permute-start | bytes 393224 | tf_op jit(solution)/shard_map/ppermute | solution.py:281
  146.9 0.9 copy-start.8
  162.8 103.8 %collective-permute-start.17 = (bf16[2,2,128,768]{3,2,1,0:T(8,128)(2,1)S(1)}, bf16[2,2,128,768]{3,2,1,0:T(8,128)(2,1)S(1)}, u32[]{:S(2)}, u32[]{:S(2)}) collective-permute-start(bf16[2,2,128,768]{3,2,1,0:T(8,128)(2,1)S(1)} %get-tuple-element.56), channel_id=1, source_target_pairs={{0,4},{1,5},{2,6},{3,7},{4,8},{5,9},{6,10},{7,11},{8,12},{9,13},{1... | collective-permute-start | bytes 2359304 | tf_op jit(solution)/shard_map/ppermute | solution.py:281
  165.1 103.2 %collective-permute-start.18 = (bf16[2,2,128,768]{3,2,1,0:T(8,128)(2,1)S(1)}, bf16[2,2,128,768]{3,2,1,0:T(8,128)(2,1)S(1)}, u32[]{:S(2)}, u32[]{:S(2)}) collective-permute-start(bf16[2,2,128,768]{3,2,1,0:T(8,128)(2,1)S(1)} %get-tuple-element.57), channel_id=1, source_target_pairs={{4,0},{5,1},{6,2},{7,3},{8,4},{9,5},{10,6},{11,7},{12,8},{13,9},{1... | collective-permute-start | bytes 2359304 | tf_op jit(solution)/shard_map/ppermute | solution.py:281
  183.1 69.7 %collective-permute-start.33 = (bf16[2,2,128,512]{3,2,1,0:T(8,128)(2,1)S(1)}, bf16[2,2,128,512]{3,2,1,0:T(8,128)(2,1)S(1)}, u32[]{:S(2)}, u32[]{:S(2)}) collective-permute-start(bf16[2,2,128,512]{3,2,1,0:T(8,128)(2,1)S(1)} %get-tuple-element.73), channel_id=1, source_target_pairs={{0,4},{1,5},{2,6},{3,7},{4,8},{5,9},{6,10},{7,11},{8,12},{9,13},{1... | collective-permute-start | bytes 1572872 | tf_op jit(solution)/shard_map/ppermute | solution.py:281
  185.1 70.1 %collective-permute-start.34 = (bf16[2,2,128,512]{3,2,1,0:T(8,128)(2,1)S(1)}, bf16[2,2,128,512]{3,2,1,0:T(8,128)(2,1)S(1)}, u32[]{:S(2)}, u32[]{:S(2)}) collective-permute-start(bf16[2,2,128,512]{3,2,1,0:T(8,128)(2,1)S(1)} %get-tuple-element.74), channel_id=1, source_target_pairs={{4,0},{5,1},{6,2},{7,3},{8,4},{9,5},{10,6},{11,7},{12,8},{13,9},{1... | collective-permute-start | bytes 1572872 | tf_op jit(solution)/shard_map/ppermute | solution.py:281
  192.9 58.1 %collective-permute-start.30 = (bf16[128,512]{1,0:T(8,128)(2,1)S(1)}, bf16[128,512]{1,0:T(8,128)(2,1)S(1)}, u32[]{:S(2)}, u32[]{:S(2)}) collective-permute-start(bf16[128,512]{1,0:T(8,128)(2,1)S(1)} %get-tuple-element.69), channel_id=1, source_target_pairs={{0,1},{1,2},{2,3},{3,0},{4,5},{5,6},{6,7},{7,4},{8,9},{9,10},{10,1... | collective-permute-start | bytes 393224 | tf_op jit(solution)/shard_map/ppermute | solution.py:281
  251.0 10.4 %collective-permute-start.31 = (bf16[128,512]{1,0:T(8,128)(2,1)S(1)}, bf16[128,512]{1,0:T(8,128)(2,1)S(1)}, u32[]{:S(2)}, u32[]{:S(2)}) collective-permute-start(bf16[128,512]{1,0:T(8,128)(2,1)S(1)} %get-tuple-element.70), channel_id=1, source_target_pairs={{0,2},{1,3},{2,0},{3,1},{4,6},{5,7},{6,4},{7,5},{8,10},{9,11},{10,... | collective-permute-start | bytes 393224 | tf_op jit(solution)/shard_map/ppermute | solution.py:281
  252.8 25.2 %collective-permute-start.14 = (bf16[128,768]{1,0:T(8,128)(2,1)S(1)}, bf16[128,768]{1,0:T(8,128)(2,1)S(1)}, u32[]{:S(2)}, u32[]{:S(2)}) collective-permute-start(bf16[128,768]{1,0:T(8,128)(2,1)S(1)} %get-tuple-element.52), channel_id=1, source_target_pairs={{0,1},{1,2},{2,3},{3,0},{4,5},{5,6},{6,7},{7,4},{8,9},{9,10},{10,1... | collective-permute-start | bytes 589832 | tf_op jit(solution)/shard_map/ppermute | solution.py:281
  255.1 25.3 %collective-permute-start.15 = (bf16[128,768]{1,0:T(8,128)(2,1)S(1)}, bf16[128,768]{1,0:T(8,128)(2,1)S(1)}, u32[]{:S(2)}, u32[]{:S(2)}) collective-permute-start(bf16[128,768]{1,0:T(8,128)(2,1)S(1)} %get-tuple-element.53), channel_id=1, source_target_pairs={{0,2},{1,3},{2,0},{3,1},{4,6},{5,7},{6,4},{7,5},{8,10},{9,11},{10,... | collective-permute-start | bytes 589832 | tf_op jit(solution)/shard_map/ppermute | solution.py:281
  261.4 12.9 %collective-permute-start.32 = (bf16[128,512]{1,0:T(8,128)(2,1)S(1)}, bf16[128,512]{1,0:T(8,128)(2,1)S(1)}, u32[]{:S(2)}, u32[]{:S(2)}) collective-permute-start(bf16[128,512]{1,0:T(8,128)(2,1)S(1)} %get-tuple-element.71), channel_id=1, source_target_pairs={{0,3},{1,0},{2,1},{3,2},{4,7},{5,4},{6,5},{7,6},{8,11},{9,8},{10,9... | collective-permute-start | bytes 393224 | tf_op jit(solution)/shard_map/ppermute | solution.py:281
  266.6 17.8 %collective-permute-start.35 = (bf16[2,128,512]{2,1,0:T(8,128)(2,1)S(1)}, bf16[2,128,512]{2,1,0:T(8,128)(2,1)S(1)}, u32[]{:S(2)}, u32[]{:S(2)}) collective-permute-start(bf16[2,128,512]{2,1,0:T(8,128)(2,1)S(1)} %get-tuple-element.76), channel_id=1, source_target_pairs={{0,1},{1,2},{2,3},{3,0},{4,5},{5,6},{6,7},{7,4},{8,9},{9,10},{10,1... | collective-permute-start | bytes 786440 | tf_op jit(solution)/shard_map/ppermute | solution.py:281
  268.3 13.4 %collective-permute-start.16 = (bf16[128,768]{1,0:T(8,128)(2,1)S(1)}, bf16[128,768]{1,0:T(8,128)(2,1)S(1)}, u32[]{:S(2)}, u32[]{:S(2)}) collective-permute-start(bf16[128,768]{1,0:T(8,128)(2,1)S(1)} %get-tuple-element.54), channel_id=1, source_target_pairs={{0,3},{1,0},{2,1},{3,2},{4,7},{5,4},{6,5},{7,6},{8,11},{9,8},{10,9... | collective-permute-start | bytes 589832 | tf_op jit(solution)/shard_map/ppermute | solution.py:281
  274.4 34.9 %collective-permute-start.19 = (bf16[2,128,768]{2,1,0:T(8,128)(2,1)S(1)}, bf16[2,128,768]{2,1,0:T(8,128)(2,1)S(1)}, u32[]{:S(2)}, u32[]{:S(2)}) collective-permute-start(bf16[2,128,768]{2,1,0:T(8,128)(2,1)S(1)} %get-tuple-element.59), channel_id=1, source_target_pairs={{0,1},{1,2},{2,3},{3,0},{4,5},{5,6},{6,7},{7,4},{8,9},{9,10},{10,1... | collective-permute-start | bytes 1179656 | tf_op jit(solution)/shard_map/ppermute | solution.py:281
  278.0 31.3 %collective-permute-start.20 = (bf16[2,128,768]{2,1,0:T(8,128)(2,1)S(1)}, bf16[2,128,768]{2,1,0:T(8,128)(2,1)S(1)}, u32[]{:S(2)}, u32[]{:S(2)}) collective-permute-start(bf16[2,128,768]{2,1,0:T(8,128)(2,1)S(1)} %get-tuple-element.60), channel_id=1, source_target_pairs={{0,2},{1,3},{2,0},{3,1},{4,6},{5,7},{6,4},{7,5},{8,10},{9,11},{10,... | collective-permute-start | bytes 1179656 | tf_op jit(solution)/shard_map/ppermute | solution.py:281
  280.4 28.8 %collective-permute-start.21 = (bf16[2,128,768]{2,1,0:T(8,128)(2,1)S(1)}, bf16[2,128,768]{2,1,0:T(8,128)(2,1)S(1)}, u32[]{:S(2)}, u32[]{:S(2)}) collective-permute-start(bf16[2,128,768]{2,1,0:T(8,128)(2,1)S(1)} %get-tuple-element.61), channel_id=1, source_target_pairs={{0,3},{1,0},{2,1},{3,2},{4,7},{5,4},{6,5},{7,6},{8,11},{9,8},{10,9... | collective-permute-start | bytes 1179656 | tf_op jit(solution)/shard_map/ppermute | solution.py:281
  281.7 23.6 %collective-permute-start.36 = (bf16[2,128,512]{2,1,0:T(8,128)(2,1)S(1)}, bf16[2,128,512]{2,1,0:T(8,128)(2,1)S(1)}, u32[]{:S(2)}, u32[]{:S(2)}) collective-permute-start(bf16[2,128,512]{2,1,0:T(8,128)(2,1)S(1)} %get-tuple-element.77), channel_id=1, source_target_pairs={{0,2},{1,3},{2,0},{3,1},{4,6},{5,7},{6,4},{7,5},{8,10},{9,11},{10,... | collective-permute-start | bytes 786440 | tf_op jit(solution)/shard_map/ppermute | solution.py:281
  284.4 24.8 %collective-permute-start.37 = (bf16[2,128,512]{2,1,0:T(8,128)(2,1)S(1)}, bf16[2,128,512]{2,1,0:T(8,128)(2,1)S(1)}, u32[]{:S(2)}, u32[]{:S(2)}) collective-permute-start(bf16[2,128,512]{2,1,0:T(8,128)(2,1)S(1)} %get-tuple-element.78), channel_id=1, source_target_pairs={{0,3},{1,0},{2,1},{3,2},{4,7},{5,4},{6,5},{7,6},{8,11},{9,8},{10,9... | collective-permute-start | bytes 786440 | tf_op jit(solution)/shard_map/ppermute | solution.py:281
  (1 other events, 0.7 us)

commit v5 on v4

--- a/solution.py
+++ b/solution.py
@@ -1,3 +1,4 @@
+import functools
 import math
 
 import jax
@@ -11,7 +12,7 @@
 BLK = 128
 HD = 128
 NZ = 4
-CHUNKS = ((0, 6), (6, 4))
+CHUNKS = ((0, 4), (4, 6))
 CW = 256
 SCALE = 1.0 / math.sqrt(HD)
 EXP2_SCALE = SCALE / math.log(2.0)
@@ -28,6 +29,33 @@
 
 def cost(flops, nbytes):
     return pl.CostEstimate(flops=flops, bytes_accessed=nbytes, transcendentals=0)
+
+
+def pack_direct_body(zh, a1, a2, a3, b1, b2, b3, o1, o2, o3):
+    for a, b, o in ((a1, b1, o1), (a2, b2, o2), (a3, b3, o3)):
+        o[0] = a[...]
+        o[1] = b[...]
+
+
+def pack_direct(zh, a, b, first, heads, group):
+    per, off, steps = group * HD // CW, first * HD // CW, heads * HD // CW
+
+    def src(s):
+        return pl.BlockSpec((BLK, CW), lambda i, z: (0, lax.rem(z[0] + s, NZ) * per + off + i))
+
+    out = pl.BlockSpec((2, BLK, CW), lambda i, z: (0, 0, i))
+    return pl.pallas_call(
+        pack_direct_body,
+        grid_spec=pltpu.PrefetchScalarGridSpec(
+            num_scalar_prefetch=1,
+            grid=(steps,),
+            in_specs=[src(1), src(2), src(3)] * 2,
+            out_specs=[out] * 3,
+        ),
+        out_shape=[jax.ShapeDtypeStruct((2, BLK, heads * HD), BF)] * 3,
+        cost_estimate=cost(0, 12 * BLK * heads * HD * 2),
+        compiler_params=grant(56),
+    )(zh, a, a, a, b, b, b)
 
 
 def pack_body(zh, *refs):
@@ -60,45 +88,68 @@
     )(zh, *[a for a, _ in (*plus, *minus)])
 
 
-def unpack_body(zh, k, v, mp, mm, fp, fm, lo, hi):
+def unpack_body(zh, k, v, mp, mm, fp, fm, *halves):
+    z, step = zh[0], pl.program_id(0)
+    parts = ((k, v), (mp.at[0], mp.at[1]), (fp.at[0], fm.at[0]), (mm.at[0], mm.at[1]))
+    for c, (first, heads) in enumerate(CHUNKS):
+        lo, hi = halves[2 * c : 2 * c + 2]
+
+        @pl.when((step >= first * HD // CW) & (step < (first + heads) * HD // CW))
+        def _():
+            for s, (kk, vv) in enumerate(parts):
+                b = lax.rem(z + NZ - s, NZ)
+
+                @pl.when(b < 2)
+                def _():
+                    lo[b, 0] = kk[...]
+                    lo[b, 1] = vv[...]
+
+                @pl.when(b >= 2)
+                def _():
+                    hi[b - 2, 0] = kk[...]
+                    hi[b - 2, 1] = vv[...]
+
+
+def unpack(zh, k, v, recv, group):
+    per = group * HD // CW
+    own = pl.BlockSpec((BLK, CW), lambda i, z: (0, z[0] * per + i))
+    two = pl.BlockSpec((2, BLK, CW), lambda i, z: (0, 0, i))
+    one = pl.BlockSpec((1, BLK, CW), lambda i, z: (0, 0, i))
+    specs, shapes = [], []
+    for first, heads in CHUNKS:
+        lo, n = first * HD // CW, heads * HD // CW
+        half = pl.BlockSpec(
+            (2, 2, BLK, CW), lambda i, z, lo=lo, n=n: (0, 0, 0, jnp.minimum(jnp.maximum(i - lo, 0), n - 1))
+        )
+        specs += [half, half]
+        shapes += [jax.ShapeDtypeStruct((2, 2, BLK, heads * HD), BF)] * 2
+    return pl.pallas_call(
+        unpack_body,
+        grid_spec=pltpu.PrefetchScalarGridSpec(
+            num_scalar_prefetch=1, grid=(per,), in_specs=[own, own, two, two, one, one], out_specs=specs
+        ),
+        out_shape=shapes,
+        cost_estimate=cost(0, 16 * BLK * group * HD * 2),
+        compiler_params=grant(12),
+        name="unpack",
+    )(zh, k, v, *recv)
+
+
+def attend_body(direct, zh, q0, g0, *refs):
+    n = 3 if direct else 4
+    got, refs = refs[:n], refs[n:]
+    before, lo, hi, after, bias, *refs = refs
+    if direct:
+        one, two, three = ((r.at[0], r.at[1]) for r in got)
+    else:
+        mp, mm, fp, fm = got
+        one, two, three = (mp.at[0], mp.at[1]), (fp.at[0], fm.at[0]), (mm.at[0], mm.at[1])
+    (
+        dq0, dq1, dq2, dq3, rim_before, rim_after, own,
+        qs, gs, ks, vs, dqs, dk, dv,
+    ) = refs
     z = zh[0]
-    for s, (kk, vv) in enumerate(((k, v), (mp.at[0], mp.at[1]), (fp.at[0], fm.at[0]), (mm.at[0], mm.at[1]))):
-        b = lax.rem(z + NZ - s, NZ)
-
-        @pl.when(b < 2)
-        def _():
-            lo[b, 0] = kk[...]
-            lo[b, 1] = vv[...]
-
-        @pl.when(b >= 2)
-        def _():
-            hi[b - 2, 0] = kk[...]
-            hi[b - 2, 1] = vv[...]
-
-
-def unpack(zh, k, v, recv, first, heads, group):
-    n = heads * HD
-    per, off = group * HD // CW, first * HD // CW
-    own = pl.BlockSpec((BLK, CW), lambda i, z: (0, z[0] * per + off + i))
-    two = pl.BlockSpec((2, BLK, CW), lambda i, z: (0, 0, off + i))
-    one = pl.BlockSpec((1, BLK, CW), lambda i, z: (0, 0, off + i))
-    half = pl.BlockSpec((2, 2, BLK, CW), lambda i, z: (0, 0, 0, i))
-    return pl.pallas_call(
-        unpack_body,
-        grid_spec=pltpu.PrefetchScalarGridSpec(
-            num_scalar_prefetch=1, grid=(n // CW,), in_specs=[own, own, two, two, one, one], out_specs=[half, half]
-        ),
-        out_shape=[jax.ShapeDtypeStruct((2, 2, BLK, n), BF)] * 2,
-        cost_estimate=cost(0, 16 * BLK * n * 2),
-        compiler_params=grant(8),
-    )(zh, k, v, *recv)
-
-
-def attend_body(zh, q0, g0, mp, mm, fp, fm, before, lo, hi, after, bias,
-                dq0, dq1, dq2, dq3, rim_before, rim_after, own,
-                qs, gs, ks, vs, dqs, dk, dv):
-    z = zh[0]
-    for s, (qq, gg) in enumerate(((q0, g0), (mp.at[0], mp.at[1]), (fp.at[0], fm.at[0]), (mm.at[0], mm.at[1]))):
+    for s, (qq, gg) in enumerate(((q0, g0), one, two, three)):
         row = pl.multiple_of(lax.rem(z + NZ - s, NZ) * BLK, BLK)
         qs[pl.ds(row, BLK), :] = qq[...]
         gs[pl.ds(row, BLK), :] = gg[...]
@@ -154,16 +205,18 @@
     mine = pl.BlockSpec((BLK, HD), lambda h, z: (0, z[0] * group + first + h))
     two = pl.BlockSpec((2, BLK, HD), lambda h, z: (0, 0, h))
     one = pl.BlockSpec((1, BLK, HD), lambda h, z: (0, 0, h))
+    direct = len(recv) == 3
+    got = [two] * 3 if direct else [two, two, one, one]
     flat = pl.BlockSpec((BLK, HD), lambda h, z: (0, h))
     rim = pl.BlockSpec((2, 2, BLK, HD), lambda h, z: (0, 0, 0, h))
     own = pl.BlockSpec((4, 2, BLK, HD), lambda h, z: (0, 0, 0, h))
     shape = jax.ShapeDtypeStruct
     return pl.pallas_call(
-        attend_body,
+        functools.partial(attend_body, direct),
         grid_spec=pltpu.PrefetchScalarGridSpec(
             num_scalar_prefetch=1,
             grid=(heads,),
-            in_specs=[mine, mine, two, two, one, one, rim, rim, rim, rim,
+            in_specs=[mine, mine, *got, rim, rim, rim, rim,
                       pl.BlockSpec((1, 2, 6, 2 * BLK), lambda h, z: (first + h, 0, 0, 0))],
             out_specs=[flat] * 4 + [rim, rim, own],
             scratch_shapes=[
@@ -289,6 +342,7 @@
     def to_prev(a):
         return move(("ctx", "uly"), down, a)
 
+    key, value, query, dout = (pltpu.with_memory_space_constraint(a, pltpu.HBM) for a in (key, value, query, dout))
     bias = tile_bias(tile_mask, zh_s, slab, group)
 
     def gather(a, b, first, heads, wide):
@@ -300,11 +354,12 @@
         return mp, mm, fp, fm
 
     kv = gather(key, value, 0, group, group * HD // 2)
-    qg = [gather(query, dout, first, heads, CW) for first, heads in CHUNKS]
+    qg = [gather(query, dout, *CHUNKS[0], CW), around(pack_direct(zh, query, dout, *CHUNKS[1], group))]
+    halves = unpack(zh, key, value, kv, group)
     parts = []
     for c, (first, heads) in enumerate(CHUNKS):
         recv = qg[c]
-        lo, hi = unpack(zh, key, value, kv, first, heads, group)
+        lo, hi = halves[2 * c : 2 * c + 2]
         before, after = to_next(hi), to_prev(lo)
         *dq, rim_before, rim_after, own = attend(
             zh, query, dout, recv, before, lo, hi, after, bias, first, heads, group

time: 313 us -> 305 us (0.974)
  the two profiles are of different devices: /device:TPU:32 before, /device:TPU:90 now
where the time goes in v5:
time: 305 us; the launch traced here: 304 us
  waiting for transfers between devices  167 us (55%)
  starting transfers between devices  82.6 us (27%)
  Pallas kernels  43.5 us (14%)
  local copies, waits for them, and re-layouts  8.81 us (3%)
    ppermute x35, waiting for transfers between devices, move(): return lax.ppermute(a, axes, perm)  167 us
    ppermute x35, starting transfers between devices, move(): return lax.ppermute(a, axes, perm)  82.6 us
    pallas_call x2, Pallas kernels, attend(): pl.pallas_call(functools.partial(attend_body, direct), grid_spec=pltpu.Pr...  25.5 us
    pallas_call x4, Pallas kernels, pack(): pl.pallas_call(pack_body, grid_spec=pltpu.PrefetchScalarGridSpec(num_scal...  7.7 us
  transfers between devices with their start and end apart: 35, of which 9 were waited for; matrix products, arithmetic and copies ran while one was open for 2% of the time, Pallas kernels for 13%

profile of v5, /device:TPU:90, one launch (start us, length us, event | category | flops | bytes accessed | tf_op | source)
XLA Modules:
  0.0 304.1 jit_solution(5676606615096628530)
XLA Ops:
  0.6 2.3 shard_map.78
  3.0 4.5 %collective-permute-start.6 = (bf16[2,128,1280]{2,1,0:T(8,128)(2,1)}, bf16[2,128,1280]{2,1,0:T(8,128)(2,1)S(1)}, u32[]{:S(2)}, u32[]{:S(2)}) collective-permute-start(bf16[2,128,1280]{2,1,0:T(8,128)(2,1)} %get-tuple-element.44), channel_id=1, source_target_pairs={{0,1},{1,2},{2,3},{3,0},{4,5},{5,6},{6,7},{7,4},{8,9},{9,10},{10,1... | collective-permute-start | bytes 1966088 | tf_op jit(solution)/shard_map/ppermute | solution.py:334
  7.5 1.9 shard_map.79
  9.4 1.5 collective-permute-start.10
  10.9 2.6 collective-permute-start.8
  13.5 40.5 %collective-permute-done.10 = bf16[1,128,1280]{2,1,0:T(8,128)(2,1)S(1)} collective-permute-done((bf16[1,128,1280]{2,1,0:T(8,128)(2,1)}, bf16[1,128,1280]{2,1,0:T(8,128)(2,1)S(1)}, u32[]{:S(2)}, u32[]{:S(2)}) %collective-permute-start.10) | collective-permute-done | bytes 327712 | tf_op jit(solution)/shard_map/ppermute | solution.py:334
  54.1 4.1 %collective-permute-start.9 = (bf16[1,128,1280]{2,1,0:T(8,128)(2,1)S(1)}, bf16[1,128,1280]{2,1,0:T(8,128)(2,1)S(1)}, u32[]{:S(2)}, u32[]{:S(2)}) collective-permute-start(bf16[1,128,1280]{2,1,0:T(8,128)(2,1)S(1)} %collective-permute-done.8), channel_id=1, source_target_pairs={{0,1},{1,2},{2,3},{3,0},{4,5},{5,6},{6,7},{7,4},{8,9},{9,10},{10,1... | collective-permute-start | bytes 983048 | tf_op jit(solution)/shard_map/ppermute | solution.py:334
  58.2 1.6 shard_map.77
  59.8 2.9 collective-permute-start.4
  62.7 3.1 %shard_map.82 = (bf16[2,128,768]{2,1,0:T(8,128)(2,1)}, bf16[2,128,768]{2,1,0:T(8,128)(2,1)}, bf16[2,128,768]{2,1,0:T(8,128)(2,1)}) custom-call(s32[1]{0:T(128)} %bitcast.zh, bf16[128,5120]{1,0:T(8,128)(2,1)} %q0.3, bf16[128,5120]{1,0:T(8,128)(2,1)} %q0.3, bf16[128,5120]{1,0:T(8,128)(2,1)} %q0.3, bf16[128,5120]{1,0:T(8,128)(2,1)} %g0.3, ...), custom_call_target="tpu_custom_call" | custom-call | bytes 2359296 | tf_op jit(solution)/shard_map/pallas_call | solution.py:47
  65.9 1.8 shard_map.76
  67.7 1.4 collective-permute-start.22
  69.1 2.9 collective-permute-done.11.fm
  72.0 1.5 collective-permute-start.23
  74.1 2.7 collective-permute-start
  76.8 3.2 %unpack.1 = (bf16[2,2,128,512]{3,2,1,0:T(8,128)(2,1)S(1)}, bf16[2,2,128,512]{3,2,1,0:T(8,128)(2,1)S(1)}, bf16[2,2,128,768]{3,2,1,0:T(8,128)(2,1)S(1)}, bf16[2,2,128,768]{3,2,1,0:T(8,128)(2,1)S(1)}) custom-call(s32[1]{0:T(128)} %bitcast.zh, bf16[128,5120]{1,0:T(8,128)(2,1)} %k.1, bf16[128,5120]{1,0:T(8,128)(2,1)} %v.1, ...), custom_call_target="tpu_custom_call" | custom-call | bytes 5242880 | tf_op jit(solution)/shard_map/unpack/pallas_call | solution.py:126
  81.6 3.4 %collective-permute-start.25 = (bf16[2,2,128,768]{3,2,1,0:T(8,128)(2,1)S(1)}, bf16[2,2,128,768]{3,2,1,0:T(8,128)(2,1)S(1)}, u32[]{:S(2)}, u32[]{:S(2)}) collective-permute-start(bf16[2,2,128,768]{3,2,1,0:T(8,128)(2,1)S(1)} %get-tuple-element.64.refs_5_), channel_id=1, source_target_pairs={{0,4},{1,5},{2,6},{3,7},{4,8},{5,9},{6,10},{7,11},{8,12},{9,13},{1... | collective-permute-start | bytes 2359304 | tf_op jit(solution)/shard_map/ppermute | solution.py:334
  85.0 2.4 collective-permute-start.26
  88.6 31.7 %collective-permute-done.refs_0_ = bf16[2,128,512]{2,1,0:T(8,128)(2,1)} collective-permute-done((bf16[2,128,512]{2,1,0:T(8,128)(2,1)}, bf16[2,128,512]{2,1,0:T(8,128)(2,1)}, u32[]{:S(2)}, u32[]{:S(2)}) %collective-permute-start) | collective-permute-done | bytes 262176 | tf_op jit(solution)/shard_map/ppermute | solution.py:334
  120.3 1.2 collective-permute-start.24
  121.5 3.4 %collective-permute-start.12 = (bf16[2,2,128,512]{3,2,1,0:T(8,128)(2,1)}, bf16[2,2,128,512]{3,2,1,0:T(8,128)(2,1)}, u32[]{:S(2)}, u32[]{:S(2)}) collective-permute-start(bf16[2,2,128,512]{3,2,1,0:T(8,128)(2,1)} %copy-done.4), channel_id=1, source_target_pairs={{0,4},{1,5},{2,6},{3,7},{4,8},{5,9},{6,10},{7,11},{8,12},{9,13},{1... | collective-permute-start | bytes 1572872 | tf_op jit(solution)/shard_map/ppermute | solution.py:334
  124.9 2.4 collective-permute-start.13
  128.2 1.7 broadcast_in_dim.17
  129.8 1.7 reshape.61
  132.4 5.4 %collective-permute-done.24.refs_2_ = bf16[2,128,768]{2,1,0:T(8,128)(2,1)S(1)} collective-permute-done((bf16[2,128,768]{2,1,0:T(8,128)(2,1)}, bf16[2,128,768]{2,1,0:T(8,128)(2,1)S(1)}, u32[]{:S(2)}, u32[]{:S(2)}) %collective-permute-start.24) | collective-permute-done | bytes 393248 | tf_op jit(solution)/shard_map/ppermute | solution.py:334
  137.8 4.1 %collective-permute-start.3 = (bf16[1,128,512]{2,1,0:T(8,128)(2,1)}, bf16[1,128,512]{2,1,0:T(8,128)(2,1)S(1)}, u32[]{:S(2)}, u32[]{:S(2)}) collective-permute-start(bf16[1,128,512]{2,1,0:T(8,128)(2,1)} %collective-permute-done.2), channel_id=1, source_target_pairs={{0,1},{1,2},{2,3},{3,0},{4,5},{5,6},{6,7},{7,4},{8,9},{9,10},{10,1... | collective-permute-start | bytes 393224 | tf_op jit(solution)/shard_map/ppermute | solution.py:334
  144.0 15.1 %shard_map.83 = (bf16[128,768]{1,0:T(8,128)(2,1)S(1)}, bf16[128,768]{1,0:T(8,128)(2,1)S(1)}, bf16[128,768]{1,0:T(8,128)(2,1)S(1)}, bf16[128,768]{1,0:T(8,128)(2,...) custom-call(s32[1]{0:T(128)} %bitcast.zh, ...), custom_call_target="tpu_custom_call" | custom-call | flops 3019898880 | bytes 7864320 | tf_op jit(solution)/shard_map/pallas_call | solution.py:214
  159.1 3.4 %collective-permute-start.30 = (bf16[2,2,128,768]{3,2,1,0:T(8,128)(2,1)S(1)}, bf16[2,2,128,768]{3,2,1,0:T(8,128)(2,1)S(1)}, u32[]{:S(2)}, u32[]{:S(2)}) collective-permute-start(bf16[2,2,128,768]{3,2,1,0:T(8,128)(2,1)S(1)} %get-tuple-element.71), channel_id=1, source_target_pairs={{0,4},{1,5},{2,6},{3,7},{4,8},{5,9},{6,10},{7,11},{8,12},{9,13},{1... | collective-permute-start | bytes 2359304 | tf_op jit(solution)/shard_map/ppermute | solution.py:334
  162.5 2.4 collective-permute-start.31
  165.0 10.4 %shard_map.80 = (bf16[128,512]{1,0:T(8,128)(2,1)S(1)}, bf16[128,512]{1,0:T(8,128)(2,1)S(1)}, bf16[128,512]{1,0:T(8,128)(2,1)S(1)}, bf16[128,512]{1,0:T(8,128)(2,...) custom-call(s32[1]{0:T(128)} %bitcast.zh, ...), custom_call_target="tpu_custom_call" | custom-call | flops 2013265920 | bytes 5242880 | tf_op jit(solution)/shard_map/pallas_call | solution.py:214
  175.4 3.4 %collective-permute-start.17 = (bf16[2,2,128,512]{3,2,1,0:T(8,128)(2,1)S(1)}, bf16[2,2,128,512]{3,2,1,0:T(8,128)(2,1)S(1)}, u32[]{:S(2)}, u32[]{:S(2)}) collective-permute-start(bf16[2,2,128,512]{3,2,1,0:T(8,128)(2,1)S(1)} %get-tuple-element.55), channel_id=1, source_target_pairs={{0,4},{1,5},{2,6},{3,7},{4,8},{5,9},{6,10},{7,11},{8,12},{9,13},{1... | collective-permute-start | bytes 1572872 | tf_op jit(solution)/shard_map/ppermute | solution.py:334
  178.8 3.1 %collective-permute-start.18 = (bf16[2,2,128,512]{3,2,1,0:T(8,128)(2,1)S(1)}, bf16[2,2,128,512]{3,2,1,0:T(8,128)(2,1)S(1)}, u32[]{:S(2)}, u32[]{:S(2)}) collective-permute-start(bf16[2,2,128,512]{3,2,1,0:T(8,128)(2,1)S(1)} %get-tuple-element.56), channel_id=1, source_target_pairs={{4,0},{5,1},{6,2},{7,3},{8,4},{9,5},{10,6},{11,7},{12,8},{13,9},{1... | collective-permute-start | bytes 1572872 | tf_op jit(solution)/shard_map/ppermute | solution.py:334
  181.9 3.8 %collective-permute-start.14 = (bf16[128,512]{1,0:T(8,128)(2,1)S(1)}, bf16[128,512]{1,0:T(8,128)(2,1)S(1)}, u32[]{:S(2)}, u32[]{:S(2)}) collective-permute-start(bf16[128,512]{1,0:T(8,128)(2,1)S(1)} %get-tuple-element.51), channel_id=1, source_target_pairs={{0,1},{1,2},{2,3},{3,0},{4,5},{5,6},{6,7},{7,4},{8,9},{9,10},{10,1... | collective-permute-start | bytes 393224 | tf_op jit(solution)/shard_map/ppermute | solution.py:334
  185.7 2.7 collective-permute-done.14.refs_1_
  188.4 4.3 %collective-permute-start.15 = (bf16[128,512]{1,0:T(8,128)(2,1)S(1)}, bf16[128,512]{1,0:T(8,128)(2,1)S(1)}, u32[]{:S(2)}, u32[]{:S(2)}) collective-permute-start(bf16[128,512]{1,0:T(8,128)(2,1)S(1)} %get-tuple-element.52), channel_id=1, source_target_pairs={{0,2},{1,3},{2,0},{3,1},{4,6},{5,7},{6,4},{7,5},{8,10},{9,11},{10,... | collective-permute-start | bytes 393224 | tf_op jit(solution)/shard_map/ppermute | solution.py:334
  192.7 2.8 collective-permute-start.27
  195.5 3.5 %collective-permute-start.28 = (bf16[128,768]{1,0:T(8,128)(2,1)S(1)}, bf16[128,768]{1,0:T(8,128)(2,1)S(1)}, u32[]{:S(2)}, u32[]{:S(2)}) collective-permute-start(bf16[128,768]{1,0:T(8,128)(2,1)S(1)} %get-tuple-element.68), channel_id=1, source_target_pairs={{0,2},{1,3},{2,0},{3,1},{4,6},{5,7},{6,4},{7,5},{8,10},{9,11},{10,... | collective-permute-start | bytes 589832 | tf_op jit(solution)/shard_map/ppermute | solution.py:334
  199.6 2.1 collective-permute-done.15.refs_2_
  201.6 3.9 %collective-permute-start.16 = (bf16[128,512]{1,0:T(8,128)(2,1)S(1)}, bf16[128,512]{1,0:T(8,128)(2,1)S(1)}, u32[]{:S(2)}, u32[]{:S(2)}) collective-permute-start(bf16[128,512]{1,0:T(8,128)(2,1)S(1)} %get-tuple-element.53), channel_id=1, source_target_pairs={{0,3},{1,0},{2,1},{3,2},{4,7},{5,4},{6,5},{7,6},{8,11},{9,8},{10,9... | collective-permute-start | bytes 393224 | tf_op jit(solution)/shard_map/ppermute | solution.py:334
  205.8 2.7 collective-permute-start.29
  209.5 51.0 %collective-permute-done.16.refs_3_ = bf16[128,512]{1,0:T(8,128)(2,1)S(1)} collective-permute-done((bf16[128,512]{1,0:T(8,128)(2,1)S(1)}, bf16[128,512]{1,0:T(8,128)(2,1)S(1)}, u32[]{:S(2)}, u32[]{:S(2)}) %collective-permute-start.16) | collective-permute-done | bytes 131104 | tf_op jit(solution)/shard_map/ppermute | solution.py:334
  260.4 2.9 collective-permute-start.32
  263.3 1.4 collective-permute-start.33
  264.8 1.9 collective-permute-start.34
  266.7 2.7 collective-permute-start.20
  269.4 1.9 collective-permute-start.21
  271.3 30.4 %collective-permute-done.20.refs_6_ = bf16[2,128,512]{2,1,0:T(8,128)(2,1)S(1)} collective-permute-done((bf16[2,128,512]{2,1,0:T(8,128)(2,1)S(1)}, bf16[2,128,512]{2,1,0:T(8,128)(2,1)S(1)}, u32[]{:S(2)}, u32[]{:S(2)}) %collective-permute-start.20) | collective-permute-done | bytes 262176 | tf_op jit(solution)/shard_map/ppermute | solution.py:334
  301.7 2.4 assemble.1
  (56 shorter events, 8.9 us)
Async XLA Ops:
  3.0 56.9 %collective-permute-start.6 = (bf16[2,128,1280]{2,1,0:T(8,128)(2,1)}, bf16[2,128,1280]{2,1,0:T(8,128)(2,1)S(1)}, u32[]{:S(2)}, u32[]{:S(2)}) collective-permute-start(bf16[2,128,1280]{2,1,0:T(8,128)(2,1)} %get-tuple-element.44), channel_id=1, source_target_pairs={{0,1},{1,2},{2,3},{3,0},{4,5},{5,6},{6,7},{7,4},{8,9},{9,10},{10,1... | collective-permute-start | bytes 1966088 | tf_op jit(solution)/shard_map/ppermute | solution.py:334
  7.5 60.3 %collective-permute-start.7 = (bf16[2,128,1280]{2,1,0:T(8,128)(2,1)}, bf16[2,128,1280]{2,1,0:T(8,128)(2,1)S(1)}, u32[]{:S(2)}, u32[]{:S(2)}) collective-permute-start(bf16[2,128,1280]{2,1,0:T(8,128)(2,1)} %get-tuple-element.45), channel_id=1, source_target_pairs={{0,3},{1,0},{2,1},{3,2},{4,7},{5,4},{6,5},{7,6},{8,11},{9,8},{10,9... | collective-permute-start | bytes 1966088 | tf_op jit(solution)/shard_map/ppermute | solution.py:334
  9.4 44.7 %collective-permute-start.10 = (bf16[1,128,1280]{2,1,0:T(8,128)(2,1)}, bf16[1,128,1280]{2,1,0:T(8,128)(2,1)S(1)}, u32[]{:S(2)}, u32[]{:S(2)}) collective-permute-start(bf16[1,128,1280]{2,1,0:T(8,128)(2,1)} %get-tuple-element.47), channel_id=1, source_target_pairs={{0,3},{1,0},{2,1},{3,2},{4,7},{5,4},{6,5},{7,6},{8,11},{9,8},{10,9... | collective-permute-start | bytes 983048 | tf_op jit(solution)/shard_map/ppermute | solution.py:334
  10.9 43.1 %collective-permute-start.8 = (bf16[1,128,1280]{2,1,0:T(8,128)(2,1)}, bf16[1,128,1280]{2,1,0:T(8,128)(2,1)S(1)}, u32[]{:S(2)}, u32[]{:S(2)}) collective-permute-start(bf16[1,128,1280]{2,1,0:T(8,128)(2,1)} %get-tuple-element.46), channel_id=1, source_target_pairs={{0,1},{1,2},{2,3},{3,0},{4,5},{5,6},{6,7},{7,4},{8,9},{9,10},{10,1... | collective-permute-start | bytes 983048 | tf_op jit(solution)/shard_map/ppermute | solution.py:334
  54.1 17.9 %collective-permute-start.11 = (bf16[1,128,1280]{2,1,0:T(8,128)(2,1)S(1)}, bf16[1,128,1280]{2,1,0:T(8,128)(2,1)S(1)}, u32[]{:S(2)}, u32[]{:S(2)}) collective-permute-start(bf16[1,128,1280]{2,1,0:T(8,128)(2,1)S(1)} %collective-permute-done.10), channel_id=1, source_target_pairs={{0,3},{1,0},{2,1},{3,2},{4,7},{5,4},{6,5},{7,6},{8,11},{9,8},{10,9... | collective-permute-start | bytes 983048 | tf_op jit(solution)/shard_map/ppermute | solution.py:334
  54.1 20.0 %collective-permute-start.9 = (bf16[1,128,1280]{2,1,0:T(8,128)(2,1)S(1)}, bf16[1,128,1280]{2,1,0:T(8,128)(2,1)S(1)}, u32[]{:S(2)}, u32[]{:S(2)}) collective-permute-start(bf16[1,128,1280]{2,1,0:T(8,128)(2,1)S(1)} %collective-permute-done.8), channel_id=1, source_target_pairs={{0,1},{1,2},{2,3},{3,0},{4,5},{5,6},{6,7},{7,4},{8,9},{9,10},{10,1... | collective-permute-start | bytes 983048 | tf_op jit(solution)/shard_map/ppermute | solution.py:334
  59.8 21.8 %collective-permute-start.2 = (bf16[1,128,512]{2,1,0:T(8,128)(2,1)}, bf16[1,128,512]{2,1,0:T(8,128)(2,1)}, u32[]{:S(2)}, u32[]{:S(2)}) collective-permute-start(bf16[1,128,512]{2,1,0:T(8,128)(2,1)} %get-tuple-element.42), channel_id=1, source_target_pairs={{0,1},{1,2},{2,3},{3,0},{4,5},{5,6},{6,7},{7,4},{8,9},{9,10},{10,1... | collective-permute-start | bytes 393224 | tf_op jit(solution)/shard_map/ppermute | solution.py:334
  59.8 25.2 %collective-permute-start.4 = (bf16[1,128,512]{2,1,0:T(8,128)(2,1)}, bf16[1,128,512]{2,1,0:T(8,128)(2,1)}, u32[]{:S(2)}, u32[]{:S(2)}) collective-permute-start(bf16[1,128,512]{2,1,0:T(8,128)(2,1)} %get-tuple-element.43), channel_id=1, source_target_pairs={{0,3},{1,0},{2,1},{3,2},{4,7},{5,4},{6,5},{7,6},{8,11},{9,8},{10,9... | collective-permute-start | bytes 393224 | tf_op jit(solution)/shard_map/ppermute | solution.py:334
  67.7 53.8 %collective-permute-start.22 = (bf16[2,128,768]{2,1,0:T(8,128)(2,1)}, bf16[2,128,768]{2,1,0:T(8,128)(2,1)}, u32[]{:S(2)}, u32[]{:S(2)}) collective-permute-start(bf16[2,128,768]{2,1,0:T(8,128)(2,1)} %get-tuple-element.61), channel_id=1, source_target_pairs={{0,1},{1,2},{2,3},{3,0},{4,5},{5,6},{6,7},{7,4},{8,9},{9,10},{10,1... | collective-permute-start | bytes 1179656 | tf_op jit(solution)/shard_map/ppermute | solution.py:334
  72.0 52.9 %collective-permute-start.23 = (bf16[2,128,768]{2,1,0:T(8,128)(2,1)}, bf16[2,128,768]{2,1,0:T(8,128)(2,1)}, u32[]{:S(2)}, u32[]{:S(2)}) collective-permute-start(bf16[2,128,768]{2,1,0:T(8,128)(2,1)} %get-tuple-element.62), channel_id=1, source_target_pairs={{0,2},{1,3},{2,0},{3,1},{4,6},{5,7},{6,4},{7,5},{8,10},{9,11},{10,... | collective-permute-start | bytes 1179656 | tf_op jit(solution)/shard_map/ppermute | solution.py:334
  74.1 46.1 %collective-permute-start = (bf16[2,128,512]{2,1,0:T(8,128)(2,1)}, bf16[2,128,512]{2,1,0:T(8,128)(2,1)}, u32[]{:S(2)}, u32[]{:S(2)}) collective-permute-start(bf16[2,128,512]{2,1,0:T(8,128)(2,1)} %get-tuple-element.40), channel_id=1, source_target_pairs={{0,1},{1,2},{2,3},{3,0},{4,5},{5,6},{6,7},{7,4},{8,9},{9,10},{10,1... | collective-permute-start | bytes 786440 | tf_op jit(solution)/shard_map/ppermute | solution.py:334
  80.0 0.8 copy-start.2
  80.8 0.8 copy-start.4
  81.6 56.2 %collective-permute-start.25 = (bf16[2,2,128,768]{3,2,1,0:T(8,128)(2,1)S(1)}, bf16[2,2,128,768]{3,2,1,0:T(8,128)(2,1)S(1)}, u32[]{:S(2)}, u32[]{:S(2)}) collective-permute-start(bf16[2,2,128,768]{3,2,1,0:T(8,128)(2,1)S(1)} %get-tuple-element.64.refs_5_), channel_id=1, source_target_pairs={{0,4},{1,5},{2,6},{3,7},{4,8},{5,9},{6,10},{7,11},{8,12},{9,13},{1... | collective-permute-start | bytes 2359304 | tf_op jit(solution)/shard_map/ppermute | solution.py:334
  85.0 57.0 %collective-permute-start.26 = (bf16[2,2,128,768]{3,2,1,0:T(8,128)(2,1)S(1)}, bf16[2,2,128,768]{3,2,1,0:T(8,128)(2,1)S(1)}, u32[]{:S(2)}, u32[]{:S(2)}) collective-permute-start(bf16[2,2,128,768]{3,2,1,0:T(8,128)(2,1)S(1)} %get-tuple-element.65.refs_4_), channel_id=1, source_target_pairs={{4,0},{5,1},{6,2},{7,3},{8,4},{9,5},{10,6},{11,7},{12,8},{13,9},{1... | collective-permute-start | bytes 2359304 | tf_op jit(solution)/shard_map/ppermute | solution.py:334
  120.3 17.6 %collective-permute-start.24 = (bf16[2,128,768]{2,1,0:T(8,128)(2,1)}, bf16[2,128,768]{2,1,0:T(8,128)(2,1)S(1)}, u32[]{:S(2)}, u32[]{:S(2)}) collective-permute-start(bf16[2,128,768]{2,1,0:T(8,128)(2,1)} %get-tuple-element.63), channel_id=1, source_target_pairs={{0,3},{1,0},{2,1},{3,2},{4,7},{5,4},{6,5},{7,6},{8,11},{9,8},{10,9... | collective-permute-start | bytes 1179656 | tf_op jit(solution)/shard_map/ppermute | solution.py:334
  121.5 43.5 %collective-permute-start.12 = (bf16[2,2,128,512]{3,2,1,0:T(8,128)(2,1)}, bf16[2,2,128,512]{3,2,1,0:T(8,128)(2,1)}, u32[]{:S(2)}, u32[]{:S(2)}) collective-permute-start(bf16[2,2,128,512]{3,2,1,0:T(8,128)(2,1)} %copy-done.4), channel_id=1, source_target_pairs={{0,4},{1,5},{2,6},{3,7},{4,8},{5,9},{6,10},{7,11},{8,12},{9,13},{1... | collective-permute-start | bytes 1572872 | tf_op jit(solution)/shard_map/ppermute | solution.py:334
  124.9 40.1 %collective-permute-start.13 = (bf16[2,2,128,512]{3,2,1,0:T(8,128)(2,1)}, bf16[2,2,128,512]{3,2,1,0:T(8,128)(2,1)}, u32[]{:S(2)}, u32[]{:S(2)}) collective-permute-start(bf16[2,2,128,512]{3,2,1,0:T(8,128)(2,1)} %copy-done.2), channel_id=1, source_target_pairs={{4,0},{5,1},{6,2},{7,3},{8,4},{9,5},{10,6},{11,7},{12,8},{13,9},{1... | collective-permute-start | bytes 1572872 | tf_op jit(solution)/shard_map/ppermute | solution.py:334
  137.8 21.3 %collective-permute-start.1 = (bf16[2,128,512]{2,1,0:T(8,128)(2,1)}, bf16[2,128,512]{2,1,0:T(8,128)(2,1)S(1)}, u32[]{:S(2)}, u32[]{:S(2)}) collective-permute-start(bf16[2,128,512]{2,1,0:T(8,128)(2,1)} %get-tuple-element.41), channel_id=1, source_target_pairs={{0,3},{1,0},{2,1},{3,2},{4,7},{5,4},{6,5},{7,6},{8,11},{9,8},{10,9... | collective-permute-start | bytes 786440 | tf_op jit(solution)/shard_map/ppermute | solution.py:334
  137.8 24.7 %collective-permute-start.3 = (bf16[1,128,512]{2,1,0:T(8,128)(2,1)}, bf16[1,128,512]{2,1,0:T(8,128)(2,1)S(1)}, u32[]{:S(2)}, u32[]{:S(2)}) collective-permute-start(bf16[1,128,512]{2,1,0:T(8,128)(2,1)} %collective-permute-done.2), channel_id=1, source_target_pairs={{0,1},{1,2},{2,3},{3,0},{4,5},{5,6},{6,7},{7,4},{8,9},{9,10},{10,1... | collective-permute-start | bytes 393224 | tf_op jit(solution)/shard_map/ppermute | solution.py:334
  142.0 0.9 copy-start
  142.8 22.1 %collective-permute-start.5 = (bf16[1,128,512]{2,1,0:T(8,128)(2,1)}, bf16[1,128,512]{2,1,0:T(8,128)(2,1)S(1)}, u32[]{:S(2)}, u32[]{:S(2)}) collective-permute-start(bf16[1,128,512]{2,1,0:T(8,128)(2,1)} %collective-permute-done.4), channel_id=1, source_target_pairs={{0,3},{1,0},{2,1},{3,2},{4,7},{5,4},{6,5},{7,6},{8,11},{9,8},{10,9... | collective-permute-start | bytes 393224 | tf_op jit(solution)/shard_map/ppermute | solution.py:334
  142.8 1.1 copy-start.1
  144.0 21.0 %copy-start.3 = (bf16[2,2,128,512]{3,2,1,0:T(8,128)(2,1)S(1)}, bf16[2,2,128,512]{3,2,1,0:T(8,128)(2,1)}, u32[]{:S(2)}) copy-start(bf16[2,2,128,512]{3,2,1,0:T(8,128)(2,1)} %copy-done.2) | copy-start | bytes 1572868
  144.0 21.0 %copy-start.5 = (bf16[2,2,128,512]{3,2,1,0:T(8,128)(2,1)S(1)}, bf16[2,2,128,512]{3,2,1,0:T(8,128)(2,1)}, u32[]{:S(2)}) copy-start(bf16[2,2,128,512]{3,2,1,0:T(8,128)(2,1)} %copy-done.4) | copy-start | bytes 1572868
  159.1 46.5 %collective-permute-start.30 = (bf16[2,2,128,768]{3,2,1,0:T(8,128)(2,1)S(1)}, bf16[2,2,128,768]{3,2,1,0:T(8,128)(2,1)S(1)}, u32[]{:S(2)}, u32[]{:S(2)}) collective-permute-start(bf16[2,2,128,768]{3,2,1,0:T(8,128)(2,1)S(1)} %get-tuple-element.71), channel_id=1, source_target_pairs={{0,4},{1,5},{2,6},{3,7},{4,8},{5,9},{6,10},{7,11},{8,12},{9,13},{1... | collective-permute-start | bytes 2359304 | tf_op jit(solution)/shard_map/ppermute | solution.py:334
  162.5 43.3 %collective-permute-start.31 = (bf16[2,2,128,768]{3,2,1,0:T(8,128)(2,1)S(1)}, bf16[2,2,128,768]{3,2,1,0:T(8,128)(2,1)S(1)}, u32[]{:S(2)}, u32[]{:S(2)}) collective-permute-start(bf16[2,2,128,768]{3,2,1,0:T(8,128)(2,1)S(1)} %get-tuple-element.72), channel_id=1, source_target_pairs={{4,0},{5,1},{6,2},{7,3},{8,4},{9,5},{10,6},{11,7},{12,8},{13,9},{1... | collective-permute-start | bytes 2359304 | tf_op jit(solution)/shard_map/ppermute | solution.py:334
  175.4 17.3 %collective-permute-start.17 = (bf16[2,2,128,512]{3,2,1,0:T(8,128)(2,1)S(1)}, bf16[2,2,128,512]{3,2,1,0:T(8,128)(2,1)S(1)}, u32[]{:S(2)}, u32[]{:S(2)}) collective-permute-start(bf16[2,2,128,512]{3,2,1,0:T(8,128)(2,1)S(1)} %get-tuple-element.55), channel_id=1, source_target_pairs={{0,4},{1,5},{2,6},{3,7},{4,8},{5,9},{6,10},{7,11},{8,12},{9,13},{1... | collective-permute-start | bytes 1572872 | tf_op jit(solution)/shard_map/ppermute | solution.py:334
  178.8 16.7 %collective-permute-start.18 = (bf16[2,2,128,512]{3,2,1,0:T(8,128)(2,1)S(1)}, bf16[2,2,128,512]{3,2,1,0:T(8,128)(2,1)S(1)}, u32[]{:S(2)}, u32[]{:S(2)}) collective-permute-start(bf16[2,2,128,512]{3,2,1,0:T(8,128)(2,1)S(1)} %get-tuple-element.56), channel_id=1, source_target_pairs={{4,0},{5,1},{6,2},{7,3},{8,4},{9,5},{10,6},{11,7},{12,8},{13,9},{1... | collective-permute-start | bytes 1572872 | tf_op jit(solution)/shard_map/ppermute | solution.py:334
  181.9 6.5 %collective-permute-start.14 = (bf16[128,512]{1,0:T(8,128)(2,1)S(1)}, bf16[128,512]{1,0:T(8,128)(2,1)S(1)}, u32[]{:S(2)}, u32[]{:S(2)}) collective-permute-start(bf16[128,512]{1,0:T(8,128)(2,1)S(1)} %get-tuple-element.51), channel_id=1, source_target_pairs={{0,1},{1,2},{2,3},{3,0},{4,5},{5,6},{6,7},{7,4},{8,9},{9,10},{10,1... | collective-permute-start | bytes 393224 | tf_op jit(solution)/shard_map/ppermute | solution.py:334
  188.4 13.2 %collective-permute-start.15 = (bf16[128,512]{1,0:T(8,128)(2,1)S(1)}, bf16[128,512]{1,0:T(8,128)(2,1)S(1)}, u32[]{:S(2)}, u32[]{:S(2)}) collective-permute-start(bf16[128,512]{1,0:T(8,128)(2,1)S(1)} %get-tuple-element.52), channel_id=1, source_target_pairs={{0,2},{1,3},{2,0},{3,1},{4,6},{5,7},{6,4},{7,5},{8,10},{9,11},{10,... | collective-permute-start | bytes 393224 | tf_op jit(solution)/shard_map/ppermute | solution.py:334
  192.7 70.6 %collective-permute-start.27 = (bf16[128,768]{1,0:T(8,128)(2,1)S(1)}, bf16[128,768]{1,0:T(8,128)(2,1)S(1)}, u32[]{:S(2)}, u32[]{:S(2)}) collective-permute-start(bf16[128,768]{1,0:T(8,128)(2,1)S(1)} %get-tuple-element.67), channel_id=1, source_target_pairs={{0,1},{1,2},{2,3},{3,0},{4,5},{5,6},{6,7},{7,4},{8,9},{9,10},{10,1... | collective-permute-start | bytes 589832 | tf_op jit(solution)/shard_map/ppermute | solution.py:334
  195.5 69.3 %collective-permute-start.28 = (bf16[128,768]{1,0:T(8,128)(2,1)S(1)}, bf16[128,768]{1,0:T(8,128)(2,1)S(1)}, u32[]{:S(2)}, u32[]{:S(2)}) collective-permute-start(bf16[128,768]{1,0:T(8,128)(2,1)S(1)} %get-tuple-element.68), channel_id=1, source_target_pairs={{0,2},{1,3},{2,0},{3,1},{4,6},{5,7},{6,4},{7,5},{8,10},{9,11},{10,... | collective-permute-start | bytes 589832 | tf_op jit(solution)/shard_map/ppermute | solution.py:334
  201.6 58.8 %collective-permute-start.16 = (bf16[128,512]{1,0:T(8,128)(2,1)S(1)}, bf16[128,512]{1,0:T(8,128)(2,1)S(1)}, u32[]{:S(2)}, u32[]{:S(2)}) collective-permute-start(bf16[128,512]{1,0:T(8,128)(2,1)S(1)} %get-tuple-element.53), channel_id=1, source_target_pairs={{0,3},{1,0},{2,1},{3,2},{4,7},{5,4},{6,5},{7,6},{8,11},{9,8},{10,9... | collective-permute-start | bytes 393224 | tf_op jit(solution)/shard_map/ppermute | solution.py:334
  205.6 63.8 %collective-permute-start.19 = (bf16[2,128,512]{2,1,0:T(8,128)(2,1)S(1)}, bf16[2,128,512]{2,1,0:T(8,128)(2,1)S(1)}, u32[]{:S(2)}, u32[]{:S(2)}) collective-permute-start(bf16[2,128,512]{2,1,0:T(8,128)(2,1)S(1)} %get-tuple-element.58), channel_id=1, source_target_pairs={{0,1},{1,2},{2,3},{3,0},{4,5},{5,6},{6,7},{7,4},{8,9},{9,10},{10,1... | collective-permute-start | bytes 786440 | tf_op jit(solution)/shard_map/ppermute | solution.py:334
  205.8 60.9 %collective-permute-start.29 = (bf16[128,768]{1,0:T(8,128)(2,1)S(1)}, bf16[128,768]{1,0:T(8,128)(2,1)S(1)}, u32[]{:S(2)}, u32[]{:S(2)}) collective-permute-start(bf16[128,768]{1,0:T(8,128)(2,1)S(1)} %get-tuple-element.69), channel_id=1, source_target_pairs={{0,3},{1,0},{2,1},{3,2},{4,7},{5,4},{6,5},{7,6},{8,11},{9,8},{10,9... | collective-permute-start | bytes 589832 | tf_op jit(solution)/shard_map/ppermute | solution.py:334
  260.4 41.2 %collective-permute-start.32 = (bf16[2,128,768]{2,1,0:T(8,128)(2,1)S(1)}, bf16[2,128,768]{2,1,0:T(8,128)(2,1)S(1)}, u32[]{:S(2)}, u32[]{:S(2)}) collective-permute-start(bf16[2,128,768]{2,1,0:T(8,128)(2,1)S(1)} %get-tuple-element.74), channel_id=1, source_target_pairs={{0,1},{1,2},{2,3},{3,0},{4,5},{5,6},{6,7},{7,4},{8,9},{9,10},{10,1... | collective-permute-start | bytes 1179656 | tf_op jit(solution)/shard_map/ppermute | solution.py:334
  263.3 38.4 %collective-permute-start.33 = (bf16[2,128,768]{2,1,0:T(8,128)(2,1)S(1)}, bf16[2,128,768]{2,1,0:T(8,128)(2,1)S(1)}, u32[]{:S(2)}, u32[]{:S(2)}) collective-permute-start(bf16[2,128,768]{2,1,0:T(8,128)(2,1)S(1)} %get-tuple-element.75), channel_id=1, source_target_pairs={{0,2},{1,3},{2,0},{3,1},{4,6},{5,7},{6,4},{7,5},{8,10},{9,11},{10,... | collective-permute-start | bytes 1179656 | tf_op jit(solution)/shard_map/ppermute | solution.py:334
  264.8 36.9 %collective-permute-start.34 = (bf16[2,128,768]{2,1,0:T(8,128)(2,1)S(1)}, bf16[2,128,768]{2,1,0:T(8,128)(2,1)S(1)}, u32[]{:S(2)}, u32[]{:S(2)}) collective-permute-start(bf16[2,128,768]{2,1,0:T(8,128)(2,1)S(1)} %get-tuple-element.76), channel_id=1, source_target_pairs={{0,3},{1,0},{2,1},{3,2},{4,7},{5,4},{6,5},{7,6},{8,11},{9,8},{10,9... | collective-permute-start | bytes 1179656 | tf_op jit(solution)/shard_map/ppermute | solution.py:334
  266.7 35.0 %collective-permute-start.20 = (bf16[2,128,512]{2,1,0:T(8,128)(2,1)S(1)}, bf16[2,128,512]{2,1,0:T(8,128)(2,1)S(1)}, u32[]{:S(2)}, u32[]{:S(2)}) collective-permute-start(bf16[2,128,512]{2,1,0:T(8,128)(2,1)S(1)} %get-tuple-element.59), channel_id=1, source_target_pairs={{0,2},{1,3},{2,0},{3,1},{4,6},{5,7},{6,4},{7,5},{8,10},{9,11},{10,... | collective-permute-start | bytes 786440 | tf_op jit(solution)/shard_map/ppermute | solution.py:334
  269.4 32.3 %collective-permute-start.21 = (bf16[2,128,512]{2,1,0:T(8,128)(2,1)S(1)}, bf16[2,128,512]{2,1,0:T(8,128)(2,1)S(1)}, u32[]{:S(2)}, u32[]{:S(2)}) collective-permute-start(bf16[2,128,512]{2,1,0:T(8,128)(2,1)S(1)} %get-tuple-element.60), channel_id=1, source_target_pairs={{0,3},{1,0},{2,1},{3,2},{4,7},{5,4},{6,5},{7,6},{8,11},{9,8},{10,9... | collective-permute-start | bytes 786440 | tf_op jit(solution)/shard_map/ppermute | solution.py:334

commit v6 on v5

--- a/solution.py
+++ b/solution.py
@@ -1,4 +1,3 @@
-import functools
 import math
 
 import jax
@@ -12,7 +11,7 @@
 BLK = 128
 HD = 128
 NZ = 4
-CHUNKS = ((0, 4), (4, 6))
+CHUNKS = ((0, 6), (6, 4))
 CW = 256
 SCALE = 1.0 / math.sqrt(HD)
 EXP2_SCALE = SCALE / math.log(2.0)
@@ -29,33 +28,6 @@
 
 def cost(flops, nbytes):
     return pl.CostEstimate(flops=flops, bytes_accessed=nbytes, transcendentals=0)
-
-
-def pack_direct_body(zh, a1, a2, a3, b1, b2, b3, o1, o2, o3):
-    for a, b, o in ((a1, b1, o1), (a2, b2, o2), (a3, b3, o3)):
-        o[0] = a[...]
-        o[1] = b[...]
-
-
-def pack_direct(zh, a, b, first, heads, group):
-    per, off, steps = group * HD // CW, first * HD // CW, heads * HD // CW
-
-    def src(s):
-        return pl.BlockSpec((BLK, CW), lambda i, z: (0, lax.rem(z[0] + s, NZ) * per + off + i))
-
-    out = pl.BlockSpec((2, BLK, CW), lambda i, z: (0, 0, i))
-    return pl.pallas_call(
-        pack_direct_body,
-        grid_spec=pltpu.PrefetchScalarGridSpec(
-            num_scalar_prefetch=1,
-            grid=(steps,),
-            in_specs=[src(1), src(2), src(3)] * 2,
-            out_specs=[out] * 3,
-        ),
-        out_shape=[jax.ShapeDtypeStruct((2, BLK, heads * HD), BF)] * 3,
-        cost_estimate=cost(0, 12 * BLK * heads * HD * 2),
-        compiler_params=grant(56),
-    )(zh, a, a, a, b, b, b)
 
 
 def pack_body(zh, *refs):
@@ -135,19 +107,11 @@
     )(zh, k, v, *recv)
 
 
-def attend_body(direct, zh, q0, g0, *refs):
-    n = 3 if direct else 4
-    got, refs = refs[:n], refs[n:]
-    before, lo, hi, after, bias, *refs = refs
-    if direct:
-        one, two, three = ((r.at[0], r.at[1]) for r in got)
-    else:
-        mp, mm, fp, fm = got
-        one, two, three = (mp.at[0], mp.at[1]), (fp.at[0], fm.at[0]), (mm.at[0], mm.at[1])
-    (
-        dq0, dq1, dq2, dq3, rim_before, rim_after, own,
-        qs, gs, ks, vs, dqs, dk, dv,
-    ) = refs
+def attend_body(zh, q0, g0, mp, mm, fp, fm, before, lo, hi, after, bias,
+                dq0, dq1, dq2, dq3, rim_before, rim_after, own,
+                qs, gs, ks, vs, dqs, dk, dv):
+    a = mp.shape[0] - 2
+    one, two, three = (mp.at[a], mp.at[a + 1]), (fp.at[0], fm.at[0]), (mm.at[a], mm.at[a + 1])
     z = zh[0]
     for s, (qq, gg) in enumerate(((q0, g0), one, two, three)):
         row = pl.multiple_of(lax.rem(z + NZ - s, NZ) * BLK, BLK)
@@ -203,16 +167,13 @@
 def attend(zh, q, g, recv, before, lo, hi, after, bias, first, heads, group):
     n = heads * HD
     mine = pl.BlockSpec((BLK, HD), lambda h, z: (0, z[0] * group + first + h))
-    two = pl.BlockSpec((2, BLK, HD), lambda h, z: (0, 0, h))
-    one = pl.BlockSpec((1, BLK, HD), lambda h, z: (0, 0, h))
-    direct = len(recv) == 3
-    got = [two] * 3 if direct else [two, two, one, one]
+    got = [pl.BlockSpec((a.shape[0], BLK, HD), lambda h, z: (0, 0, h)) for a in recv]
     flat = pl.BlockSpec((BLK, HD), lambda h, z: (0, h))
     rim = pl.BlockSpec((2, 2, BLK, HD), lambda h, z: (0, 0, 0, h))
     own = pl.BlockSpec((4, 2, BLK, HD), lambda h, z: (0, 0, 0, h))
     shape = jax.ShapeDtypeStruct
     return pl.pallas_call(
-        functools.partial(attend_body, direct),
+        attend_body,
         grid_spec=pltpu.PrefetchScalarGridSpec(
             num_scalar_prefetch=1,
             grid=(heads,),
@@ -354,7 +315,10 @@
         return mp, mm, fp, fm
 
     kv = gather(key, value, 0, group, group * HD // 2)
-    qg = [gather(query, dout, *CHUNKS[0], CW), around(pack_direct(zh, query, dout, *CHUNKS[1], group))]
+    p, m = pack(zh, ((query, 2), (query, 1), (dout, 1)), ((dout, 2), (query, 3), (dout, 3)), *CHUNKS[1], group)
+    p, m = move("uly", rings[1], p), move("uly", rings[3], m)
+    fp, fm = move("uly", rings[1], p[:1]), move("uly", rings[3], m[:1])
+    qg = [gather(query, dout, *CHUNKS[0], CW), (p, m, fp, fm)]
     halves = unpack(zh, key, value, kv, group)
     parts = []
     for c, (first, heads) in enumerate(CHUNKS):

time: 305 us -> 296 us (0.970)
  the two profiles are of different devices: /device:TPU:90 before, /device:TPU:32 now
where the time goes in v6:
time: 296 us; the launch traced here: 295 us
  starting transfers between devices  126 us (43%)
  waiting for transfers between devices  114 us (39%)
  Pallas kernels  44.9 us (15%)
  local copies, waits for them, and re-layouts  6.82 us (2%)
    ppermute x36, starting transfers between devices, move(): return lax.ppermute(a, axes, perm)  126 us
    ppermute x36, waiting for transfers between devices, move(): return lax.ppermute(a, axes, perm)  114 us
    pallas_call x2, Pallas kernels, attend(): pl.pallas_call(attend_body, grid_spec=pltpu.PrefetchScalarGridSpec(num_sc...  25.5 us
    pallas_call x5, Pallas kernels, pack(): pl.pallas_call(pack_body, grid_spec=pltpu.PrefetchScalarGridSpec(num_scal...  11.7 us
  transfers between devices with their start and end apart: 36, of which 7 were waited for; matrix products, arithmetic and copies ran while one was open for 2% of the time, Pallas kernels for 14%

profile of v6, /device:TPU:32, one launch (start us, length us, event | category | flops | bytes accessed | tf_op | source)
XLA Modules:
  0.0 294.7 jit_solution(17117509800391179612)
XLA Ops:
  0.6 2.3 shard_map.78
  3.0 3.3 %collective-permute-start.6 = (bf16[2,128,1280]{2,1,0:T(8,128)(2,1)}, bf16[2,128,1280]{2,1,0:T(8,128)(2,1)S(1)}, u32[]{:S(2)}, u32[]{:S(2)}) collective-permute-start(bf16[2,128,1280]{2,1,0:T(8,128)(2,1)} %get-tuple-element.43), channel_id=1, source_target_pairs={{0,1},{1,2},{2,3},{3,0},{4,5},{5,6},{6,7},{7,4},{8,9},{9,10},{10,1... | collective-permute-start | bytes 1966088 | tf_op jit(solution)/shard_map/ppermute | solution.py:295
  6.2 2.2 collective-permute-start.7
  8.4 1.9 shard_map.79
  10.4 1.4 collective-permute-start.8
  11.8 2.7 collective-permute-start.10
  14.5 37.0 %collective-permute-done.8 = bf16[1,128,1280]{2,1,0:T(8,128)(2,1)S(1)} collective-permute-done((bf16[1,128,1280]{2,1,0:T(8,128)(2,1)}, bf16[1,128,1280]{2,1,0:T(8,128)(2,1)S(1)}, u32[]{:S(2)}, u32[]{:S(2)}) %collective-permute-start.8) | collective-permute-done | bytes 327712 | tf_op jit(solution)/shard_map/ppermute | solution.py:295
  51.6 4.1 %collective-permute-start.11 = (bf16[1,128,1280]{2,1,0:T(8,128)(2,1)S(1)}, bf16[1,128,1280]{2,1,0:T(8,128)(2,1)S(1)}, u32[]{:S(2)}, u32[]{:S(2)}) collective-permute-start(bf16[1,128,1280]{2,1,0:T(8,128)(2,1)S(1)} %collective-permute-done.10), channel_id=1, source_target_pairs={{0,3},{1,0},{2,1},{3,2},{4,7},{5,4},{6,5},{7,6},{8,11},{9,8},{10,9... | collective-permute-start | bytes 983048 | tf_op jit(solution)/shard_map/ppermute | solution.py:295
  55.6 2.5 shard_map.77
  58.5 3.8 %collective-permute-start.4 = (bf16[1,128,768]{2,1,0:T(8,128)(2,1)}, bf16[1,128,768]{2,1,0:T(8,128)(2,1)}, u32[]{:S(2)}, u32[]{:S(2)}) collective-permute-start(bf16[1,128,768]{2,1,0:T(8,128)(2,1)} %get-tuple-element.42), channel_id=1, source_target_pairs={{0,3},{1,0},{2,1},{3,2},{4,7},{5,4},{6,5},{7,6},{8,11},{9,8},{10,9... | collective-permute-start | bytes 589832 | tf_op jit(solution)/shard_map/ppermute | solution.py:295
  62.3 2.9 shard_map.76
  65.6 3.5 %collective-permute-done.9.fp = bf16[1,128,1280]{2,1,0:T(8,128)(2,1)S(1)} collective-permute-done((bf16[1,128,1280]{2,1,0:T(8,128)(2,1)S(1)}, bf16[1,128,1280]{2,1,0:T(8,128)(2,1)S(1)}, u32[]{:S(2)}, u32[]{:S(2)}) %collective-permute-start.9) | collective-permute-done | bytes 327712 | tf_op jit(solution)/shard_map/ppermute | solution.py:295
  69.8 2.0 shard_map.82
  71.8 2.4 collective-permute-start.22
  74.2 3.8 %unpack.1 = (bf16[2,2,128,768]{3,2,1,0:T(8,128)(2,1)S(1)}, bf16[2,2,128,768]{3,2,1,0:T(8,128)(2,1)}, bf16[2,2,128,512]{3,2,1,0:T(8,128)(2,1)S(1)}, bf16[2,2,128,512]{3,2,1,0:T(8,128)(2,1)S(1)}) custom-call(s32[1]{0:T(128)} %bitcast.zh, bf16[128,5120]{1,0:T(8,128)(2,1)} %k.1, bf16[128,5120]{1,0:T(8,128)(2,1)} %v.1, ...), custom_call_target="tpu_custom_call" | custom-call | bytes 5242880 | tf_op jit(solution)/shard_map/unpack/pallas_call | solution.py:98
  79.6 3.4 %collective-permute-start.12 = (bf16[2,2,128,768]{3,2,1,0:T(8,128)(2,1)}, bf16[2,2,128,768]{3,2,1,0:T(8,128)(2,1)S(1)}, u32[]{:S(2)}, u32[]{:S(2)}) collective-permute-start(bf16[2,2,128,768]{3,2,1,0:T(8,128)(2,1)} %get-tuple-element.47.hi), channel_id=1, source_target_pairs={{0,4},{1,5},{2,6},{3,7},{4,8},{5,9},{6,10},{7,11},{8,12},{9,13},{1... | collective-permute-start | bytes 2359304 | tf_op jit(solution)/shard_map/ppermute | solution.py:295
  83.0 13.3 %collective-permute-start.13 = (bf16[2,2,128,768]{3,2,1,0:T(8,128)(2,1)S(1)}, bf16[2,2,128,768]{3,2,1,0:T(8,128)(2,1)S(1)}, u32[]{:S(2)}, u32[]{:S(2)}) collective-permute-start(bf16[2,2,128,768]{3,2,1,0:T(8,128)(2,1)S(1)} %get-tuple-element.48.lo), channel_id=1, source_target_pairs={{4,0},{5,1},{6,2},{7,3},{8,4},{9,5},{10,6},{11,7},{12,8},{13,9},{1... | collective-permute-start | bytes 2359304 | tf_op jit(solution)/shard_map/ppermute | solution.py:295
  96.9 1.7 collective-permute-start.23
  98.7 1.2 collective-permute-start.3
  100.9 8.5 %collective-permute-done.3.fp = bf16[1,128,768]{2,1,0:T(8,128)(2,1)} collective-permute-done((bf16[1,128,768]{2,1,0:T(8,128)(2,1)}, bf16[1,128,768]{2,1,0:T(8,128)(2,1)}, u32[]{:S(2)}, u32[]{:S(2)}) %collective-permute-start.3) | collective-permute-done | bytes 196640 | tf_op jit(solution)/shard_map/ppermute | solution.py:295
  109.4 3.1 %collective-permute-start.26 = (bf16[2,2,128,512]{3,2,1,0:T(8,128)(2,1)}, bf16[2,2,128,512]{3,2,1,0:T(8,128)(2,1)}, u32[]{:S(2)}, u32[]{:S(2)}) collective-permute-start(bf16[2,2,128,512]{3,2,1,0:T(8,128)(2,1)} %copy-done.2), channel_id=1, source_target_pairs={{0,4},{1,5},{2,6},{3,7},{4,8},{5,9},{6,10},{7,11},{8,12},{9,13},{1... | collective-permute-start | bytes 1572872 | tf_op jit(solution)/shard_map/ppermute | solution.py:295
  112.5 24.1 %collective-permute-start.27 = (bf16[2,2,128,512]{3,2,1,0:T(8,128)(2,1)}, bf16[2,2,128,512]{3,2,1,0:T(8,128)(2,1)}, u32[]{:S(2)}, u32[]{:S(2)}) collective-permute-start(bf16[2,2,128,512]{3,2,1,0:T(8,128)(2,1)} %copy-done), channel_id=1, source_target_pairs={{4,0},{5,1},{6,2},{7,3},{8,4},{9,5},{10,6},{11,7},{12,8},{13,9},{1... | collective-permute-start | bytes 1572872 | tf_op jit(solution)/shard_map/ppermute | solution.py:295
  136.7 5.9 %collective-permute-start.5 = (bf16[1,128,768]{2,1,0:T(8,128)(2,1)}, bf16[1,128,768]{2,1,0:T(8,128)(2,1)}, u32[]{:S(2)}, u32[]{:S(2)}) collective-permute-start(bf16[1,128,768]{2,1,0:T(8,128)(2,1)} %collective-permute-done.4), channel_id=1, source_target_pairs={{0,3},{1,0},{2,1},{3,2},{4,7},{5,4},{6,5},{7,6},{8,11},{9,8},{10,9... | collective-permute-start | bytes 589832 | tf_op jit(solution)/shard_map/ppermute | solution.py:295
  143.3 1.7 broadcast_in_dim.17
  145.0 1.7 reshape.61
  146.7 0.9 copy.12.bias
  147.7 5.9 %collective-permute-done.5.fm = bf16[1,128,768]{2,1,0:T(8,128)(2,1)} collective-permute-done((bf16[1,128,768]{2,1,0:T(8,128)(2,1)}, bf16[1,128,768]{2,1,0:T(8,128)(2,1)}, u32[]{:S(2)}, u32[]{:S(2)}) %collective-permute-start.5) | collective-permute-done | bytes 196640 | tf_op jit(solution)/shard_map/ppermute | solution.py:295
  153.6 1.5 collective-permute-start.24
  155.1 2.6 collective-permute-start.25
  157.7 15.0 %shard_map.80 = (bf16[128,768]{1,0:T(8,128)(2,1)S(1)}, bf16[128,768]{1,0:T(8,128)(2,1)S(1)}, bf16[128,768]{1,0:T(8,128)(2,1)S(1)}, bf16[128,768]{1,0:T(8,128)(2,...) custom-call(s32[1]{0:T(128)} %bitcast.zh, ...), custom_call_target="tpu_custom_call" | custom-call | flops 3019898880 | bytes 7864320 | tf_op jit(solution)/shard_map/pallas_call | solution.py:175
  172.7 1.9 collective-permute-start.17
  174.7 7.9 %collective-permute-start.18 = (bf16[2,2,128,768]{3,2,1,0:T(8,128)(2,1)S(1)}, bf16[2,2,128,768]{3,2,1,0:T(8,128)(2,1)S(1)}, u32[]{:S(2)}, u32[]{:S(2)}) collective-permute-start(bf16[2,2,128,768]{3,2,1,0:T(8,128)(2,1)S(1)} %get-tuple-element.55), channel_id=1, source_target_pairs={{4,0},{5,1},{6,2},{7,3},{8,4},{9,5},{10,6},{11,7},{12,8},{13,9},{1... | collective-permute-start | bytes 2359304 | tf_op jit(solution)/shard_map/ppermute | solution.py:295
  182.6 10.5 %shard_map.83 = (bf16[128,512]{1,0:T(8,128)(2,1)S(1)}, bf16[128,512]{1,0:T(8,128)(2,1)S(1)}, bf16[128,512]{1,0:T(8,128)(2,1)S(1)}, bf16[128,512]{1,0:T(8,128)(2,...) custom-call(s32[1]{0:T(128)} %bitcast.zh, ...), custom_call_target="tpu_custom_call" | custom-call | flops 2013265920 | bytes 5242880 | tf_op jit(solution)/shard_map/pallas_call | solution.py:175
  193.1 1.9 collective-permute-start.31
  195.0 7.9 %collective-permute-start.32 = (bf16[2,2,128,512]{3,2,1,0:T(8,128)(2,1)S(1)}, bf16[2,2,128,512]{3,2,1,0:T(8,128)(2,1)S(1)}, u32[]{:S(2)}, u32[]{:S(2)}) collective-permute-start(bf16[2,2,128,512]{3,2,1,0:T(8,128)(2,1)S(1)} %get-tuple-element.70), channel_id=1, source_target_pairs={{4,0},{5,1},{6,2},{7,3},{8,4},{9,5},{10,6},{11,7},{12,8},{13,9},{1... | collective-permute-start | bytes 1572872 | tf_op jit(solution)/shard_map/ppermute | solution.py:295
  203.2 40.8 %collective-permute-done.28.refs_9_ = bf16[128,512]{1,0:T(8,128)(2,1)S(1)} collective-permute-done((bf16[128,512]{1,0:T(8,128)(2,1)S(1)}, bf16[128,512]{1,0:T(8,128)(2,1)S(1)}, u32[]{:S(2)}, u32[]{:S(2)}) %collective-permute-start.28) | collective-permute-done | bytes 131104 | tf_op jit(solution)/shard_map/ppermute | solution.py:295
  244.0 3.5 %collective-permute-start.29 = (bf16[128,512]{1,0:T(8,128)(2,1)S(1)}, bf16[128,512]{1,0:T(8,128)(2,1)S(1)}, u32[]{:S(2)}, u32[]{:S(2)}) collective-permute-start(bf16[128,512]{1,0:T(8,128)(2,1)S(1)} %get-tuple-element.66), channel_id=1, source_target_pairs={{0,2},{1,3},{2,0},{3,1},{4,6},{5,7},{6,4},{7,5},{8,10},{9,11},{10,... | collective-permute-start | bytes 393224 | tf_op jit(solution)/shard_map/ppermute | solution.py:295
  247.5 2.4 collective-permute-start.14
  249.9 2.5 collective-permute-start.15
  253.0 4.8 %collective-permute-start.30 = (bf16[128,512]{1,0:T(8,128)(2,1)S(1)}, bf16[128,512]{1,0:T(8,128)(2,1)S(1)}, u32[]{:S(2)}, u32[]{:S(2)}) collective-permute-start(bf16[128,512]{1,0:T(8,128)(2,1)S(1)} %get-tuple-element.67), channel_id=1, source_target_pairs={{0,3},{1,0},{2,1},{3,2},{4,7},{5,4},{6,5},{7,6},{8,11},{9,8},{10,9... | collective-permute-start | bytes 393224 | tf_op jit(solution)/shard_map/ppermute | solution.py:295
  257.8 4.1 %collective-permute-start.16 = (bf16[128,768]{1,0:T(8,128)(2,1)S(1)}, bf16[128,768]{1,0:T(8,128)(2,1)S(1)}, u32[]{:S(2)}, u32[]{:S(2)}) collective-permute-start(bf16[128,768]{1,0:T(8,128)(2,1)S(1)} %get-tuple-element.52), channel_id=1, source_target_pairs={{0,3},{1,0},{2,1},{3,2},{4,7},{5,4},{6,5},{7,6},{8,11},{9,8},{10,9... | collective-permute-start | bytes 589832 | tf_op jit(solution)/shard_map/ppermute | solution.py:295
  262.0 0.9 shard_map.81
  263.8 3.5 %collective-permute-start.20 = (bf16[2,128,768]{2,1,0:T(8,128)(2,1)S(1)}, bf16[2,128,768]{2,1,0:T(8,128)(2,1)S(1)}, u32[]{:S(2)}, u32[]{:S(2)}) collective-permute-start(bf16[2,128,768]{2,1,0:T(8,128)(2,1)S(1)} %get-tuple-element.58), channel_id=1, source_target_pairs={{0,2},{1,3},{2,0},{3,1},{4,6},{5,7},{6,4},{7,5},{8,10},{9,11},{10,... | collective-permute-start | bytes 1179656 | tf_op jit(solution)/shard_map/ppermute | solution.py:295
  267.3 2.3 collective-permute-start.21
  269.6 3.5 %collective-permute-start.34 = (bf16[2,128,512]{2,1,0:T(8,128)(2,1)S(1)}, bf16[2,128,512]{2,1,0:T(8,128)(2,1)S(1)}, u32[]{:S(2)}, u32[]{:S(2)}) collective-permute-start(bf16[2,128,512]{2,1,0:T(8,128)(2,1)S(1)} %get-tuple-element.73), channel_id=1, source_target_pairs={{0,2},{1,3},{2,0},{3,1},{4,6},{5,7},{6,4},{7,5},{8,10},{9,11},{10,... | collective-permute-start | bytes 786440 | tf_op jit(solution)/shard_map/ppermute | solution.py:295
  273.8 14.5 %collective-permute-done.34.refs_14_ = bf16[2,128,512]{2,1,0:T(8,128)(2,1)S(1)} collective-permute-done((bf16[2,128,512]{2,1,0:T(8,128)(2,1)S(1)}, bf16[2,128,512]{2,1,0:T(8,128)(2,1)S(1)}, u32[]{:S(2)}, u32[]{:S(2)}) %collective-permute-start.34) | collective-permute-done | bytes 262176 | tf_op jit(solution)/shard_map/ppermute | solution.py:295
  288.2 4.0 %collective-permute-done.35.refs_15_ = bf16[2,128,512]{2,1,0:T(8,128)(2,1)S(1)} collective-permute-done((bf16[2,128,512]{2,1,0:T(8,128)(2,1)S(1)}, bf16[2,128,512]{2,1,0:T(8,128)(2,1)S(1)}, u32[]{:S(2)}, u32[]{:S(2)}) %collective-permute-start.35) | collective-permute-done | bytes 262176 | tf_op jit(solution)/shard_map/ppermute | solution.py:295
  292.3 2.4 assemble.1
  (56 shorter events, 8.2 us)
Async XLA Ops:
  3.0 55.6 %collective-permute-start.6 = (bf16[2,128,1280]{2,1,0:T(8,128)(2,1)}, bf16[2,128,1280]{2,1,0:T(8,128)(2,1)S(1)}, u32[]{:S(2)}, u32[]{:S(2)}) collective-permute-start(bf16[2,128,1280]{2,1,0:T(8,128)(2,1)} %get-tuple-element.43), channel_id=1, source_target_pairs={{0,1},{1,2},{2,3},{3,0},{4,5},{5,6},{6,7},{7,4},{8,9},{9,10},{10,1... | collective-permute-start | bytes 1966088 | tf_op jit(solution)/shard_map/ppermute | solution.py:295
  6.2 59.0 %collective-permute-start.7 = (bf16[2,128,1280]{2,1,0:T(8,128)(2,1)}, bf16[2,128,1280]{2,1,0:T(8,128)(2,1)S(1)}, u32[]{:S(2)}, u32[]{:S(2)}) collective-permute-start(bf16[2,128,1280]{2,1,0:T(8,128)(2,1)} %get-tuple-element.44), channel_id=1, source_target_pairs={{0,3},{1,0},{2,1},{3,2},{4,7},{5,4},{6,5},{7,6},{8,11},{9,8},{10,9... | collective-permute-start | bytes 1966088 | tf_op jit(solution)/shard_map/ppermute | solution.py:295
  10.4 41.1 %collective-permute-start.8 = (bf16[1,128,1280]{2,1,0:T(8,128)(2,1)}, bf16[1,128,1280]{2,1,0:T(8,128)(2,1)S(1)}, u32[]{:S(2)}, u32[]{:S(2)}) collective-permute-start(bf16[1,128,1280]{2,1,0:T(8,128)(2,1)} %get-tuple-element.45), channel_id=1, source_target_pairs={{0,1},{1,2},{2,3},{3,0},{4,5},{5,6},{6,7},{7,4},{8,9},{9,10},{10,1... | collective-permute-start | bytes 983048 | tf_op jit(solution)/shard_map/ppermute | solution.py:295
  11.8 39.8 %collective-permute-start.10 = (bf16[1,128,1280]{2,1,0:T(8,128)(2,1)}, bf16[1,128,1280]{2,1,0:T(8,128)(2,1)S(1)}, u32[]{:S(2)}, u32[]{:S(2)}) collective-permute-start(bf16[1,128,1280]{2,1,0:T(8,128)(2,1)} %get-tuple-element.46), channel_id=1, source_target_pairs={{0,3},{1,0},{2,1},{3,2},{4,7},{5,4},{6,5},{7,6},{8,11},{9,8},{10,9... | collective-permute-start | bytes 983048 | tf_op jit(solution)/shard_map/ppermute | solution.py:295
  51.5 17.6 %collective-permute-start.9 = (bf16[1,128,1280]{2,1,0:T(8,128)(2,1)S(1)}, bf16[1,128,1280]{2,1,0:T(8,128)(2,1)S(1)}, u32[]{:S(2)}, u32[]{:S(2)}) collective-permute-start(bf16[1,128,1280]{2,1,0:T(8,128)(2,1)S(1)} %collective-permute-done.8), channel_id=1, source_target_pairs={{0,1},{1,2},{2,3},{3,0},{4,5},{5,6},{6,7},{7,4},{8,9},{9,10},{10,1... | collective-permute-start | bytes 983048 | tf_op jit(solution)/shard_map/ppermute | solution.py:295
  51.6 20.2 %collective-permute-start.11 = (bf16[1,128,1280]{2,1,0:T(8,128)(2,1)S(1)}, bf16[1,128,1280]{2,1,0:T(8,128)(2,1)S(1)}, u32[]{:S(2)}, u32[]{:S(2)}) collective-permute-start(bf16[1,128,1280]{2,1,0:T(8,128)(2,1)S(1)} %collective-permute-done.10), channel_id=1, source_target_pairs={{0,3},{1,0},{2,1},{3,2},{4,7},{5,4},{6,5},{7,6},{8,11},{9,8},{10,9... | collective-permute-start | bytes 983048 | tf_op jit(solution)/shard_map/ppermute | solution.py:295
  58.2 21.4 %collective-permute-start.2 = (bf16[1,128,768]{2,1,0:T(8,128)(2,1)}, bf16[1,128,768]{2,1,0:T(8,128)(2,1)}, u32[]{:S(2)}, u32[]{:S(2)}) collective-permute-start(bf16[1,128,768]{2,1,0:T(8,128)(2,1)} %get-tuple-element.41), channel_id=1, source_target_pairs={{0,1},{1,2},{2,3},{3,0},{4,5},{5,6},{6,7},{7,4},{8,9},{9,10},{10,1... | collective-permute-start | bytes 589832 | tf_op jit(solution)/shard_map/ppermute | solution.py:295
  58.5 24.4 %collective-permute-start.4 = (bf16[1,128,768]{2,1,0:T(8,128)(2,1)}, bf16[1,128,768]{2,1,0:T(8,128)(2,1)}, u32[]{:S(2)}, u32[]{:S(2)}) collective-permute-start(bf16[1,128,768]{2,1,0:T(8,128)(2,1)} %get-tuple-element.42), channel_id=1, source_target_pairs={{0,3},{1,0},{2,1},{3,2},{4,7},{5,4},{6,5},{7,6},{8,11},{9,8},{10,9... | collective-permute-start | bytes 589832 | tf_op jit(solution)/shard_map/ppermute | solution.py:295
  65.2 31.7 %collective-permute-start = (bf16[2,128,768]{2,1,0:T(8,128)(2,1)}, bf16[2,128,768]{2,1,0:T(8,128)(2,1)S(1)}, u32[]{:S(2)}, u32[]{:S(2)}) collective-permute-start(bf16[2,128,768]{2,1,0:T(8,128)(2,1)} %get-tuple-element.39), channel_id=1, source_target_pairs={{0,1},{1,2},{2,3},{3,0},{4,5},{5,6},{6,7},{7,4},{8,9},{9,10},{10,1... | collective-permute-start | bytes 1179656 | tf_op jit(solution)/shard_map/ppermute | solution.py:295
  69.1 29.5 %collective-permute-start.1 = (bf16[2,128,768]{2,1,0:T(8,128)(2,1)}, bf16[2,128,768]{2,1,0:T(8,128)(2,1)}, u32[]{:S(2)}, u32[]{:S(2)}) collective-permute-start(bf16[2,128,768]{2,1,0:T(8,128)(2,1)} %get-tuple-element.40), channel_id=1, source_target_pairs={{0,3},{1,0},{2,1},{3,2},{4,7},{5,4},{6,5},{7,6},{8,11},{9,8},{10,9... | collective-permute-start | bytes 1179656 | tf_op jit(solution)/shard_map/ppermute | solution.py:295
  71.8 40.7 %collective-permute-start.22 = (bf16[3,128,512]{2,1,0:T(8,128)(2,1)}, bf16[3,128,512]{2,1,0:T(8,128)(2,1)S(1)}, u32[]{:S(2)}, u32[]{:S(2)}) collective-permute-start(bf16[3,128,512]{2,1,0:T(8,128)(2,1)} %get-tuple-element.60), channel_id=1, source_target_pairs={{0,1},{1,2},{2,3},{3,0},{4,5},{5,6},{6,7},{7,4},{8,9},{9,10},{10,1... | collective-permute-start | bytes 1179656 | tf_op jit(solution)/shard_map/ppermute | solution.py:295
  78.0 0.8 copy-start
  78.8 0.8 copy-start.2
  79.6 75.5 %collective-permute-start.12 = (bf16[2,2,128,768]{3,2,1,0:T(8,128)(2,1)}, bf16[2,2,128,768]{3,2,1,0:T(8,128)(2,1)S(1)}, u32[]{:S(2)}, u32[]{:S(2)}) collective-permute-start(bf16[2,2,128,768]{3,2,1,0:T(8,128)(2,1)} %get-tuple-element.47.hi), channel_id=1, source_target_pairs={{0,4},{1,5},{2,6},{3,7},{4,8},{5,9},{6,10},{7,11},{8,12},{9,13},{1... | collective-permute-start | bytes 2359304 | tf_op jit(solution)/shard_map/ppermute | solution.py:295
  83.0 74.8 %collective-permute-start.13 = (bf16[2,2,128,768]{3,2,1,0:T(8,128)(2,1)S(1)}, bf16[2,2,128,768]{3,2,1,0:T(8,128)(2,1)S(1)}, u32[]{:S(2)}, u32[]{:S(2)}) collective-permute-start(bf16[2,2,128,768]{3,2,1,0:T(8,128)(2,1)S(1)} %get-tuple-element.48.lo), channel_id=1, source_target_pairs={{4,0},{5,1},{6,2},{7,3},{8,4},{9,5},{10,6},{11,7},{12,8},{13,9},{1... | collective-permute-start | bytes 2359304 | tf_op jit(solution)/shard_map/ppermute | solution.py:295
  96.9 39.7 %collective-permute-start.23 = (bf16[3,128,512]{2,1,0:T(8,128)(2,1)}, bf16[3,128,512]{2,1,0:T(8,128)(2,1)S(1)}, u32[]{:S(2)}, u32[]{:S(2)}) collective-permute-start(bf16[3,128,512]{2,1,0:T(8,128)(2,1)} %get-tuple-element.61), channel_id=1, source_target_pairs={{0,3},{1,0},{2,1},{3,2},{4,7},{5,4},{6,5},{7,6},{8,11},{9,8},{10,9... | collective-permute-start | bytes 1179656 | tf_op jit(solution)/shard_map/ppermute | solution.py:295
  98.7 10.8 %collective-permute-start.3 = (bf16[1,128,768]{2,1,0:T(8,128)(2,1)}, bf16[1,128,768]{2,1,0:T(8,128)(2,1)}, u32[]{:S(2)}, u32[]{:S(2)}) collective-permute-start(bf16[1,128,768]{2,1,0:T(8,128)(2,1)} %collective-permute-done.2), channel_id=1, source_target_pairs={{0,1},{1,2},{2,3},{3,0},{4,5},{5,6},{6,7},{7,4},{8,9},{9,10},{10,1... | collective-permute-start | bytes 589832 | tf_op jit(solution)/shard_map/ppermute | solution.py:295
  109.4 73.1 %collective-permute-start.26 = (bf16[2,2,128,512]{3,2,1,0:T(8,128)(2,1)}, bf16[2,2,128,512]{3,2,1,0:T(8,128)(2,1)}, u32[]{:S(2)}, u32[]{:S(2)}) collective-permute-start(bf16[2,2,128,512]{3,2,1,0:T(8,128)(2,1)} %copy-done.2), channel_id=1, source_target_pairs={{0,4},{1,5},{2,6},{3,7},{4,8},{5,9},{6,10},{7,11},{8,12},{9,13},{1... | collective-permute-start | bytes 1572872 | tf_op jit(solution)/shard_map/ppermute | solution.py:295
  112.5 70.0 %collective-permute-start.27 = (bf16[2,2,128,512]{3,2,1,0:T(8,128)(2,1)}, bf16[2,2,128,512]{3,2,1,0:T(8,128)(2,1)}, u32[]{:S(2)}, u32[]{:S(2)}) collective-permute-start(bf16[2,2,128,512]{3,2,1,0:T(8,128)(2,1)} %copy-done), channel_id=1, source_target_pairs={{4,0},{5,1},{6,2},{7,3},{8,4},{9,5},{10,6},{11,7},{12,8},{13,9},{1... | collective-permute-start | bytes 1572872 | tf_op jit(solution)/shard_map/ppermute | solution.py:295
  136.7 16.9 %collective-permute-start.5 = (bf16[1,128,768]{2,1,0:T(8,128)(2,1)}, bf16[1,128,768]{2,1,0:T(8,128)(2,1)}, u32[]{:S(2)}, u32[]{:S(2)}) collective-permute-start(bf16[1,128,768]{2,1,0:T(8,128)(2,1)} %collective-permute-done.4), channel_id=1, source_target_pairs={{0,3},{1,0},{2,1},{3,2},{4,7},{5,4},{6,5},{7,6},{8,11},{9,8},{10,9... | collective-permute-start | bytes 589832 | tf_op jit(solution)/shard_map/ppermute | solution.py:295
  147.6 34.9 %copy-start.1 = (bf16[2,2,128,512]{3,2,1,0:T(8,128)(2,1)S(1)}, bf16[2,2,128,512]{3,2,1,0:T(8,128)(2,1)}, u32[]{:S(2)}) copy-start(bf16[2,2,128,512]{3,2,1,0:T(8,128)(2,1)} %copy-done) | copy-start | bytes 1572868
  147.6 34.9 %copy-start.3 = (bf16[2,2,128,512]{3,2,1,0:T(8,128)(2,1)S(1)}, bf16[2,2,128,512]{3,2,1,0:T(8,128)(2,1)}, u32[]{:S(2)}) copy-start(bf16[2,2,128,512]{3,2,1,0:T(8,128)(2,1)} %copy-done.2) | copy-start | bytes 1572868
  153.6 21.1 %collective-permute-start.24 = (bf16[1,128,512]{2,1,0:T(8,128)(2,1)S(1)}, bf16[1,128,512]{2,1,0:T(8,128)(2,1)S(1)}, u32[]{:S(2)}, u32[]{:S(2)}) collective-permute-start(bf16[1,128,512]{2,1,0:T(8,128)(2,1)S(1)} %slice.18), channel_id=1, source_target_pairs={{0,1},{1,2},{2,3},{3,0},{4,5},{5,6},{6,7},{7,4},{8,9},{9,10},{10,1... | collective-permute-start | bytes 393224 | tf_op jit(solution)/shard_map/ppermute | solution.py:295
  155.1 27.5 %collective-permute-start.25 = (bf16[1,128,512]{2,1,0:T(8,128)(2,1)S(1)}, bf16[1,128,512]{2,1,0:T(8,128)(2,1)S(1)}, u32[]{:S(2)}, u32[]{:S(2)}) collective-permute-start(bf16[1,128,512]{2,1,0:T(8,128)(2,1)S(1)} %slice.19), channel_id=1, source_target_pairs={{0,3},{1,0},{2,1},{3,2},{4,7},{5,4},{6,5},{7,6},{8,11},{9,8},{10,9... | collective-permute-start | bytes 393224 | tf_op jit(solution)/shard_map/ppermute | solution.py:295
  172.7 85.1 %collective-permute-start.17 = (bf16[2,2,128,768]{3,2,1,0:T(8,128)(2,1)S(1)}, bf16[2,2,128,768]{3,2,1,0:T(8,128)(2,1)S(1)}, u32[]{:S(2)}, u32[]{:S(2)}) collective-permute-start(bf16[2,2,128,768]{3,2,1,0:T(8,128)(2,1)S(1)} %get-tuple-element.54), channel_id=1, source_target_pairs={{0,4},{1,5},{2,6},{3,7},{4,8},{5,9},{6,10},{7,11},{8,12},{9,13},{1... | collective-permute-start | bytes 2359304 | tf_op jit(solution)/shard_map/ppermute | solution.py:295
  174.7 83.2 %collective-permute-start.18 = (bf16[2,2,128,768]{3,2,1,0:T(8,128)(2,1)S(1)}, bf16[2,2,128,768]{3,2,1,0:T(8,128)(2,1)S(1)}, u32[]{:S(2)}, u32[]{:S(2)}) collective-permute-start(bf16[2,2,128,768]{3,2,1,0:T(8,128)(2,1)S(1)} %get-tuple-element.55), channel_id=1, source_target_pairs={{4,0},{5,1},{6,2},{7,3},{8,4},{9,5},{10,6},{11,7},{12,8},{13,9},{1... | collective-permute-start | bytes 2359304 | tf_op jit(solution)/shard_map/ppermute | solution.py:295
  193.1 54.5 %collective-permute-start.31 = (bf16[2,2,128,512]{3,2,1,0:T(8,128)(2,1)S(1)}, bf16[2,2,128,512]{3,2,1,0:T(8,128)(2,1)S(1)}, u32[]{:S(2)}, u32[]{:S(2)}) collective-permute-start(bf16[2,2,128,512]{3,2,1,0:T(8,128)(2,1)S(1)} %get-tuple-element.69), channel_id=1, source_target_pairs={{0,4},{1,5},{2,6},{3,7},{4,8},{5,9},{6,10},{7,11},{8,12},{9,13},{1... | collective-permute-start | bytes 1572872 | tf_op jit(solution)/shard_map/ppermute | solution.py:295
  195.0 54.9 %collective-permute-start.32 = (bf16[2,2,128,512]{3,2,1,0:T(8,128)(2,1)S(1)}, bf16[2,2,128,512]{3,2,1,0:T(8,128)(2,1)S(1)}, u32[]{:S(2)}, u32[]{:S(2)}) collective-permute-start(bf16[2,2,128,512]{3,2,1,0:T(8,128)(2,1)S(1)} %get-tuple-element.70), channel_id=1, source_target_pairs={{4,0},{5,1},{6,2},{7,3},{8,4},{9,5},{10,6},{11,7},{12,8},{13,9},{1... | collective-permute-start | bytes 1572872 | tf_op jit(solution)/shard_map/ppermute | solution.py:295
  202.9 41.2 %collective-permute-start.28 = (bf16[128,512]{1,0:T(8,128)(2,1)S(1)}, bf16[128,512]{1,0:T(8,128)(2,1)S(1)}, u32[]{:S(2)}, u32[]{:S(2)}) collective-permute-start(bf16[128,512]{1,0:T(8,128)(2,1)S(1)} %get-tuple-element.65), channel_id=1, source_target_pairs={{0,1},{1,2},{2,3},{3,0},{4,5},{5,6},{6,7},{7,4},{8,9},{9,10},{10,1... | collective-permute-start | bytes 393224 | tf_op jit(solution)/shard_map/ppermute | solution.py:295
  244.0 9.0 %collective-permute-start.29 = (bf16[128,512]{1,0:T(8,128)(2,1)S(1)}, bf16[128,512]{1,0:T(8,128)(2,1)S(1)}, u32[]{:S(2)}, u32[]{:S(2)}) collective-permute-start(bf16[128,512]{1,0:T(8,128)(2,1)S(1)} %get-tuple-element.66), channel_id=1, source_target_pairs={{0,2},{1,3},{2,0},{3,1},{4,6},{5,7},{6,4},{7,5},{8,10},{9,11},{10,... | collective-permute-start | bytes 393224 | tf_op jit(solution)/shard_map/ppermute | solution.py:295
  247.5 16.3 %collective-permute-start.14 = (bf16[128,768]{1,0:T(8,128)(2,1)S(1)}, bf16[128,768]{1,0:T(8,128)(2,1)S(1)}, u32[]{:S(2)}, u32[]{:S(2)}) collective-permute-start(bf16[128,768]{1,0:T(8,128)(2,1)S(1)} %get-tuple-element.50), channel_id=1, source_target_pairs={{0,1},{1,2},{2,3},{3,0},{4,5},{5,6},{6,7},{7,4},{8,9},{9,10},{10,1... | collective-permute-start | bytes 589832 | tf_op jit(solution)/shard_map/ppermute | solution.py:295
  249.9 17.4 %collective-permute-start.15 = (bf16[128,768]{1,0:T(8,128)(2,1)S(1)}, bf16[128,768]{1,0:T(8,128)(2,1)S(1)}, u32[]{:S(2)}, u32[]{:S(2)}) collective-permute-start(bf16[128,768]{1,0:T(8,128)(2,1)S(1)} %get-tuple-element.51), channel_id=1, source_target_pairs={{0,2},{1,3},{2,0},{3,1},{4,6},{5,7},{6,4},{7,5},{8,10},{9,11},{10,... | collective-permute-start | bytes 589832 | tf_op jit(solution)/shard_map/ppermute | solution.py:295
  253.0 9.9 %collective-permute-start.30 = (bf16[128,512]{1,0:T(8,128)(2,1)S(1)}, bf16[128,512]{1,0:T(8,128)(2,1)S(1)}, u32[]{:S(2)}, u32[]{:S(2)}) collective-permute-start(bf16[128,512]{1,0:T(8,128)(2,1)S(1)} %get-tuple-element.67), channel_id=1, source_target_pairs={{0,3},{1,0},{2,1},{3,2},{4,7},{5,4},{6,5},{7,6},{8,11},{9,8},{10,9... | collective-permute-start | bytes 393224 | tf_op jit(solution)/shard_map/ppermute | solution.py:295
  257.8 15.2 %collective-permute-start.33 = (bf16[2,128,512]{2,1,0:T(8,128)(2,1)S(1)}, bf16[2,128,512]{2,1,0:T(8,128)(2,1)S(1)}, u32[]{:S(2)}, u32[]{:S(2)}) collective-permute-start(bf16[2,128,512]{2,1,0:T(8,128)(2,1)S(1)} %get-tuple-element.72), channel_id=1, source_target_pairs={{0,1},{1,2},{2,3},{3,0},{4,5},{5,6},{6,7},{7,4},{8,9},{9,10},{10,1... | collective-permute-start | bytes 786440 | tf_op jit(solution)/shard_map/ppermute | solution.py:295
  257.8 11.8 %collective-permute-start.16 = (bf16[128,768]{1,0:T(8,128)(2,1)S(1)}, bf16[128,768]{1,0:T(8,128)(2,1)S(1)}, u32[]{:S(2)}, u32[]{:S(2)}) collective-permute-start(bf16[128,768]{1,0:T(8,128)(2,1)S(1)} %get-tuple-element.52), channel_id=1, source_target_pairs={{0,3},{1,0},{2,1},{3,2},{4,7},{5,4},{6,5},{7,6},{8,11},{9,8},{10,9... | collective-permute-start | bytes 589832 | tf_op jit(solution)/shard_map/ppermute | solution.py:295
  262.9 29.4 %collective-permute-start.19 = (bf16[2,128,768]{2,1,0:T(8,128)(2,1)S(1)}, bf16[2,128,768]{2,1,0:T(8,128)(2,1)S(1)}, u32[]{:S(2)}, u32[]{:S(2)}) collective-permute-start(bf16[2,128,768]{2,1,0:T(8,128)(2,1)S(1)} %get-tuple-element.57), channel_id=1, source_target_pairs={{0,1},{1,2},{2,3},{3,0},{4,5},{5,6},{6,7},{7,4},{8,9},{9,10},{10,1... | collective-permute-start | bytes 1179656 | tf_op jit(solution)/shard_map/ppermute | solution.py:295
  263.8 28.5 %collective-permute-start.20 = (bf16[2,128,768]{2,1,0:T(8,128)(2,1)S(1)}, bf16[2,128,768]{2,1,0:T(8,128)(2,1)S(1)}, u32[]{:S(2)}, u32[]{:S(2)}) collective-permute-start(bf16[2,128,768]{2,1,0:T(8,128)(2,1)S(1)} %get-tuple-element.58), channel_id=1, source_target_pairs={{0,2},{1,3},{2,0},{3,1},{4,6},{5,7},{6,4},{7,5},{8,10},{9,11},{10,... | collective-permute-start | bytes 1179656 | tf_op jit(solution)/shard_map/ppermute | solution.py:295
  267.3 25.0 %collective-permute-start.21 = (bf16[2,128,768]{2,1,0:T(8,128)(2,1)S(1)}, bf16[2,128,768]{2,1,0:T(8,128)(2,1)S(1)}, u32[]{:S(2)}, u32[]{:S(2)}) collective-permute-start(bf16[2,128,768]{2,1,0:T(8,128)(2,1)S(1)} %get-tuple-element.59), channel_id=1, source_target_pairs={{0,3},{1,0},{2,1},{3,2},{4,7},{5,4},{6,5},{7,6},{8,11},{9,8},{10,9... | collective-permute-start | bytes 1179656 | tf_op jit(solution)/shard_map/ppermute | solution.py:295
  269.6 18.6 %collective-permute-start.34 = (bf16[2,128,512]{2,1,0:T(8,128)(2,1)S(1)}, bf16[2,128,512]{2,1,0:T(8,128)(2,1)S(1)}, u32[]{:S(2)}, u32[]{:S(2)}) collective-permute-start(bf16[2,128,512]{2,1,0:T(8,128)(2,1)S(1)} %get-tuple-element.73), channel_id=1, source_target_pairs={{0,2},{1,3},{2,0},{3,1},{4,6},{5,7},{6,4},{7,5},{8,10},{9,11},{10,... | collective-permute-start | bytes 786440 | tf_op jit(solution)/shard_map/ppermute | solution.py:295
  273.1 19.2 %collective-permute-start.35 = (bf16[2,128,512]{2,1,0:T(8,128)(2,1)S(1)}, bf16[2,128,512]{2,1,0:T(8,128)(2,1)S(1)}, u32[]{:S(2)}, u32[]{:S(2)}) collective-permute-start(bf16[2,128,512]{2,1,0:T(8,128)(2,1)S(1)} %get-tuple-element.74), channel_id=1, source_target_pairs={{0,3},{1,0},{2,1},{3,2},{4,7},{5,4},{6,5},{7,6},{8,11},{9,8},{10,9... | collective-permute-start | bytes 786440 | tf_op jit(solution)/shard_map/ppermute | solution.py:295

commit v7 on v6

--- a/solution.py
+++ b/solution.py
@@ -11,7 +11,7 @@
 BLK = 128
 HD = 128
 NZ = 4
-CHUNKS = ((0, 6), (6, 4))
+CHUNKS = ((0, 4), (4, 6))
 CW = 256
 SCALE = 1.0 / math.sqrt(HD)
 EXP2_SCALE = SCALE / math.log(2.0)
@@ -198,18 +198,18 @@
     )(zh, q, g, *recv, before, lo, hi, after, bias)
 
 
-def finish_body(zh, own, from_before, from_after, o0, o1, o2, o3):
+def finish_body(zh, own, before, before_seam, after, after_seam, o0, o1, o2, o3):
     z = zh[0]
     for s, o in enumerate((o0, o1, o2, o3)):
         b = lax.rem(z + s, NZ)
 
         @pl.when(b < 2)
         def _():
-            o[...] = (own[b] + from_before[b].astype(F32)).astype(BF)
+            o[...] = (own[b] + (before[b].astype(F32) + before_seam[b].astype(F32))).astype(BF)
 
         @pl.when(b >= 2)
         def _():
-            o[...] = (own[b] + from_after[b - 2].astype(F32)).astype(BF)
+            o[...] = (own[b] + (after[b - 2].astype(F32) + after_seam[b - 2].astype(F32))).astype(BF)
 
 
 def finish(zh, own, from_before, from_after):
@@ -221,13 +221,13 @@
         grid_spec=pltpu.PrefetchScalarGridSpec(
             num_scalar_prefetch=1,
             grid=(n // CW,),
-            in_specs=[pl.BlockSpec((4, 2, BLK, CW), lambda i, z: (0, 0, 0, i)), rim, rim],
+            in_specs=[pl.BlockSpec((4, 2, BLK, CW), lambda i, z: (0, 0, 0, i)), rim, rim, rim, rim],
             out_specs=[out] * 4,
         ),
         out_shape=[jax.ShapeDtypeStruct((2, BLK, n), BF)] * 4,
         cost_estimate=cost(0, 32 * BLK * n * 2),
-        compiler_params=grant(12),
-    )(zh, own, from_before, from_after)
+        compiler_params=grant(14),
+    )(zh, own, *from_before, *from_after)
 
 
 def assemble_body(zh, *refs):
@@ -290,6 +290,10 @@
     ]
     up = [(NZ * i + j, NZ * (i + 1) + j) for i in range(n_slabs - 1) for j in range(NZ)]
     down = [(b, a) for a, b in up]
+    seam = n_slabs // 2 - 1
+    low, high = ([NZ * (seam + i) + j for j in range(NZ)] for i in range(2))
+    via_up = [3 * n_uly + NZ + j for j in range(NZ)]
+    via_down = [12 * n_uly + 2 * NZ + j for j in range(NZ)]
 
     def move(axes, perm, a):
         return lax.ppermute(a, axes, perm)
@@ -302,6 +306,12 @@
 
     def to_prev(a):
         return move(("ctx", "uly"), down, a)
+
+    def rim_move(perm, first, via, last, a):
+        both = ("ctx", "uly")
+        direct = move(both, [p for p in perm if p[0] not in first], a)
+        hop = move(both, list(zip(first, via)), a)
+        return direct, move(both, list(zip(via, last)), hop)
 
     key, value, query, dout = (pltpu.with_memory_space_constraint(a, pltpu.HBM) for a in (key, value, query, dout))
     bias = tile_bias(tile_mask, zh_s, slab, group)
@@ -328,7 +338,8 @@
         *dq, rim_before, rim_after, own = attend(
             zh, query, dout, recv, before, lo, hi, after, bias, first, heads, group
         )
-        from_after, from_before = to_prev(rim_before), to_next(rim_after)
+        from_after = rim_move(down, high, via_down, low, rim_before)
+        from_before = rim_move(up, low, via_up, high, rim_after)
         back_q = [dq[0], *around(dq[1:])]
         dkv = finish(zh, own, from_before, from_after)
         back_kv = [dkv[0], *around(dkv[1:])]

time: 296 us -> 348 us (1.18)
  the two profiles are of different devices: /device:TPU:32 before, /device:TPU:90 now
where the time goes in v7:
time: 348 us; the launch traced here: 347 us
  waiting for transfers between devices  197 us (57%)
  starting transfers between devices  94.1 us (27%)
  Pallas kernels  45.2 us (13%)
  local copies, waits for them, and re-layouts  8.8 us (3%)
    ppermute x44, waiting for transfers between devices, move(): return lax.ppermute(a, axes, perm)  197 us
    ppermute x44, starting transfers between devices, move(): return lax.ppermute(a, axes, perm)  94.1 us
    pallas_call x2, Pallas kernels, attend(): pl.pallas_call(attend_body, grid_spec=pltpu.PrefetchScalarGridSpec(num_sc...  25.5 us
    pallas_call x5, Pallas kernels, pack(): pl.pallas_call(pack_body, grid_spec=pltpu.PrefetchScalarGridSpec(num_scal...  10.8 us
  transfers between devices with their start and end apart: 44, of which 11 were waited for; matrix products, arithmetic and copies ran while one was open for 2% of the time, Pallas kernels for 12%

profile of v7, /device:TPU:90, one launch (start us, length us, event | category | flops | bytes accessed | tf_op | source)
XLA Modules:
  0.0 346.8 jit_solution(6225358495397305453)
XLA Ops:
  0.6 2.3 shard_map.78
  3.0 4.5 %collective-permute-start.6 = (bf16[2,128,1280]{2,1,0:T(8,128)(2,1)}, bf16[2,128,1280]{2,1,0:T(8,128)(2,1)S(1)}, u32[]{:S(2)}, u32[]{:S(2)}) collective-permute-start(bf16[2,128,1280]{2,1,0:T(8,128)(2,1)} %get-tuple-element.43), channel_id=1, source_target_pairs={{0,1},{1,2},{2,3},{3,0},{4,5},{5,6},{6,7},{7,4},{8,9},{9,10},{10,1... | collective-permute-start | bytes 1966088 | tf_op jit(solution)/shard_map/ppermute | solution.py:299
  7.5 1.9 shard_map.79
  9.4 1.5 collective-permute-start.10
  10.9 2.6 collective-permute-start.8
  13.5 1.6 shard_map.77
  15.2 2.9 collective-permute-start.2
  18.0 37.3 %collective-permute-done.2 = bf16[1,128,512]{2,1,0:T(8,128)(2,1)S(1)} collective-permute-done((bf16[1,128,512]{2,1,0:T(8,128)(2,1)}, bf16[1,128,512]{2,1,0:T(8,128)(2,1)S(1)}, u32[]{:S(2)}, u32[]{:S(2)}) %collective-permute-start.2) | collective-permute-done | bytes 131104 | tf_op jit(solution)/shard_map/ppermute | solution.py:299
  56.0 4.2 %collective-permute-start.11 = (bf16[1,128,1280]{2,1,0:T(8,128)(2,1)}, bf16[1,128,1280]{2,1,0:T(8,128)(2,1)S(1)}, u32[]{:S(2)}, u32[]{:S(2)}) collective-permute-start(bf16[1,128,1280]{2,1,0:T(8,128)(2,1)} %collective-permute-done.10), channel_id=1, source_target_pairs={{0,3},{1,0},{2,1},{3,2},{4,7},{5,4},{6,5},{7,6},{8,11},{9,8},{10,9... | collective-permute-start | bytes 983048 | tf_op jit(solution)/shard_map/ppermute | solution.py:299
  60.3 3.2 shard_map.82
  63.4 17.5 %collective-permute-done.4 = bf16[1,128,512]{2,1,0:T(8,128)(2,1)S(1)} collective-permute-done((bf16[1,128,512]{2,1,0:T(8,128)(2,1)}, bf16[1,128,512]{2,1,0:T(8,128)(2,1)S(1)}, u32[]{:S(2)}, u32[]{:S(2)}) %collective-permute-start.4) | collective-permute-done | bytes 131104 | tf_op jit(solution)/shard_map/ppermute | solution.py:299
  81.0 5.4 %collective-permute-start.26 = (bf16[3,128,768]{2,1,0:T(8,128)(2,1)}, bf16[3,128,768]{2,1,0:T(8,128)(2,1)S(1)}, u32[]{:S(2)}, u32[]{:S(2)}) collective-permute-start(bf16[3,128,768]{2,1,0:T(8,128)(2,1)} %get-tuple-element.60), channel_id=1, source_target_pairs={{0,1},{1,2},{2,3},{3,0},{4,5},{5,6},{6,7},{7,4},{8,9},{9,10},{10,1... | collective-permute-start | bytes 1769480 | tf_op jit(solution)/shard_map/ppermute | solution.py:299
  86.8 2.6 collective-permute-start.27
  89.3 1.8 shard_map.76
  91.1 1.7 collective-permute-start
  92.8 5.4 %collective-permute-done.11.fm = bf16[1,128,1280]{2,1,0:T(8,128)(2,1)S(1)} collective-permute-done((bf16[1,128,1280]{2,1,0:T(8,128)(2,1)}, bf16[1,128,1280]{2,1,0:T(8,128)(2,1)S(1)}, u32[]{:S(2)}, u32[]{:S(2)}) %collective-permute-start.11) | collective-permute-done | bytes 327712 | tf_op jit(solution)/shard_map/ppermute | solution.py:299
  98.3 16.3 %collective-permute-done.9.fp = bf16[1,128,1280]{2,1,0:T(8,128)(2,1)S(1)} collective-permute-done((bf16[1,128,1280]{2,1,0:T(8,128)(2,1)}, bf16[1,128,1280]{2,1,0:T(8,128)(2,1)S(1)}, u32[]{:S(2)}, u32[]{:S(2)}) %collective-permute-start.9) | collective-permute-done | bytes 327712 | tf_op jit(solution)/shard_map/ppermute | solution.py:299
  114.6 2.4 collective-permute-start.3
  117.1 4.3 %unpack.1 = (bf16[2,2,128,512]{3,2,1,0:T(8,128)(2,1)}, bf16[2,2,128,512]{3,2,1,0:T(8,128)(2,1)}, bf16[2,2,128,768]{3,2,1,0:T(8,128)(2,1)}, bf16[2,2,128,768]{3,2,1,0:T(8,128)(2,1)}) custom-call(s32[1]{0:T(128)} %bitcast.zh, bf16[128,5120]{1,0:T(8,128)(2,1)} %k.1, bf16[128,5120]{1,0:T(8,128)(2,1)} %v.1, bf16[2,128,1280]{2,1,0:T(8,128)(2,1)S(1)} %collective-permute-done.6.mp, ...), custom_call_target="tpu_custom_call" | custom-call | bytes 5242880 | tf_op jit(solution)/shard_map/unpack/pallas_call | solution.py:98
  121.4 3.4 collective-permute-start.30
  124.8 2.4 collective-permute-start.31
  127.2 3.4 collective-permute-start.12
  130.6 2.8 collective-permute-start.13
  136.9 5.2 %collective-permute-done.5.fm = bf16[1,128,512]{2,1,0:T(8,128)(2,1)S(1)} collective-permute-done((bf16[1,128,512]{2,1,0:T(8,128)(2,1)}, bf16[1,128,512]{2,1,0:T(8,128)(2,1)S(1)}, u32[]{:S(2)}, u32[]{:S(2)}) %collective-permute-start.5) | collective-permute-done | bytes 131104 | tf_op jit(solution)/shard_map/ppermute | solution.py:299
  143.4 10.4 %collective-permute-done.12.before = bf16[2,2,128,512]{3,2,1,0:T(8,128)(2,1)} collective-permute-done((bf16[2,2,128,512]{3,2,1,0:T(8,128)(2,1)}, bf16[2,2,128,512]{3,2,1,0:T(8,128)(2,1)}, u32[]{:S(2)}, u32[]{:S(2)}) %collective-permute-start.12) | collective-permute-done | bytes 524320 | tf_op jit(solution)/shard_map/ppermute | solution.py:299
  155.7 1.7 broadcast_in_dim.17
  157.3 1.7 reshape.61
  160.9 10.4 %shard_map.80 = (bf16[128,512]{1,0:T(8,128)(2,1)S(1)}, bf16[128,512]{1,0:T(8,128)(2,1)S(1)}, bf16[128,512]{1,0:T(8,128)(2,1)S(1)}, bf16[128,512]{1,0:T(8,128)(2,...) custom-call(s32[1]{0:T(128)} %bitcast.zh, ...), custom_call_target="tpu_custom_call" | custom-call | flops 2013265920 | bytes 5242880 | tf_op jit(solution)/shard_map/pallas_call | solution.py:175
  172.7 3.2 collective-permute-start.14
  175.9 15.1 %shard_map.83 = (bf16[128,768]{1,0:T(8,128)(2,1)S(1)}, bf16[128,768]{1,0:T(8,128)(2,1)S(1)}, bf16[128,768]{1,0:T(8,128)(2,1)S(1)}, bf16[128,768]{1,0:T(8,128)(2,...) custom-call(s32[1]{0:T(128)} %bitcast.zh, ...), custom_call_target="tpu_custom_call" | custom-call | flops 3019898880 | bytes 7864320 | tf_op jit(solution)/shard_map/pallas_call | solution.py:175
  192.4 3.1 collective-permute-start.15
  195.6 6.9 %collective-permute-done.15.refs_2_ = bf16[128,512]{1,0:T(8,128)(2,1)S(1)} collective-permute-done((bf16[128,512]{1,0:T(8,128)(2,1)S(1)}, bf16[128,512]{1,0:T(8,128)(2,1)S(1)}, u32[]{:S(2)}, u32[]{:S(2)}) %collective-permute-start.15) | collective-permute-done | bytes 131104 | tf_op jit(solution)/shard_map/ppermute | solution.py:299
  202.4 3.4 collective-permute-start.35
  205.8 8.4 %collective-permute-start.17 = (bf16[2,2,128,512]{3,2,1,0:T(8,128)(2,1)S(1)}, bf16[2,2,128,512]{3,2,1,0:T(8,128)(2,1)S(1)}, u32[]{:S(2)}, u32[]{:S(2)}) collective-permute-start(bf16[2,2,128,512]{3,2,1,0:T(8,128)(2,1)S(1)} %get-tuple-element.54), channel_id=1, source_target_pairs={{0,4},{1,5},{2,6},{3,7},{4,8},{5,9},{6,10},{7,11},{8,12},{9,13},{1... | collective-permute-start | bytes 1572872 | tf_op jit(solution)/shard_map/ppermute | solution.py:299
  214.3 1.9 collective-permute-start.20
  216.2 17.7 %collective-permute-done.17.before = bf16[2,2,128,512]{3,2,1,0:T(8,128)(2,1)S(1)} collective-permute-done((bf16[2,2,128,512]{3,2,1,0:T(8,128)(2,1)S(1)}, bf16[2,2,128,512]{3,2,1,0:T(8,128)(2,1)S(1)}, u32[]{:S(2)}, u32[]{:S(2)}) %collective-permute-start.17) | collective-permute-done | bytes 524320 | tf_op jit(solution)/shard_map/ppermute | solution.py:299
  233.9 7.6 %collective-permute-start.38 = (bf16[2,2,128,768]{3,2,1,0:T(8,128)(2,1)S(1)}, bf16[2,2,128,768]{3,2,1,0:T(8,128)(2,1)S(1)}, u32[]{:S(2)}, u32[]{:S(2)}) collective-permute-start(bf16[2,2,128,768]{3,2,1,0:T(8,128)(2,1)S(1)} %get-tuple-element.70), channel_id=1, source_target_pairs={{4,0},{5,1},{6,2},{7,3},{8,4},{9,5},{10,6},{11,7},{12,8},{13,9},{1... | collective-permute-start | bytes 2359304 | tf_op jit(solution)/shard_map/ppermute | solution.py:299
  244.5 3.0 collective-permute-start.33
  248.4 10.9 %collective-permute-done.38.after = bf16[2,2,128,768]{3,2,1,0:T(8,128)(2,1)S(1)} collective-permute-done((bf16[2,2,128,768]{3,2,1,0:T(8,128)(2,1)S(1)}, bf16[2,2,128,768]{3,2,1,0:T(8,128)(2,1)S(1)}, u32[]{:S(2)}, u32[]{:S(2)}) %collective-permute-start.38) | collective-permute-done | bytes 786464 | tf_op jit(solution)/shard_map/ppermute | solution.py:299
  259.3 4.1 %collective-permute-start.23 = (bf16[2,128,512]{2,1,0:T(8,128)(2,1)S(1)}, bf16[2,128,512]{2,1,0:T(8,128)(2,1)S(1)}, u32[]{:S(2)}, u32[]{:S(2)}) collective-permute-start(bf16[2,128,512]{2,1,0:T(8,128)(2,1)S(1)} %get-tuple-element.57), channel_id=1, source_target_pairs={{0,1},{1,2},{2,3},{3,0},{4,5},{5,6},{6,7},{7,4},{8,9},{9,10},{10,1... | collective-permute-start | bytes 786440 | tf_op jit(solution)/shard_map/ppermute | solution.py:299
  264.7 38.7 %collective-permute-done.16.refs_3_ = bf16[128,512]{1,0:T(8,128)(2,1)S(1)} collective-permute-done((bf16[128,512]{1,0:T(8,128)(2,1)S(1)}, bf16[128,512]{1,0:T(8,128)(2,1)S(1)}, u32[]{:S(2)}, u32[]{:S(2)}) %collective-permute-start.16) | collective-permute-done | bytes 131104 | tf_op jit(solution)/shard_map/ppermute | solution.py:299
  303.4 2.3 collective-permute-start.41
  305.7 1.6 collective-permute-start.42
  307.3 1.4 collective-permute-start.43
  308.7 3.6 %collective-permute-start.24 = (bf16[2,128,512]{2,1,0:T(8,128)(2,1)S(1)}, bf16[2,128,512]{2,1,0:T(8,128)(2,1)S(1)}, u32[]{:S(2)}, u32[]{:S(2)}) collective-permute-start(bf16[2,128,512]{2,1,0:T(8,128)(2,1)S(1)} %get-tuple-element.58), channel_id=1, source_target_pairs={{0,2},{1,3},{2,0},{3,1},{4,6},{5,7},{6,4},{7,5},{8,10},{9,11},{10,... | collective-permute-start | bytes 786440 | tf_op jit(solution)/shard_map/ppermute | solution.py:299
  312.3 1.6 collective-permute-start.25
  313.8 30.5 %collective-permute-done.24.refs_6_ = bf16[2,128,512]{2,1,0:T(8,128)(2,1)S(1)} collective-permute-done((bf16[2,128,512]{2,1,0:T(8,128)(2,1)S(1)}, bf16[2,128,512]{2,1,0:T(8,128)(2,1)S(1)}, u32[]{:S(2)}, u32[]{:S(2)}) %collective-permute-start.24) | collective-permute-done | bytes 262176 | tf_op jit(solution)/shard_map/ppermute | solution.py:299
  344.4 2.4 assemble.1
  (72 shorter events, 17.6 us)
Async XLA Ops:
  3.0 83.8 %collective-permute-start.6 = (bf16[2,128,1280]{2,1,0:T(8,128)(2,1)}, bf16[2,128,1280]{2,1,0:T(8,128)(2,1)S(1)}, u32[]{:S(2)}, u32[]{:S(2)}) collective-permute-start(bf16[2,128,1280]{2,1,0:T(8,128)(2,1)} %get-tuple-element.43), channel_id=1, source_target_pairs={{0,1},{1,2},{2,3},{3,0},{4,5},{5,6},{6,7},{7,4},{8,9},{9,10},{10,1... | collective-permute-start | bytes 1966088 | tf_op jit(solution)/shard_map/ppermute | solution.py:299
  7.5 83.7 %collective-permute-start.7 = (bf16[2,128,1280]{2,1,0:T(8,128)(2,1)}, bf16[2,128,1280]{2,1,0:T(8,128)(2,1)S(1)}, u32[]{:S(2)}, u32[]{:S(2)}) collective-permute-start(bf16[2,128,1280]{2,1,0:T(8,128)(2,1)} %get-tuple-element.44), channel_id=1, source_target_pairs={{0,3},{1,0},{2,1},{3,2},{4,7},{5,4},{6,5},{7,6},{8,11},{9,8},{10,9... | collective-permute-start | bytes 1966088 | tf_op jit(solution)/shard_map/ppermute | solution.py:299
  9.4 46.6 %collective-permute-start.10 = (bf16[1,128,1280]{2,1,0:T(8,128)(2,1)}, bf16[1,128,1280]{2,1,0:T(8,128)(2,1)}, u32[]{:S(2)}, u32[]{:S(2)}) collective-permute-start(bf16[1,128,1280]{2,1,0:T(8,128)(2,1)} %get-tuple-element.46), channel_id=1, source_target_pairs={{0,3},{1,0},{2,1},{3,2},{4,7},{5,4},{6,5},{7,6},{8,11},{9,8},{10,9... | collective-permute-start | bytes 983048 | tf_op jit(solution)/shard_map/ppermute | solution.py:299
  10.9 75.5 %collective-permute-start.8 = (bf16[1,128,1280]{2,1,0:T(8,128)(2,1)}, bf16[1,128,1280]{2,1,0:T(8,128)(2,1)}, u32[]{:S(2)}, u32[]{:S(2)}) collective-permute-start(bf16[1,128,1280]{2,1,0:T(8,128)(2,1)} %get-tuple-element.45), channel_id=1, source_target_pairs={{0,1},{1,2},{2,3},{3,0},{4,5},{5,6},{6,7},{7,4},{8,9},{9,10},{10,1... | collective-permute-start | bytes 983048 | tf_op jit(solution)/shard_map/ppermute | solution.py:299
  15.2 40.2 %collective-permute-start.2 = (bf16[1,128,512]{2,1,0:T(8,128)(2,1)}, bf16[1,128,512]{2,1,0:T(8,128)(2,1)S(1)}, u32[]{:S(2)}, u32[]{:S(2)}) collective-permute-start(bf16[1,128,512]{2,1,0:T(8,128)(2,1)} %get-tuple-element.41), channel_id=1, source_target_pairs={{0,1},{1,2},{2,3},{3,0},{4,5},{5,6},{6,7},{7,4},{8,9},{9,10},{10,1... | collective-permute-start | bytes 393224 | tf_op jit(solution)/shard_map/ppermute | solution.py:299
  55.4 0.6 copy-start.3
  55.4 25.6 %collective-permute-start.4 = (bf16[1,128,512]{2,1,0:T(8,128)(2,1)}, bf16[1,128,512]{2,1,0:T(8,128)(2,1)S(1)}, u32[]{:S(2)}, u32[]{:S(2)}) collective-permute-start(bf16[1,128,512]{2,1,0:T(8,128)(2,1)} %get-tuple-element.42), channel_id=1, source_target_pairs={{0,3},{1,0},{2,1},{3,2},{4,7},{5,4},{6,5},{7,6},{8,11},{9,8},{10,9... | collective-permute-start | bytes 393224 | tf_op jit(solution)/shard_map/ppermute | solution.py:299
  56.0 42.1 %collective-permute-start.11 = (bf16[1,128,1280]{2,1,0:T(8,128)(2,1)}, bf16[1,128,1280]{2,1,0:T(8,128)(2,1)S(1)}, u32[]{:S(2)}, u32[]{:S(2)}) collective-permute-start(bf16[1,128,1280]{2,1,0:T(8,128)(2,1)} %collective-permute-done.10), channel_id=1, source_target_pairs={{0,3},{1,0},{2,1},{3,2},{4,7},{5,4},{6,5},{7,6},{8,11},{9,8},{10,9... | collective-permute-start | bytes 983048 | tf_op jit(solution)/shard_map/ppermute | solution.py:299
  81.0 5.8 %copy-start.2 = (bf16[1,128,512]{2,1,0:T(8,128)(2,1)}, bf16[1,128,512]{2,1,0:T(8,128)(2,1)S(1)}, u32[]{:S(2)}) copy-start(bf16[1,128,512]{2,1,0:T(8,128)(2,1)S(1)} %collective-permute-done.4) | copy-start | bytes 393220
  81.0 49.7 %collective-permute-start.26 = (bf16[3,128,768]{2,1,0:T(8,128)(2,1)}, bf16[3,128,768]{2,1,0:T(8,128)(2,1)S(1)}, u32[]{:S(2)}, u32[]{:S(2)}) collective-permute-start(bf16[3,128,768]{2,1,0:T(8,128)(2,1)} %get-tuple-element.60), channel_id=1, source_target_pairs={{0,1},{1,2},{2,3},{3,0},{4,5},{5,6},{6,7},{7,4},{8,9},{9,10},{10,1... | collective-permute-start | bytes 1769480 | tf_op jit(solution)/shard_map/ppermute | solution.py:299
  86.4 28.3 %collective-permute-start.9 = (bf16[1,128,1280]{2,1,0:T(8,128)(2,1)}, bf16[1,128,1280]{2,1,0:T(8,128)(2,1)S(1)}, u32[]{:S(2)}, u32[]{:S(2)}) collective-permute-start(bf16[1,128,1280]{2,1,0:T(8,128)(2,1)} %collective-permute-done.8), channel_id=1, source_target_pairs={{0,1},{1,2},{2,3},{3,0},{4,5},{5,6},{6,7},{7,4},{8,9},{9,10},{10,1... | collective-permute-start | bytes 983048 | tf_op jit(solution)/shard_map/ppermute | solution.py:299
  86.8 47.8 %collective-permute-start.27 = (bf16[3,128,768]{2,1,0:T(8,128)(2,1)}, bf16[3,128,768]{2,1,0:T(8,128)(2,1)S(1)}, u32[]{:S(2)}, u32[]{:S(2)}) collective-permute-start(bf16[3,128,768]{2,1,0:T(8,128)(2,1)} %get-tuple-element.61), channel_id=1, source_target_pairs={{0,3},{1,0},{2,1},{3,2},{4,7},{5,4},{6,5},{7,6},{8,11},{9,8},{10,9... | collective-permute-start | bytes 1769480 | tf_op jit(solution)/shard_map/ppermute | solution.py:299
  91.1 30.2 %collective-permute-start = (bf16[2,128,512]{2,1,0:T(8,128)(2,1)}, bf16[2,128,512]{2,1,0:T(8,128)(2,1)S(1)}, u32[]{:S(2)}, u32[]{:S(2)}) collective-permute-start(bf16[2,128,512]{2,1,0:T(8,128)(2,1)} %get-tuple-element.39), channel_id=1, source_target_pairs={{0,1},{1,2},{2,3},{3,0},{4,5},{5,6},{6,7},{7,4},{8,9},{9,10},{10,1... | collective-permute-start | bytes 786440 | tf_op jit(solution)/shard_map/ppermute | solution.py:299
  98.1 26.6 %collective-permute-start.1 = (bf16[2,128,512]{2,1,0:T(8,128)(2,1)}, bf16[2,128,512]{2,1,0:T(8,128)(2,1)}, u32[]{:S(2)}, u32[]{:S(2)}) collective-permute-start(bf16[2,128,512]{2,1,0:T(8,128)(2,1)} %get-tuple-element.40), channel_id=1, source_target_pairs={{0,3},{1,0},{2,1},{3,2},{4,7},{5,4},{6,5},{7,6},{8,11},{9,8},{10,9... | collective-permute-start | bytes 786440 | tf_op jit(solution)/shard_map/ppermute | solution.py:299
  114.6 12.6 %collective-permute-start.3 = (bf16[1,128,512]{2,1,0:T(8,128)(2,1)}, bf16[1,128,512]{2,1,0:T(8,128)(2,1)S(1)}, u32[]{:S(2)}, u32[]{:S(2)}) collective-permute-start(bf16[1,128,512]{2,1,0:T(8,128)(2,1)} %copy-done.3), channel_id=1, source_target_pairs={{0,1},{1,2},{2,3},{3,0},{4,5},{5,6},{6,7},{7,4},{8,9},{9,10},{10,1... | collective-permute-start | bytes 393224 | tf_op jit(solution)/shard_map/ppermute | solution.py:299
  121.4 54.5 %collective-permute-start.30 = (bf16[2,2,128,768]{3,2,1,0:T(8,128)(2,1)}, bf16[2,2,128,768]{3,2,1,0:T(8,128)(2,1)S(1)}, u32[]{:S(2)}, u32[]{:S(2)}) collective-permute-start(bf16[2,2,128,768]{3,2,1,0:T(8,128)(2,1)} %get-tuple-element.62.hi), channel_id=1, source_target_pairs={{0,4},{1,5},{2,6},{3,7},{4,8},{5,9},{6,10},{7,11},{8,12},{9,13},{1... | collective-permute-start | bytes 2359304 | tf_op jit(solution)/shard_map/ppermute | solution.py:299
  124.8 51.1 %collective-permute-start.31 = (bf16[2,2,128,768]{3,2,1,0:T(8,128)(2,1)}, bf16[2,2,128,768]{3,2,1,0:T(8,128)(2,1)S(1)}, u32[]{:S(2)}, u32[]{:S(2)}) collective-permute-start(bf16[2,2,128,768]{3,2,1,0:T(8,128)(2,1)} %get-tuple-element.63.lo), channel_id=1, source_target_pairs={{4,0},{5,1},{6,2},{7,3},{8,4},{9,5},{10,6},{11,7},{12,8},{13,9},{1... | collective-permute-start | bytes 2359304 | tf_op jit(solution)/shard_map/ppermute | solution.py:299
  127.2 26.6 %collective-permute-start.12 = (bf16[2,2,128,512]{3,2,1,0:T(8,128)(2,1)}, bf16[2,2,128,512]{3,2,1,0:T(8,128)(2,1)}, u32[]{:S(2)}, u32[]{:S(2)}) collective-permute-start(bf16[2,2,128,512]{3,2,1,0:T(8,128)(2,1)} %get-tuple-element.47.hi), channel_id=1, source_target_pairs={{0,4},{1,5},{2,6},{3,7},{4,8},{5,9},{6,10},{7,11},{8,12},{9,13},{1... | collective-permute-start | bytes 1572872 | tf_op jit(solution)/shard_map/ppermute | solution.py:299
  130.6 29.3 %collective-permute-start.13 = (bf16[2,2,128,512]{3,2,1,0:T(8,128)(2,1)}, bf16[2,2,128,512]{3,2,1,0:T(8,128)(2,1)}, u32[]{:S(2)}, u32[]{:S(2)}) collective-permute-start(bf16[2,2,128,512]{3,2,1,0:T(8,128)(2,1)} %get-tuple-element.48.lo), channel_id=1, source_target_pairs={{4,0},{5,1},{6,2},{7,3},{8,4},{9,5},{10,6},{11,7},{12,8},{13,9},{1... | collective-permute-start | bytes 1572872 | tf_op jit(solution)/shard_map/ppermute | solution.py:299
  134.5 7.5 %collective-permute-start.5 = (bf16[1,128,512]{2,1,0:T(8,128)(2,1)}, bf16[1,128,512]{2,1,0:T(8,128)(2,1)S(1)}, u32[]{:S(2)}, u32[]{:S(2)}) collective-permute-start(bf16[1,128,512]{2,1,0:T(8,128)(2,1)} %copy-done.2), channel_id=1, source_target_pairs={{0,3},{1,0},{2,1},{3,2},{4,7},{5,4},{6,5},{7,6},{8,11},{9,8},{10,9... | collective-permute-start | bytes 393224 | tf_op jit(solution)/shard_map/ppermute | solution.py:299
  142.1 0.7 copy-start
  142.7 29.2 %collective-permute-start.28 = (bf16[1,128,768]{2,1,0:T(8,128)(2,1)}, bf16[1,128,768]{2,1,0:T(8,128)(2,1)S(1)}, u32[]{:S(2)}, u32[]{:S(2)}) collective-permute-start(bf16[1,128,768]{2,1,0:T(8,128)(2,1)} %slice.18), channel_id=1, source_target_pairs={{0,1},{1,2},{2,3},{3,0},{4,5},{5,6},{6,7},{7,4},{8,9},{9,10},{10,1... | collective-permute-start | bytes 589832 | tf_op jit(solution)/shard_map/ppermute | solution.py:299
  153.8 18.9 %collective-permute-start.29 = (bf16[1,128,768]{2,1,0:T(8,128)(2,1)}, bf16[1,128,768]{2,1,0:T(8,128)(2,1)S(1)}, u32[]{:S(2)}, u32[]{:S(2)}) collective-permute-start(bf16[1,128,768]{2,1,0:T(8,128)(2,1)} %slice.19), channel_id=1, source_target_pairs={{0,3},{1,0},{2,1},{3,2},{4,7},{5,4},{6,5},{7,6},{8,11},{9,8},{10,9... | collective-permute-start | bytes 589832 | tf_op jit(solution)/shard_map/ppermute | solution.py:299
  160.0 0.9 copy-start.1
  171.3 34.6 %collective-permute-start.18 = (bf16[2,2,128,512]{3,2,1,0:T(8,128)(2,1)S(1)}, bf16[2,2,128,512]{3,2,1,0:T(8,128)(2,1)S(1)}, u32[]{:S(2)}, u32[]{:S(2)}) collective-permute-start(bf16[2,2,128,512]{3,2,1,0:T(8,128)(2,1)S(1)} %get-tuple-element.54), channel_id=1, source_target_pairs={{124,52},{125,53},{126,54},{127,55}} | collective-permute-start | bytes 1572872 | tf_op jit(solution)/shard_map/ppermute | solution.py:299
  172.0 42.3 %collective-permute-start.21 = (bf16[2,2,128,512]{3,2,1,0:T(8,128)(2,1)S(1)}, bf16[2,2,128,512]{3,2,1,0:T(8,128)(2,1)S(1)}, u32[]{:S(2)}, u32[]{:S(2)}) collective-permute-start(bf16[2,2,128,512]{3,2,1,0:T(8,128)(2,1)S(1)} %get-tuple-element.55), channel_id=1, source_target_pairs={{128,200},{129,201},{130,202},{131,203}} | collective-permute-start | bytes 1572872 | tf_op jit(solution)/shard_map/ppermute | solution.py:299
  172.7 19.7 %collective-permute-start.14 = (bf16[128,512]{1,0:T(8,128)(2,1)S(1)}, bf16[128,512]{1,0:T(8,128)(2,1)S(1)}, u32[]{:S(2)}, u32[]{:S(2)}) collective-permute-start(bf16[128,512]{1,0:T(8,128)(2,1)S(1)} %get-tuple-element.50), channel_id=1, source_target_pairs={{0,1},{1,2},{2,3},{3,0},{4,5},{5,6},{6,7},{7,4},{8,9},{9,10},{10,1... | collective-permute-start | bytes 393224 | tf_op jit(solution)/shard_map/ppermute | solution.py:299
  191.0 50.5 %collective-permute-start.36 = (bf16[2,2,128,768]{3,2,1,0:T(8,128)(2,1)S(1)}, bf16[2,2,128,768]{3,2,1,0:T(8,128)(2,1)S(1)}, u32[]{:S(2)}, u32[]{:S(2)}) collective-permute-start(bf16[2,2,128,768]{3,2,1,0:T(8,128)(2,1)S(1)} %get-tuple-element.69), channel_id=1, source_target_pairs={{124,52},{125,53},{126,54},{127,55}} | collective-permute-start | bytes 2359304 | tf_op jit(solution)/shard_map/ppermute | solution.py:299
  191.7 50.5 %collective-permute-start.39 = (bf16[2,2,128,768]{3,2,1,0:T(8,128)(2,1)S(1)}, bf16[2,2,128,768]{3,2,1,0:T(8,128)(2,1)S(1)}, u32[]{:S(2)}, u32[]{:S(2)}) collective-permute-start(bf16[2,2,128,768]{3,2,1,0:T(8,128)(2,1)S(1)} %get-tuple-element.70), channel_id=1, source_target_pairs={{128,200},{129,201},{130,202},{131,203}} | collective-permute-start | bytes 2359304 | tf_op jit(solution)/shard_map/ppermute | solution.py:299
  192.4 10.0 %collective-permute-start.15 = (bf16[128,512]{1,0:T(8,128)(2,1)S(1)}, bf16[128,512]{1,0:T(8,128)(2,1)S(1)}, u32[]{:S(2)}, u32[]{:S(2)}) collective-permute-start(bf16[128,512]{1,0:T(8,128)(2,1)S(1)} %get-tuple-element.51), channel_id=1, source_target_pairs={{0,2},{1,3},{2,0},{3,1},{4,6},{5,7},{6,4},{7,5},{8,10},{9,11},{10,... | collective-permute-start | bytes 393224 | tf_op jit(solution)/shard_map/ppermute | solution.py:299
  202.4 41.2 %collective-permute-start.35 = (bf16[2,2,128,768]{3,2,1,0:T(8,128)(2,1)S(1)}, bf16[2,2,128,768]{3,2,1,0:T(8,128)(2,1)S(1)}, u32[]{:S(2)}, u32[]{:S(2)}) collective-permute-start(bf16[2,2,128,768]{3,2,1,0:T(8,128)(2,1)S(1)} %get-tuple-element.69), channel_id=1, source_target_pairs={{0,4},{1,5},{2,6},{3,7},{4,8},{5,9},{6,10},{7,11},{8,12},{9,13},{1... | collective-permute-start | bytes 2359304 | tf_op jit(solution)/shard_map/ppermute | solution.py:299
  205.8 28.1 %collective-permute-start.17 = (bf16[2,2,128,512]{3,2,1,0:T(8,128)(2,1)S(1)}, bf16[2,2,128,512]{3,2,1,0:T(8,128)(2,1)S(1)}, u32[]{:S(2)}, u32[]{:S(2)}) collective-permute-start(bf16[2,2,128,512]{3,2,1,0:T(8,128)(2,1)S(1)} %get-tuple-element.54), channel_id=1, source_target_pairs={{0,4},{1,5},{2,6},{3,7},{4,8},{5,9},{6,10},{7,11},{8,12},{9,13},{1... | collective-permute-start | bytes 1572872 | tf_op jit(solution)/shard_map/ppermute | solution.py:299
  214.3 28.7 %collective-permute-start.20 = (bf16[2,2,128,512]{3,2,1,0:T(8,128)(2,1)S(1)}, bf16[2,2,128,512]{3,2,1,0:T(8,128)(2,1)S(1)}, u32[]{:S(2)}, u32[]{:S(2)}) collective-permute-start(bf16[2,2,128,512]{3,2,1,0:T(8,128)(2,1)S(1)} %get-tuple-element.55), channel_id=1, source_target_pairs={{4,0},{5,1},{6,2},{7,3},{8,4},{9,5},{10,6},{11,7},{12,8},{13,9},{1... | collective-permute-start | bytes 1572872 | tf_op jit(solution)/shard_map/ppermute | solution.py:299
  233.9 25.4 %collective-permute-start.38 = (bf16[2,2,128,768]{3,2,1,0:T(8,128)(2,1)S(1)}, bf16[2,2,128,768]{3,2,1,0:T(8,128)(2,1)S(1)}, u32[]{:S(2)}, u32[]{:S(2)}) collective-permute-start(bf16[2,2,128,768]{3,2,1,0:T(8,128)(2,1)S(1)} %get-tuple-element.70), channel_id=1, source_target_pairs={{4,0},{5,1},{6,2},{7,3},{8,4},{9,5},{10,6},{11,7},{12,8},{13,9},{1... | collective-permute-start | bytes 2359304 | tf_op jit(solution)/shard_map/ppermute | solution.py:299
  241.5 17.8 %collective-permute-start.37 = (bf16[2,2,128,768]{3,2,1,0:T(8,128)(2,1)S(1)}, bf16[2,2,128,768]{3,2,1,0:T(8,128)(2,1)S(1)}, u32[]{:S(2)}, u32[]{:S(2)}) collective-permute-start(bf16[2,2,128,768]{3,2,1,0:T(8,128)(2,1)S(1)} %collective-permute-done.36), channel_id=1, source_target_pairs={{52,128},{53,129},{54,130},{55,131}} | collective-permute-start | bytes 2359304 | tf_op jit(solution)/shard_map/ppermute | solution.py:299
  242.2 21.2 %collective-permute-start.40 = (bf16[2,2,128,768]{3,2,1,0:T(8,128)(2,1)S(1)}, bf16[2,2,128,768]{3,2,1,0:T(8,128)(2,1)S(1)}, u32[]{:S(2)}, u32[]{:S(2)}) collective-permute-start(bf16[2,2,128,768]{3,2,1,0:T(8,128)(2,1)S(1)} %collective-permute-done.39), channel_id=1, source_target_pairs={{200,124},{201,125},{202,126},{203,127}} | collective-permute-start | bytes 2359304 | tf_op jit(solution)/shard_map/ppermute | solution.py:299
  243.0 1.4 collective-permute-start.19
  243.7 0.8 collective-permute-start.22
  244.4 61.3 %collective-permute-start.32 = (bf16[128,768]{1,0:T(8,128)(2,1)S(1)}, bf16[128,768]{1,0:T(8,128)(2,1)S(1)}, u32[]{:S(2)}, u32[]{:S(2)}) collective-permute-start(bf16[128,768]{1,0:T(8,128)(2,1)S(1)} %get-tuple-element.65), channel_id=1, source_target_pairs={{0,1},{1,2},{2,3},{3,0},{4,5},{5,6},{6,7},{7,4},{8,9},{9,10},{10,1... | collective-permute-start | bytes 589832 | tf_op jit(solution)/shard_map/ppermute | solution.py:299
  244.5 62.9 %collective-permute-start.33 = (bf16[128,768]{1,0:T(8,128)(2,1)S(1)}, bf16[128,768]{1,0:T(8,128)(2,1)S(1)}, u32[]{:S(2)}, u32[]{:S(2)}) collective-permute-start(bf16[128,768]{1,0:T(8,128)(2,1)S(1)} %get-tuple-element.66), channel_id=1, source_target_pairs={{0,2},{1,3},{2,0},{3,1},{4,6},{5,7},{6,4},{7,5},{8,10},{9,11},{10,... | collective-permute-start | bytes 589832 | tf_op jit(solution)/shard_map/ppermute | solution.py:299
  259.3 44.1 %collective-permute-start.16 = (bf16[128,512]{1,0:T(8,128)(2,1)S(1)}, bf16[128,512]{1,0:T(8,128)(2,1)S(1)}, u32[]{:S(2)}, u32[]{:S(2)}) collective-permute-start(bf16[128,512]{1,0:T(8,128)(2,1)S(1)} %get-tuple-element.52), channel_id=1, source_target_pairs={{0,3},{1,0},{2,1},{3,2},{4,7},{5,4},{6,5},{7,6},{8,11},{9,8},{10,9... | collective-permute-start | bytes 393224 | tf_op jit(solution)/shard_map/ppermute | solution.py:299
  259.3 52.9 %collective-permute-start.23 = (bf16[2,128,512]{2,1,0:T(8,128)(2,1)S(1)}, bf16[2,128,512]{2,1,0:T(8,128)(2,1)S(1)}, u32[]{:S(2)}, u32[]{:S(2)}) collective-permute-start(bf16[2,128,512]{2,1,0:T(8,128)(2,1)S(1)} %get-tuple-element.57), channel_id=1, source_target_pairs={{0,1},{1,2},{2,3},{3,0},{4,5},{5,6},{6,7},{7,4},{8,9},{9,10},{10,1... | collective-permute-start | bytes 786440 | tf_op jit(solution)/shard_map/ppermute | solution.py:299
  263.5 45.2 %collective-permute-start.34 = (bf16[128,768]{1,0:T(8,128)(2,1)S(1)}, bf16[128,768]{1,0:T(8,128)(2,1)S(1)}, u32[]{:S(2)}, u32[]{:S(2)}) collective-permute-start(bf16[128,768]{1,0:T(8,128)(2,1)S(1)} %get-tuple-element.67), channel_id=1, source_target_pairs={{0,3},{1,0},{2,1},{3,2},{4,7},{5,4},{6,5},{7,6},{8,11},{9,8},{10,9... | collective-permute-start | bytes 589832 | tf_op jit(solution)/shard_map/ppermute | solution.py:299
  303.4 41.0 %collective-permute-start.41 = (bf16[2,128,768]{2,1,0:T(8,128)(2,1)S(1)}, bf16[2,128,768]{2,1,0:T(8,128)(2,1)S(1)}, u32[]{:S(2)}, u32[]{:S(2)}) collective-permute-start(bf16[2,128,768]{2,1,0:T(8,128)(2,1)S(1)} %get-tuple-element.72), channel_id=1, source_target_pairs={{0,1},{1,2},{2,3},{3,0},{4,5},{5,6},{6,7},{7,4},{8,9},{9,10},{10,1... | collective-permute-start | bytes 1179656 | tf_op jit(solution)/shard_map/ppermute | solution.py:299
  305.7 38.6 %collective-permute-start.42 = (bf16[2,128,768]{2,1,0:T(8,128)(2,1)S(1)}, bf16[2,128,768]{2,1,0:T(8,128)(2,1)S(1)}, u32[]{:S(2)}, u32[]{:S(2)}) collective-permute-start(bf16[2,128,768]{2,1,0:T(8,128)(2,1)S(1)} %get-tuple-element.73), channel_id=1, source_target_pairs={{0,2},{1,3},{2,0},{3,1},{4,6},{5,7},{6,4},{7,5},{8,10},{9,11},{10,... | collective-permute-start | bytes 1179656 | tf_op jit(solution)/shard_map/ppermute | solution.py:299
  307.3 37.0 %collective-permute-start.43 = (bf16[2,128,768]{2,1,0:T(8,128)(2,1)S(1)}, bf16[2,128,768]{2,1,0:T(8,128)(2,1)S(1)}, u32[]{:S(2)}, u32[]{:S(2)}) collective-permute-start(bf16[2,128,768]{2,1,0:T(8,128)(2,1)S(1)} %get-tuple-element.74), channel_id=1, source_target_pairs={{0,3},{1,0},{2,1},{3,2},{4,7},{5,4},{6,5},{7,6},{8,11},{9,8},{10,9... | collective-permute-start | bytes 1179656 | tf_op jit(solution)/shard_map/ppermute | solution.py:299
  308.7 35.6 %collective-permute-start.24 = (bf16[2,128,512]{2,1,0:T(8,128)(2,1)S(1)}, bf16[2,128,512]{2,1,0:T(8,128)(2,1)S(1)}, u32[]{:S(2)}, u32[]{:S(2)}) collective-permute-start(bf16[2,128,512]{2,1,0:T(8,128)(2,1)S(1)} %get-tuple-element.58), channel_id=1, source_target_pairs={{0,2},{1,3},{2,0},{3,1},{4,6},{5,7},{6,4},{7,5},{8,10},{9,11},{10,... | collective-permute-start | bytes 786440 | tf_op jit(solution)/shard_map/ppermute | solution.py:299
  312.3 32.1 %collective-permute-start.25 = (bf16[2,128,512]{2,1,0:T(8,128)(2,1)S(1)}, bf16[2,128,512]{2,1,0:T(8,128)(2,1)S(1)}, u32[]{:S(2)}, u32[]{:S(2)}) collective-permute-start(bf16[2,128,512]{2,1,0:T(8,128)(2,1)S(1)} %get-tuple-element.59), channel_id=1, source_target_pairs={{0,3},{1,0},{2,1},{3,2},{4,7},{5,4},{6,5},{7,6},{8,11},{9,8},{10,9... | collective-permute-start | bytes 786440 | tf_op jit(solution)/shard_map/ppermute | solution.py:299

commit v8 on v7

--- a/solution.py
+++ b/solution.py
@@ -198,18 +198,20 @@
     )(zh, q, g, *recv, before, lo, hi, after, bias)
 
 
-def finish_body(zh, own, before, before_seam, after, after_seam, o0, o1, o2, o3):
+def finish_body(zh, own, *refs):
+    n = (len(refs) - NZ) // 2
+    before, after, outs = refs[:n], refs[n : 2 * n], refs[2 * n :]
     z = zh[0]
-    for s, o in enumerate((o0, o1, o2, o3)):
+    for s, o in enumerate(outs):
         b = lax.rem(z + s, NZ)
 
         @pl.when(b < 2)
         def _():
-            o[...] = (own[b] + (before[b].astype(F32) + before_seam[b].astype(F32))).astype(BF)
+            o[...] = (own[b] + sum(r[b].astype(F32) for r in before)).astype(BF)
 
         @pl.when(b >= 2)
         def _():
-            o[...] = (own[b] + (after[b - 2].astype(F32) + after_seam[b - 2].astype(F32))).astype(BF)
+            o[...] = (own[b] + sum(r[b - 2].astype(F32) for r in after)).astype(BF)
 
 
 def finish(zh, own, from_before, from_after):
@@ -221,7 +223,7 @@
         grid_spec=pltpu.PrefetchScalarGridSpec(
             num_scalar_prefetch=1,
             grid=(n // CW,),
-            in_specs=[pl.BlockSpec((4, 2, BLK, CW), lambda i, z: (0, 0, 0, i)), rim, rim, rim, rim],
+            in_specs=[pl.BlockSpec((4, 2, BLK, CW), lambda i, z: (0, 0, 0, i))] + [rim] * (2 * len(from_before)),
             out_specs=[out] * 4,
         ),
         out_shape=[jax.ShapeDtypeStruct((2, BLK, n), BF)] * 4,
@@ -338,8 +340,11 @@
         *dq, rim_before, rim_after, own = attend(
             zh, query, dout, recv, before, lo, hi, after, bias, first, heads, group
         )
-        from_after = rim_move(down, high, via_down, low, rim_before)
-        from_before = rim_move(up, low, via_up, high, rim_after)
+        if c == 0:
+            from_after = rim_move(down, high, via_down, low, rim_before)
+            from_before = rim_move(up, low, via_up, high, rim_after)
+        else:
+            from_after, from_before = (to_prev(rim_before),), (to_next(rim_after),)
         back_q = [dq[0], *around(dq[1:])]
         dkv = finish(zh, own, from_before, from_after)
         back_kv = [dkv[0], *around(dkv[1:])]

time: 348 us -> 332 us (0.954)
  starting transfers between devices: 94.1 us -> 78.2 us
  local copies, waits for them, and re-layouts: 8.8 us -> 0.71 us
  waiting for transfers between devices: 197 us -> 205 us
    ppermute x44 -> x40, starting transfers between devices: 94.1 us -> 78.2 us  [move(): return lax.ppermute(a, axes, perm)]
    ppermute x44 -> x40, waiting for transfers between devices: 197 us -> 205 us  [move(): return lax.ppermute(a, axes, perm)]
  transfers between devices with their start and end apart: 44 -> 40, of which waited for: 11 -> 12; matrix products, arithmetic and copies ran while one was open for 2% -> 1% of each run, Pallas kernels for 12% -> 12%
where the time goes in v8:
time: 332 us; the launch traced here: 331 us
  waiting for transfers between devices  205 us (62%)
  starting transfers between devices  78.2 us (24%)
  Pallas kernels  44.9 us (14%)
    ppermute x40, waiting for transfers between devices, move(): return lax.ppermute(a, axes, perm)  205 us
    ppermute x40, starting transfers between devices, move(): return lax.ppermute(a, axes, perm)  78.2 us
    pallas_call x2, Pallas kernels, attend(): pl.pallas_call(attend_body, grid_spec=pltpu.PrefetchScalarGridSpec(num_sc...  25.5 us
    pallas_call x5, Pallas kernels, pack(): pl.pallas_call(pack_body, grid_spec=pltpu.PrefetchScalarGridSpec(num_scal...  10.9 us
  transfers between devices with their start and end apart: 40, of which 12 were waited for; matrix products, arithmetic and copies ran while one was open for 1% of the time, Pallas kernels for 12%

profile of v8, /device:TPU:90, one launch (start us, length us, event | category | flops | bytes accessed | tf_op | source)
XLA Modules:
  0.0 330.5 jit_solution(4998785759831898157)
XLA Ops:
  0.6 2.3 shard_map.78
  3.0 4.5 %collective-permute-start.6 = (bf16[2,128,1280]{2,1,0:T(8,128)(2,1)}, bf16[2,128,1280]{2,1,0:T(8,128)(2,1)S(1)}, u32[]{:S(2)}, u32[]{:S(2)}) collective-permute-start(bf16[2,128,1280]{2,1,0:T(8,128)(2,1)} %get-tuple-element.43), channel_id=1, source_target_pairs={{0,1},{1,2},{2,3},{3,0},{4,5},{5,6},{6,7},{7,4},{8,9},{9,10},{10,1... | collective-permute-start | bytes 1966088 | tf_op jit(solution)/shard_map/ppermute | solution.py:301
  7.5 1.9 shard_map.79
  9.4 1.5 collective-permute-start.10
  10.9 2.6 collective-permute-start.8
  13.6 1.6 shard_map.77
  15.2 2.9 collective-permute-start.2
  18.1 37.3 %collective-permute-done.2 = bf16[1,128,512]{2,1,0:T(8,128)(2,1)S(1)} collective-permute-done((bf16[1,128,512]{2,1,0:T(8,128)(2,1)}, bf16[1,128,512]{2,1,0:T(8,128)(2,1)S(1)}, u32[]{:S(2)}, u32[]{:S(2)}) %collective-permute-start.2) | collective-permute-done | bytes 131104 | tf_op jit(solution)/shard_map/ppermute | solution.py:301
  55.4 3.2 shard_map.82
  58.6 7.3 %collective-permute-done.4 = bf16[1,128,512]{2,1,0:T(8,128)(2,1)} collective-permute-done((bf16[1,128,512]{2,1,0:T(8,128)(2,1)}, bf16[1,128,512]{2,1,0:T(8,128)(2,1)}, u32[]{:S(2)}, u32[]{:S(2)}) %collective-permute-start.4) | collective-permute-done | bytes 131104 | tf_op jit(solution)/shard_map/ppermute | solution.py:301
  65.9 1.6 collective-permute-start.26
  67.4 1.3 collective-permute-start.11
  68.8 2.8 collective-permute-start.9
  71.6 1.8 shard_map.76
  74.1 2.3 collective-permute-start.1
  76.4 23.5 %collective-permute-done.11.fm = bf16[1,128,1280]{2,1,0:T(8,128)(2,1)S(1)} collective-permute-done((bf16[1,128,1280]{2,1,0:T(8,128)(2,1)S(1)}, bf16[1,128,1280]{2,1,0:T(8,128)(2,1)S(1)}, u32[]{:S(2)}, u32[]{:S(2)}) %collective-permute-start.11) | collective-permute-done | bytes 327712 | tf_op jit(solution)/shard_map/ppermute | solution.py:301
  100.7 14.7 %collective-permute-done.9.fp = bf16[1,128,1280]{2,1,0:T(8,128)(2,1)S(1)} collective-permute-done((bf16[1,128,1280]{2,1,0:T(8,128)(2,1)}, bf16[1,128,1280]{2,1,0:T(8,128)(2,1)S(1)}, u32[]{:S(2)}, u32[]{:S(2)}) %collective-permute-start.9) | collective-permute-done | bytes 327712 | tf_op jit(solution)/shard_map/ppermute | solution.py:301
  115.4 1.1 collective-permute-start.3
  116.5 4.3 %unpack.1 = (bf16[2,2,128,512]{3,2,1,0:T(8,128)(2,1)}, bf16[2,2,128,512]{3,2,1,0:T(8,128)(2,1)}, bf16[2,2,128,768]{3,2,1,0:T(8,128)(2,1)}, bf16[2,2,128,768]{3,2,1,0:T(8,128)(2,1)}) custom-call(s32[1]{0:T(128)} %bitcast.zh, bf16[128,5120]{1,0:T(8,128)(2,1)} %k.1, bf16[128,5120]{1,0:T(8,128)(2,1)} %v.1, bf16[2,128,1280]{2,1,0:T(8,128)(2,1)S(1)} %collective-permute-done.6.mp, ...), custom_call_target="tpu_custom_call" | custom-call | bytes 5242880 | tf_op jit(solution)/shard_map/unpack/pallas_call | solution.py:98
  121.0 3.4 %collective-permute-start.30 = (bf16[2,2,128,768]{3,2,1,0:T(8,128)(2,1)}, bf16[2,2,128,768]{3,2,1,0:T(8,128)(2,1)S(1)}, u32[]{:S(2)}, u32[]{:S(2)}) collective-permute-start(bf16[2,2,128,768]{3,2,1,0:T(8,128)(2,1)} %get-tuple-element.62.hi), channel_id=1, source_target_pairs={{0,4},{1,5},{2,6},{3,7},{4,8},{5,9},{6,10},{7,11},{8,12},{9,13},{1... | collective-permute-start | bytes 2359304 | tf_op jit(solution)/shard_map/ppermute | solution.py:301
  124.4 2.4 collective-permute-start.31
  126.9 3.4 %collective-permute-start.12 = (bf16[2,2,128,512]{3,2,1,0:T(8,128)(2,1)}, bf16[2,2,128,512]{3,2,1,0:T(8,128)(2,1)}, u32[]{:S(2)}, u32[]{:S(2)}) collective-permute-start(bf16[2,2,128,512]{3,2,1,0:T(8,128)(2,1)} %get-tuple-element.47.hi), channel_id=1, source_target_pairs={{0,4},{1,5},{2,6},{3,7},{4,8},{5,9},{6,10},{7,11},{8,12},{9,13},{1... | collective-permute-start | bytes 1572872 | tf_op jit(solution)/shard_map/ppermute | solution.py:301
  130.3 2.8 collective-permute-start.13
  134.2 1.9 collective-permute-start.5
  136.6 5.1 %collective-permute-done.5.fm = bf16[1,128,512]{2,1,0:T(8,128)(2,1)S(1)} collective-permute-done((bf16[1,128,512]{2,1,0:T(8,128)(2,1)}, bf16[1,128,512]{2,1,0:T(8,128)(2,1)S(1)}, u32[]{:S(2)}, u32[]{:S(2)}) %collective-permute-start.5) | collective-permute-done | bytes 131104 | tf_op jit(solution)/shard_map/ppermute | solution.py:301
  141.8 12.0 %collective-permute-done.12.before = bf16[2,2,128,512]{3,2,1,0:T(8,128)(2,1)} collective-permute-done((bf16[2,2,128,512]{3,2,1,0:T(8,128)(2,1)}, bf16[2,2,128,512]{3,2,1,0:T(8,128)(2,1)}, u32[]{:S(2)}, u32[]{:S(2)}) %collective-permute-start.12) | collective-permute-done | bytes 524320 | tf_op jit(solution)/shard_map/ppermute | solution.py:301
  153.8 1.3 collective-permute-start.29
  155.1 1.8 collective-permute-done.13.after
  156.9 10.4 %shard_map.80 = (bf16[128,512]{1,0:T(8,128)(2,1)S(1)}, bf16[128,512]{1,0:T(8,128)(2,1)S(1)}, bf16[128,512]{1,0:T(8,128)(2,1)S(1)}, bf16[128,512]{1,0:T(8,128)(2,...) custom-call(s32[1]{0:T(128)} %bitcast.zh, ...), custom_call_target="tpu_custom_call" | custom-call | flops 2013265920 | bytes 5242880 | tf_op jit(solution)/shard_map/pallas_call | solution.py:175
  168.8 3.1 collective-permute-start.17
  171.9 1.4 collective-permute-start.14
  173.3 15.1 %shard_map.83 = (bf16[128,768]{1,0:T(8,128)(2,1)S(1)}, bf16[128,768]{1,0:T(8,128)(2,1)S(1)}, bf16[128,768]{1,0:T(8,128)(2,1)S(1)}, bf16[128,768]{1,0:T(8,128)(2,...) custom-call(s32[1]{0:T(128)} %bitcast.zh, ...), custom_call_target="tpu_custom_call" | custom-call | flops 3019898880 | bytes 7864320 | tf_op jit(solution)/shard_map/pallas_call | solution.py:175
  188.4 3.1 collective-permute-start.35
  191.5 2.7 collective-permute-start.36
  194.3 4.8 %collective-permute-start.20 = (bf16[2,2,128,512]{3,2,1,0:T(8,128)(2,1)S(1)}, bf16[2,2,128,512]{3,2,1,0:T(8,128)(2,1)S(1)}, u32[]{:S(2)}, u32[]{:S(2)}) collective-permute-start(bf16[2,2,128,512]{3,2,1,0:T(8,128)(2,1)S(1)} %get-tuple-element.55), channel_id=1, source_target_pairs={{4,0},{5,1},{6,2},{7,3},{8,4},{9,5},{10,6},{11,7},{12,8},{13,9},{1... | collective-permute-start | bytes 1572872 | tf_op jit(solution)/shard_map/ppermute | solution.py:301
  200.4 24.6 %collective-permute-done.20.refs_2_ = bf16[2,2,128,512]{3,2,1,0:T(8,128)(2,1)S(1)} collective-permute-done((bf16[2,2,128,512]{3,2,1,0:T(8,128)(2,1)S(1)}, bf16[2,2,128,512]{3,2,1,0:T(8,128)(2,1)S(1)}, u32[]{:S(2)}, u32[]{:S(2)}) %collective-permute-start.20) | collective-permute-done | bytes 524320 | tf_op jit(solution)/shard_map/ppermute | solution.py:301
  225.0 2.4 collective-permute-start.15
  228.4 3.0 collective-permute-start.33
  232.2 8.4 %collective-permute-done.15.refs_2_ = bf16[128,512]{1,0:T(8,128)(2,1)S(1)} collective-permute-done((bf16[128,512]{1,0:T(8,128)(2,1)S(1)}, bf16[128,512]{1,0:T(8,128)(2,1)S(1)}, u32[]{:S(2)}, u32[]{:S(2)}) %collective-permute-start.15) | collective-permute-done | bytes 131104 | tf_op jit(solution)/shard_map/ppermute | solution.py:301
  240.6 4.1 %collective-permute-start.23 = (bf16[2,128,512]{2,1,0:T(8,128)(2,1)S(1)}, bf16[2,128,512]{2,1,0:T(8,128)(2,1)S(1)}, u32[]{:S(2)}, u32[]{:S(2)}) collective-permute-start(bf16[2,128,512]{2,1,0:T(8,128)(2,1)S(1)} %get-tuple-element.57), channel_id=1, source_target_pairs={{0,1},{1,2},{2,3},{3,0},{4,5},{5,6},{6,7},{7,4},{8,9},{9,10},{10,1... | collective-permute-start | bytes 786440 | tf_op jit(solution)/shard_map/ppermute | solution.py:301
  245.7 39.4 %collective-permute-done.16.refs_3_ = bf16[128,512]{1,0:T(8,128)(2,1)S(1)} collective-permute-done((bf16[128,512]{1,0:T(8,128)(2,1)S(1)}, bf16[128,512]{1,0:T(8,128)(2,1)S(1)}, u32[]{:S(2)}, u32[]{:S(2)}) %collective-permute-start.16) | collective-permute-done | bytes 131104 | tf_op jit(solution)/shard_map/ppermute | solution.py:301
  285.1 1.6 collective-permute-start.37
  286.7 4.3 %collective-permute-start.38 = (bf16[2,128,768]{2,1,0:T(8,128)(2,1)S(1)}, bf16[2,128,768]{2,1,0:T(8,128)(2,1)S(1)}, u32[]{:S(2)}, u32[]{:S(2)}) collective-permute-start(bf16[2,128,768]{2,1,0:T(8,128)(2,1)S(1)} %get-tuple-element.73), channel_id=1, source_target_pairs={{0,2},{1,3},{2,0},{3,1},{4,6},{5,7},{6,4},{7,5},{8,10},{9,11},{10,... | collective-permute-start | bytes 1179656 | tf_op jit(solution)/shard_map/ppermute | solution.py:301
  291.0 1.0 collective-permute-start.39
  292.0 2.0 collective-permute-start.24
  294.0 3.5 %collective-permute-start.25 = (bf16[2,128,512]{2,1,0:T(8,128)(2,1)S(1)}, bf16[2,128,512]{2,1,0:T(8,128)(2,1)S(1)}, u32[]{:S(2)}, u32[]{:S(2)}) collective-permute-start(bf16[2,128,512]{2,1,0:T(8,128)(2,1)S(1)} %get-tuple-element.59), channel_id=1, source_target_pairs={{0,3},{1,0},{2,1},{3,2},{4,7},{5,4},{6,5},{7,6},{8,11},{9,8},{10,9... | collective-permute-start | bytes 786440 | tf_op jit(solution)/shard_map/ppermute | solution.py:301
  297.5 30.6 %collective-permute-done.24.refs_6_ = bf16[2,128,512]{2,1,0:T(8,128)(2,1)S(1)} collective-permute-done((bf16[2,128,512]{2,1,0:T(8,128)(2,1)S(1)}, bf16[2,128,512]{2,1,0:T(8,128)(2,1)S(1)}, u32[]{:S(2)}, u32[]{:S(2)}) %collective-permute-start.24) | collective-permute-done | bytes 262176 | tf_op jit(solution)/shard_map/ppermute | solution.py:301
  328.1 2.4 assemble.1
  (58 shorter events, 9.1 us)
Async XLA Ops:
  3.0 70.4 %collective-permute-start.6 = (bf16[2,128,1280]{2,1,0:T(8,128)(2,1)}, bf16[2,128,1280]{2,1,0:T(8,128)(2,1)S(1)}, u32[]{:S(2)}, u32[]{:S(2)}) collective-permute-start(bf16[2,128,1280]{2,1,0:T(8,128)(2,1)} %get-tuple-element.43), channel_id=1, source_target_pairs={{0,1},{1,2},{2,3},{3,0},{4,5},{5,6},{6,7},{7,4},{8,9},{9,10},{10,1... | collective-permute-start | bytes 1966088 | tf_op jit(solution)/shard_map/ppermute | solution.py:301
  7.5 66.7 %collective-permute-start.7 = (bf16[2,128,1280]{2,1,0:T(8,128)(2,1)}, bf16[2,128,1280]{2,1,0:T(8,128)(2,1)S(1)}, u32[]{:S(2)}, u32[]{:S(2)}) collective-permute-start(bf16[2,128,1280]{2,1,0:T(8,128)(2,1)} %get-tuple-element.44), channel_id=1, source_target_pairs={{0,3},{1,0},{2,1},{3,2},{4,7},{5,4},{6,5},{7,6},{8,11},{9,8},{10,9... | collective-permute-start | bytes 1966088 | tf_op jit(solution)/shard_map/ppermute | solution.py:301
  9.4 58.1 %collective-permute-start.10 = (bf16[1,128,1280]{2,1,0:T(8,128)(2,1)}, bf16[1,128,1280]{2,1,0:T(8,128)(2,1)S(1)}, u32[]{:S(2)}, u32[]{:S(2)}) collective-permute-start(bf16[1,128,1280]{2,1,0:T(8,128)(2,1)} %get-tuple-element.46), channel_id=1, source_target_pairs={{0,3},{1,0},{2,1},{3,2},{4,7},{5,4},{6,5},{7,6},{8,11},{9,8},{10,9... | collective-permute-start | bytes 983048 | tf_op jit(solution)/shard_map/ppermute | solution.py:301
  10.9 57.9 %collective-permute-start.8 = (bf16[1,128,1280]{2,1,0:T(8,128)(2,1)}, bf16[1,128,1280]{2,1,0:T(8,128)(2,1)}, u32[]{:S(2)}, u32[]{:S(2)}) collective-permute-start(bf16[1,128,1280]{2,1,0:T(8,128)(2,1)} %get-tuple-element.45), channel_id=1, source_target_pairs={{0,1},{1,2},{2,3},{3,0},{4,5},{5,6},{6,7},{7,4},{8,9},{9,10},{10,1... | collective-permute-start | bytes 983048 | tf_op jit(solution)/shard_map/ppermute | solution.py:301
  15.2 40.2 %collective-permute-start.2 = (bf16[1,128,512]{2,1,0:T(8,128)(2,1)}, bf16[1,128,512]{2,1,0:T(8,128)(2,1)S(1)}, u32[]{:S(2)}, u32[]{:S(2)}) collective-permute-start(bf16[1,128,512]{2,1,0:T(8,128)(2,1)} %get-tuple-element.41), channel_id=1, source_target_pairs={{0,1},{1,2},{2,3},{3,0},{4,5},{5,6},{6,7},{7,4},{8,9},{9,10},{10,1... | collective-permute-start | bytes 393224 | tf_op jit(solution)/shard_map/ppermute | solution.py:301
  55.4 3.2 copy-start
  55.4 10.5 %collective-permute-start.4 = (bf16[1,128,512]{2,1,0:T(8,128)(2,1)}, bf16[1,128,512]{2,1,0:T(8,128)(2,1)}, u32[]{:S(2)}, u32[]{:S(2)}) collective-permute-start(bf16[1,128,512]{2,1,0:T(8,128)(2,1)} %get-tuple-element.42), channel_id=1, source_target_pairs={{0,3},{1,0},{2,1},{3,2},{4,7},{5,4},{6,5},{7,6},{8,11},{9,8},{10,9... | collective-permute-start | bytes 393224 | tf_op jit(solution)/shard_map/ppermute | solution.py:301
  65.9 64.4 %collective-permute-start.26 = (bf16[3,128,768]{2,1,0:T(8,128)(2,1)}, bf16[3,128,768]{2,1,0:T(8,128)(2,1)S(1)}, u32[]{:S(2)}, u32[]{:S(2)}) collective-permute-start(bf16[3,128,768]{2,1,0:T(8,128)(2,1)} %get-tuple-element.60), channel_id=1, source_target_pairs={{0,1},{1,2},{2,3},{3,0},{4,5},{5,6},{6,7},{7,4},{8,9},{9,10},{10,1... | collective-permute-start | bytes 1769480 | tf_op jit(solution)/shard_map/ppermute | solution.py:301
  67.4 32.4 %collective-permute-start.11 = (bf16[1,128,1280]{2,1,0:T(8,128)(2,1)S(1)}, bf16[1,128,1280]{2,1,0:T(8,128)(2,1)S(1)}, u32[]{:S(2)}, u32[]{:S(2)}) collective-permute-start(bf16[1,128,1280]{2,1,0:T(8,128)(2,1)S(1)} %collective-permute-done.10), channel_id=1, source_target_pairs={{0,3},{1,0},{2,1},{3,2},{4,7},{5,4},{6,5},{7,6},{8,11},{9,8},{10,9... | collective-permute-start | bytes 983048 | tf_op jit(solution)/shard_map/ppermute | solution.py:301
  68.8 46.6 %collective-permute-start.9 = (bf16[1,128,1280]{2,1,0:T(8,128)(2,1)}, bf16[1,128,1280]{2,1,0:T(8,128)(2,1)S(1)}, u32[]{:S(2)}, u32[]{:S(2)}) collective-permute-start(bf16[1,128,1280]{2,1,0:T(8,128)(2,1)} %collective-permute-done.8), channel_id=1, source_target_pairs={{0,1},{1,2},{2,3},{3,0},{4,5},{5,6},{6,7},{7,4},{8,9},{9,10},{10,1... | collective-permute-start | bytes 983048 | tf_op jit(solution)/shard_map/ppermute | solution.py:301
  73.4 47.6 %collective-permute-start = (bf16[2,128,512]{2,1,0:T(8,128)(2,1)}, bf16[2,128,512]{2,1,0:T(8,128)(2,1)S(1)}, u32[]{:S(2)}, u32[]{:S(2)}) collective-permute-start(bf16[2,128,512]{2,1,0:T(8,128)(2,1)} %get-tuple-element.39), channel_id=1, source_target_pairs={{0,1},{1,2},{2,3},{3,0},{4,5},{5,6},{6,7},{7,4},{8,9},{9,10},{10,1... | collective-permute-start | bytes 786440 | tf_op jit(solution)/shard_map/ppermute | solution.py:301
  74.1 50.3 %collective-permute-start.1 = (bf16[2,128,512]{2,1,0:T(8,128)(2,1)}, bf16[2,128,512]{2,1,0:T(8,128)(2,1)}, u32[]{:S(2)}, u32[]{:S(2)}) collective-permute-start(bf16[2,128,512]{2,1,0:T(8,128)(2,1)} %get-tuple-element.40), channel_id=1, source_target_pairs={{0,3},{1,0},{2,1},{3,2},{4,7},{5,4},{6,5},{7,6},{8,11},{9,8},{10,9... | collective-permute-start | bytes 786440 | tf_op jit(solution)/shard_map/ppermute | solution.py:301
  99.9 34.3 %collective-permute-start.27 = (bf16[3,128,768]{2,1,0:T(8,128)(2,1)}, bf16[3,128,768]{2,1,0:T(8,128)(2,1)S(1)}, u32[]{:S(2)}, u32[]{:S(2)}) collective-permute-start(bf16[3,128,768]{2,1,0:T(8,128)(2,1)} %get-tuple-element.61), channel_id=1, source_target_pairs={{0,3},{1,0},{2,1},{3,2},{4,7},{5,4},{6,5},{7,6},{8,11},{9,8},{10,9... | collective-permute-start | bytes 1769480 | tf_op jit(solution)/shard_map/ppermute | solution.py:301
  115.4 11.5 %collective-permute-start.3 = (bf16[1,128,512]{2,1,0:T(8,128)(2,1)}, bf16[1,128,512]{2,1,0:T(8,128)(2,1)S(1)}, u32[]{:S(2)}, u32[]{:S(2)}) collective-permute-start(bf16[1,128,512]{2,1,0:T(8,128)(2,1)} %copy-done), channel_id=1, source_target_pairs={{0,1},{1,2},{2,3},{3,0},{4,5},{5,6},{6,7},{7,4},{8,9},{9,10},{10,1... | collective-permute-start | bytes 393224 | tf_op jit(solution)/shard_map/ppermute | solution.py:301
  121.0 50.9 %collective-permute-start.30 = (bf16[2,2,128,768]{3,2,1,0:T(8,128)(2,1)}, bf16[2,2,128,768]{3,2,1,0:T(8,128)(2,1)S(1)}, u32[]{:S(2)}, u32[]{:S(2)}) collective-permute-start(bf16[2,2,128,768]{3,2,1,0:T(8,128)(2,1)} %get-tuple-element.62.hi), channel_id=1, source_target_pairs={{0,4},{1,5},{2,6},{3,7},{4,8},{5,9},{6,10},{7,11},{8,12},{9,13},{1... | collective-permute-start | bytes 2359304 | tf_op jit(solution)/shard_map/ppermute | solution.py:301
  124.4 48.9 %collective-permute-start.31 = (bf16[2,2,128,768]{3,2,1,0:T(8,128)(2,1)}, bf16[2,2,128,768]{3,2,1,0:T(8,128)(2,1)S(1)}, u32[]{:S(2)}, u32[]{:S(2)}) collective-permute-start(bf16[2,2,128,768]{3,2,1,0:T(8,128)(2,1)} %get-tuple-element.63.lo), channel_id=1, source_target_pairs={{4,0},{5,1},{6,2},{7,3},{8,4},{9,5},{10,6},{11,7},{12,8},{13,9},{1... | collective-permute-start | bytes 2359304 | tf_op jit(solution)/shard_map/ppermute | solution.py:301
  126.9 26.9 %collective-permute-start.12 = (bf16[2,2,128,512]{3,2,1,0:T(8,128)(2,1)}, bf16[2,2,128,512]{3,2,1,0:T(8,128)(2,1)}, u32[]{:S(2)}, u32[]{:S(2)}) collective-permute-start(bf16[2,2,128,512]{3,2,1,0:T(8,128)(2,1)} %get-tuple-element.47.hi), channel_id=1, source_target_pairs={{0,4},{1,5},{2,6},{3,7},{4,8},{5,9},{6,10},{7,11},{8,12},{9,13},{1... | collective-permute-start | bytes 1572872 | tf_op jit(solution)/shard_map/ppermute | solution.py:301
  130.3 26.7 %collective-permute-start.13 = (bf16[2,2,128,512]{3,2,1,0:T(8,128)(2,1)}, bf16[2,2,128,512]{3,2,1,0:T(8,128)(2,1)}, u32[]{:S(2)}, u32[]{:S(2)}) collective-permute-start(bf16[2,2,128,512]{3,2,1,0:T(8,128)(2,1)} %get-tuple-element.48.lo), channel_id=1, source_target_pairs={{4,0},{5,1},{6,2},{7,3},{8,4},{9,5},{10,6},{11,7},{12,8},{13,9},{1... | collective-permute-start | bytes 1572872 | tf_op jit(solution)/shard_map/ppermute | solution.py:301
  134.2 7.6 %collective-permute-start.5 = (bf16[1,128,512]{2,1,0:T(8,128)(2,1)}, bf16[1,128,512]{2,1,0:T(8,128)(2,1)S(1)}, u32[]{:S(2)}, u32[]{:S(2)}) collective-permute-start(bf16[1,128,512]{2,1,0:T(8,128)(2,1)} %collective-permute-done.4), channel_id=1, source_target_pairs={{0,3},{1,0},{2,1},{3,2},{4,7},{5,4},{6,5},{7,6},{8,11},{9,8},{10,9... | collective-permute-start | bytes 393224 | tf_op jit(solution)/shard_map/ppermute | solution.py:301
  141.8 26.3 %collective-permute-start.28 = (bf16[1,128,768]{2,1,0:T(8,128)(2,1)S(1)}, bf16[1,128,768]{2,1,0:T(8,128)(2,1)S(1)}, u32[]{:S(2)}, u32[]{:S(2)}) collective-permute-start(bf16[1,128,768]{2,1,0:T(8,128)(2,1)S(1)} %slice.18), channel_id=1, source_target_pairs={{0,1},{1,2},{2,3},{3,0},{4,5},{5,6},{6,7},{7,4},{8,9},{9,10},{10,1... | collective-permute-start | bytes 589832 | tf_op jit(solution)/shard_map/ppermute | solution.py:301
  153.8 15.0 %collective-permute-start.29 = (bf16[1,128,768]{2,1,0:T(8,128)(2,1)S(1)}, bf16[1,128,768]{2,1,0:T(8,128)(2,1)S(1)}, u32[]{:S(2)}, u32[]{:S(2)}) collective-permute-start(bf16[1,128,768]{2,1,0:T(8,128)(2,1)S(1)} %slice.19), channel_id=1, source_target_pairs={{0,3},{1,0},{2,1},{3,2},{4,7},{5,4},{6,5},{7,6},{8,11},{9,8},{10,9... | collective-permute-start | bytes 589832 | tf_op jit(solution)/shard_map/ppermute | solution.py:301
  167.3 26.9 %collective-permute-start.18 = (bf16[2,2,128,512]{3,2,1,0:T(8,128)(2,1)S(1)}, bf16[2,2,128,512]{3,2,1,0:T(8,128)(2,1)S(1)}, u32[]{:S(2)}, u32[]{:S(2)}) collective-permute-start(bf16[2,2,128,512]{3,2,1,0:T(8,128)(2,1)S(1)} %get-tuple-element.54), channel_id=1, source_target_pairs={{124,52},{125,53},{126,54},{127,55}} | collective-permute-start | bytes 1572872 | tf_op jit(solution)/shard_map/ppermute | solution.py:301
  168.1 31.0 %collective-permute-start.21 = (bf16[2,2,128,512]{3,2,1,0:T(8,128)(2,1)S(1)}, bf16[2,2,128,512]{3,2,1,0:T(8,128)(2,1)S(1)}, u32[]{:S(2)}, u32[]{:S(2)}) collective-permute-start(bf16[2,2,128,512]{3,2,1,0:T(8,128)(2,1)S(1)} %get-tuple-element.55), channel_id=1, source_target_pairs={{128,200},{129,201},{130,202},{131,203}} | collective-permute-start | bytes 1572872 | tf_op jit(solution)/shard_map/ppermute | solution.py:301
  168.8 31.0 %collective-permute-start.17 = (bf16[2,2,128,512]{3,2,1,0:T(8,128)(2,1)S(1)}, bf16[2,2,128,512]{3,2,1,0:T(8,128)(2,1)S(1)}, u32[]{:S(2)}, u32[]{:S(2)}) collective-permute-start(bf16[2,2,128,512]{3,2,1,0:T(8,128)(2,1)S(1)} %get-tuple-element.54), channel_id=1, source_target_pairs={{0,4},{1,5},{2,6},{3,7},{4,8},{5,9},{6,10},{7,11},{8,12},{9,13},{1... | collective-permute-start | bytes 1572872 | tf_op jit(solution)/shard_map/ppermute | solution.py:301
  171.9 19.6 %collective-permute-start.14 = (bf16[128,512]{1,0:T(8,128)(2,1)S(1)}, bf16[128,512]{1,0:T(8,128)(2,1)S(1)}, u32[]{:S(2)}, u32[]{:S(2)}) collective-permute-start(bf16[128,512]{1,0:T(8,128)(2,1)S(1)} %get-tuple-element.50), channel_id=1, source_target_pairs={{0,1},{1,2},{2,3},{3,0},{4,5},{5,6},{6,7},{7,4},{8,9},{9,10},{10,1... | collective-permute-start | bytes 393224 | tf_op jit(solution)/shard_map/ppermute | solution.py:301
  188.4 52.3 %collective-permute-start.35 = (bf16[2,2,128,768]{3,2,1,0:T(8,128)(2,1)S(1)}, bf16[2,2,128,768]{3,2,1,0:T(8,128)(2,1)S(1)}, u32[]{:S(2)}, u32[]{:S(2)}) collective-permute-start(bf16[2,2,128,768]{3,2,1,0:T(8,128)(2,1)S(1)} %get-tuple-element.69), channel_id=1, source_target_pairs={{0,4},{1,5},{2,6},{3,7},{4,8},{5,9},{6,10},{7,11},{8,12},{9,13},{1... | collective-permute-start | bytes 2359304 | tf_op jit(solution)/shard_map/ppermute | solution.py:301
  191.5 53.3 %collective-permute-start.36 = (bf16[2,2,128,768]{3,2,1,0:T(8,128)(2,1)S(1)}, bf16[2,2,128,768]{3,2,1,0:T(8,128)(2,1)S(1)}, u32[]{:S(2)}, u32[]{:S(2)}) collective-permute-start(bf16[2,2,128,768]{3,2,1,0:T(8,128)(2,1)S(1)} %get-tuple-element.70), channel_id=1, source_target_pairs={{4,0},{5,1},{6,2},{7,3},{8,4},{9,5},{10,6},{11,7},{12,8},{13,9},{1... | collective-permute-start | bytes 2359304 | tf_op jit(solution)/shard_map/ppermute | solution.py:301
  194.3 30.8 %collective-permute-start.20 = (bf16[2,2,128,512]{3,2,1,0:T(8,128)(2,1)S(1)}, bf16[2,2,128,512]{3,2,1,0:T(8,128)(2,1)S(1)}, u32[]{:S(2)}, u32[]{:S(2)}) collective-permute-start(bf16[2,2,128,512]{3,2,1,0:T(8,128)(2,1)S(1)} %get-tuple-element.55), channel_id=1, source_target_pairs={{4,0},{5,1},{6,2},{7,3},{8,4},{9,5},{10,6},{11,7},{12,8},{13,9},{1... | collective-permute-start | bytes 1572872 | tf_op jit(solution)/shard_map/ppermute | solution.py:301
  199.0 28.4 %collective-permute-start.19 = (bf16[2,2,128,512]{3,2,1,0:T(8,128)(2,1)S(1)}, bf16[2,2,128,512]{3,2,1,0:T(8,128)(2,1)S(1)}, u32[]{:S(2)}, u32[]{:S(2)}) collective-permute-start(bf16[2,2,128,512]{3,2,1,0:T(8,128)(2,1)S(1)} %collective-permute-done.18), channel_id=1, source_target_pairs={{52,128},{53,129},{54,130},{55,131}} | collective-permute-start | bytes 1572872 | tf_op jit(solution)/shard_map/ppermute | solution.py:301
  199.7 28.6 %collective-permute-start.22 = (bf16[2,2,128,512]{3,2,1,0:T(8,128)(2,1)S(1)}, bf16[2,2,128,512]{3,2,1,0:T(8,128)(2,1)S(1)}, u32[]{:S(2)}, u32[]{:S(2)}) collective-permute-start(bf16[2,2,128,512]{3,2,1,0:T(8,128)(2,1)S(1)} %collective-permute-done.21), channel_id=1, source_target_pairs={{200,124},{201,125},{202,126},{203,127}} | collective-permute-start | bytes 1572872 | tf_op jit(solution)/shard_map/ppermute | solution.py:301
  225.0 15.6 %collective-permute-start.15 = (bf16[128,512]{1,0:T(8,128)(2,1)S(1)}, bf16[128,512]{1,0:T(8,128)(2,1)S(1)}, u32[]{:S(2)}, u32[]{:S(2)}) collective-permute-start(bf16[128,512]{1,0:T(8,128)(2,1)S(1)} %get-tuple-element.51), channel_id=1, source_target_pairs={{0,2},{1,3},{2,0},{3,1},{4,6},{5,7},{6,4},{7,5},{8,10},{9,11},{10,... | collective-permute-start | bytes 393224 | tf_op jit(solution)/shard_map/ppermute | solution.py:301
  227.4 59.3 %collective-permute-start.32 = (bf16[128,768]{1,0:T(8,128)(2,1)S(1)}, bf16[128,768]{1,0:T(8,128)(2,1)S(1)}, u32[]{:S(2)}, u32[]{:S(2)}) collective-permute-start(bf16[128,768]{1,0:T(8,128)(2,1)S(1)} %get-tuple-element.65), channel_id=1, source_target_pairs={{0,1},{1,2},{2,3},{3,0},{4,5},{5,6},{6,7},{7,4},{8,9},{9,10},{10,1... | collective-permute-start | bytes 589832 | tf_op jit(solution)/shard_map/ppermute | solution.py:301
  228.4 62.6 %collective-permute-start.33 = (bf16[128,768]{1,0:T(8,128)(2,1)S(1)}, bf16[128,768]{1,0:T(8,128)(2,1)S(1)}, u32[]{:S(2)}, u32[]{:S(2)}) collective-permute-start(bf16[128,768]{1,0:T(8,128)(2,1)S(1)} %get-tuple-element.66), channel_id=1, source_target_pairs={{0,2},{1,3},{2,0},{3,1},{4,6},{5,7},{6,4},{7,5},{8,10},{9,11},{10,... | collective-permute-start | bytes 589832 | tf_op jit(solution)/shard_map/ppermute | solution.py:301
  240.6 44.5 %collective-permute-start.16 = (bf16[128,512]{1,0:T(8,128)(2,1)S(1)}, bf16[128,512]{1,0:T(8,128)(2,1)S(1)}, u32[]{:S(2)}, u32[]{:S(2)}) collective-permute-start(bf16[128,512]{1,0:T(8,128)(2,1)S(1)} %get-tuple-element.52), channel_id=1, source_target_pairs={{0,3},{1,0},{2,1},{3,2},{4,7},{5,4},{6,5},{7,6},{8,11},{9,8},{10,9... | collective-permute-start | bytes 393224 | tf_op jit(solution)/shard_map/ppermute | solution.py:301
  240.6 53.3 %collective-permute-start.23 = (bf16[2,128,512]{2,1,0:T(8,128)(2,1)S(1)}, bf16[2,128,512]{2,1,0:T(8,128)(2,1)S(1)}, u32[]{:S(2)}, u32[]{:S(2)}) collective-permute-start(bf16[2,128,512]{2,1,0:T(8,128)(2,1)S(1)} %get-tuple-element.57), channel_id=1, source_target_pairs={{0,1},{1,2},{2,3},{3,0},{4,5},{5,6},{6,7},{7,4},{8,9},{9,10},{10,1... | collective-permute-start | bytes 786440 | tf_op jit(solution)/shard_map/ppermute | solution.py:301
  244.8 47.2 %collective-permute-start.34 = (bf16[128,768]{1,0:T(8,128)(2,1)S(1)}, bf16[128,768]{1,0:T(8,128)(2,1)S(1)}, u32[]{:S(2)}, u32[]{:S(2)}) collective-permute-start(bf16[128,768]{1,0:T(8,128)(2,1)S(1)} %get-tuple-element.67), channel_id=1, source_target_pairs={{0,3},{1,0},{2,1},{3,2},{4,7},{5,4},{6,5},{7,6},{8,11},{9,8},{10,9... | collective-permute-start | bytes 589832 | tf_op jit(solution)/shard_map/ppermute | solution.py:301
  285.1 43.0 %collective-permute-start.37 = (bf16[2,128,768]{2,1,0:T(8,128)(2,1)S(1)}, bf16[2,128,768]{2,1,0:T(8,128)(2,1)S(1)}, u32[]{:S(2)}, u32[]{:S(2)}) collective-permute-start(bf16[2,128,768]{2,1,0:T(8,128)(2,1)S(1)} %get-tuple-element.72), channel_id=1, source_target_pairs={{0,1},{1,2},{2,3},{3,0},{4,5},{5,6},{6,7},{7,4},{8,9},{9,10},{10,1... | collective-permute-start | bytes 1179656 | tf_op jit(solution)/shard_map/ppermute | solution.py:301
  286.7 41.4 %collective-permute-start.38 = (bf16[2,128,768]{2,1,0:T(8,128)(2,1)S(1)}, bf16[2,128,768]{2,1,0:T(8,128)(2,1)S(1)}, u32[]{:S(2)}, u32[]{:S(2)}) collective-permute-start(bf16[2,128,768]{2,1,0:T(8,128)(2,1)S(1)} %get-tuple-element.73), channel_id=1, source_target_pairs={{0,2},{1,3},{2,0},{3,1},{4,6},{5,7},{6,4},{7,5},{8,10},{9,11},{10,... | collective-permute-start | bytes 1179656 | tf_op jit(solution)/shard_map/ppermute | solution.py:301
  291.0 37.1 %collective-permute-start.39 = (bf16[2,128,768]{2,1,0:T(8,128)(2,1)S(1)}, bf16[2,128,768]{2,1,0:T(8,128)(2,1)S(1)}, u32[]{:S(2)}, u32[]{:S(2)}) collective-permute-start(bf16[2,128,768]{2,1,0:T(8,128)(2,1)S(1)} %get-tuple-element.74), channel_id=1, source_target_pairs={{0,3},{1,0},{2,1},{3,2},{4,7},{5,4},{6,5},{7,6},{8,11},{9,8},{10,9... | collective-permute-start | bytes 1179656 | tf_op jit(solution)/shard_map/ppermute | solution.py:301
  292.0 36.1 %collective-permute-start.24 = (bf16[2,128,512]{2,1,0:T(8,128)(2,1)S(1)}, bf16[2,128,512]{2,1,0:T(8,128)(2,1)S(1)}, u32[]{:S(2)}, u32[]{:S(2)}) collective-permute-start(bf16[2,128,512]{2,1,0:T(8,128)(2,1)S(1)} %get-tuple-element.58), channel_id=1, source_target_pairs={{0,2},{1,3},{2,0},{3,1},{4,6},{5,7},{6,4},{7,5},{8,10},{9,11},{10,... | collective-permute-start | bytes 786440 | tf_op jit(solution)/shard_map/ppermute | solution.py:301
  294.0 34.1 %collective-permute-start.25 = (bf16[2,128,512]{2,1,0:T(8,128)(2,1)S(1)}, bf16[2,128,512]{2,1,0:T(8,128)(2,1)S(1)}, u32[]{:S(2)}, u32[]{:S(2)}) collective-permute-start(bf16[2,128,512]{2,1,0:T(8,128)(2,1)S(1)} %get-tuple-element.59), channel_id=1, source_target_pairs={{0,3},{1,0},{2,1},{3,2},{4,7},{5,4},{6,5},{7,6},{8,11},{9,8},{10,9... | collective-permute-start | bytes 786440 | tf_op jit(solution)/shard_map/ppermute | solution.py:301
